TPU v7x, 32 devices: a whole 2x2x4 slice. The times are simulated.
32 devices in a mesh: rows: 4 (over y, x), cols: 8 (over z, core).
Axes of the slice: x: 2, y: 2, z: 4, core: 2. Of those that a mesh axis runs over, the one named last changes fastest.
Arguments:
- spectra: bfloat16 [1024, 4096], P(('rows', 'cols')), may hold values from -6 to 6
- band_weights: float32 [2048], replicated, may hold values from 0.3 to 3
- lag_weights: float32 [4], replicated, may hold values from 0.5 to 2
- selected_bins: int32 [8], replicated, may hold values from 0 to 7
Outputs:
- correlations: float32 [4, 1024, 1024], P(None, 'rows', 'cols')
- gradient: float32 [1024, 4096], P(('rows', 'cols'))
All inputs are finite; a program needn't handle non-finite values.
Results may differ from a plain program's by a relative error of at most 0.0045.
Values may be sent and summed in bfloat16 or wider, within the bound.
No kernel may reach another device: no remote copies, remote signals or barrier semaphores. Data moves between devices by JAX's collectives and lax.ppermute only.
A program may use at most 128 MiB of HBM per device.

v0:
```python
import jax
import jax.numpy as jnp
from jax import lax
from jax.sharding import PartitionSpec as P

LAGS = 4
LAG_STEP = 8
BIN = 128


def per_device(spectra, band_weights, lag_weights, selected_bins):
    n_rows = lax.axis_size("rows")
    n_cols = lax.axis_size("cols")
    row_index = lax.axis_index("rows")
    col_index = lax.axis_index("cols")
    freqs = band_weights.shape[0]
    raw = spectra.astype(jnp.float32)
    mean_power = jnp.mean(raw * raw, axis=1, keepdims=True)
    bin_gains = jnp.concatenate([band_weights, band_weights])
    whitened = (raw * lax.rsqrt(mean_power + 1e-05) * bin_gains[None, :]).astype(jnp.bfloat16)
    row_tile = lax.all_gather(whitened, "cols", axis=0, tiled=True)
    row_len = row_tile.shape[0]
    fold_ratio = n_cols // n_rows
    col_len = row_len // fold_ratio
    slot_part = col_index % fold_ratio
    owner_row = col_index // fold_ratio
    own_piece = lax.dynamic_slice_in_dim(row_tile, slot_part * col_len, col_len, 0)
    stacked = lax.all_gather(own_piece, "rows", axis=0, tiled=True)
    col_tile = lax.dynamic_slice_in_dim(stacked, owner_row * col_len, col_len, 0)
    row_chan = row_index * row_len + jnp.arange(row_len, dtype=jnp.int32)
    col_chan = col_index * col_len + jnp.arange(col_len, dtype=jnp.int32)
    distance = jnp.abs(row_chan[:, None] - col_chan[None, :]) // BIN
    selected = jnp.any(distance[:, :, None] == selected_bins[None, None, :], axis=2).astype(
        jnp.float32
    )
    norm_scale = 1.0 / jnp.sqrt(jnp.float32(2 * freqs))
    bin_index = jnp.arange(freqs, dtype=jnp.float32)
    real_part = row_tile[:, :freqs].astype(jnp.float32)
    imag_part = row_tile[:, freqs:].astype(jnp.float32)
    outputs = []
    row_grad = jnp.zeros((row_len, 2 * freqs), jnp.float32)
    col_grad = jnp.zeros((col_len, 2 * freqs), jnp.float32)
    for lag_index in range(LAGS):
        shift_lag = float((lag_index - LAGS // 2) * LAG_STEP)
        theta = jnp.pi * bin_index * shift_lag / freqs
        cosine = jnp.cos(theta)
        sine_part = jnp.sin(theta)
        rotated = jnp.concatenate(
            [
                real_part * cosine - imag_part * sine_part,
                imag_part * cosine + real_part * sine_part,
            ],
            axis=1,
        ).astype(jnp.bfloat16)
        correlation = (
            lax.dot_general(
                rotated, col_tile, (((1,), (1,)), ((), ())), preferred_element_type=jnp.float32
            )
            * norm_scale
        )
        outputs.append(correlation)
        adjoint = (lag_weights[lag_index] * selected * correlation).astype(jnp.bfloat16)
        back = jnp.dot(adjoint, col_tile, preferred_element_type=jnp.float32) * norm_scale
        back_real = back[:, :freqs]
        back_imag = back[:, freqs:]
        row_grad = row_grad + jnp.concatenate(
            [
                back_real * cosine + back_imag * sine_part,
                back_imag * cosine - back_real * sine_part,
            ],
            axis=1,
        )
        col_grad = (
            col_grad
            + lax.dot_general(
                adjoint, rotated, (((0,), (0,)), ((), ())), preferred_element_type=jnp.float32
            )
            * norm_scale
        )
    col_total = lax.psum(col_grad, "rows")
    is_owner = (owner_row == row_index).astype(jnp.float32)
    addition = lax.dynamic_update_slice_in_dim(
        jnp.zeros_like(row_grad), col_total * is_owner, slot_part * col_len, 0
    )
    gradient = lax.psum_scatter(row_grad + addition, "cols", scatter_dimension=0, tiled=True)
    return (jnp.stack(outputs), gradient)


def solution(mesh):
    placed = (P(("rows", "cols"), None), P(), P(), P())
    return jax.shard_map(
        per_device,
        mesh=mesh,
        in_specs=placed,
        out_specs=(P(None, "rows", "cols"), P(("rows", "cols"), None)),
        check_vma=False,
    )
```

profile of v0, /device:TPU:0, one launch (start us, length us, event | category | flops | bytes accessed | tf_op | source)
XLA Modules:
  0.0 241.0 jit_solution(7234839947374207454)
XLA Ops:
  7.2 0.8 pad_maximum_fusion.21
  8.0 1.1 fusion.28
  9.1 1.8 fusion.30
  11.0 32.0 %all-gather.3.cloned.1.call-done = bf16[256,4096]{1,0:T(8,128)(2,1)} async-done(((bf16[32,4096]{1,0:T(8,128)(2,1)}), bf16[256,4096]{1,0:T(8,128)(2,1)}) %all-gather.3.cloned.1.call-update) | async-done | bytes 2097168 | tf_op jit(solution)/shard_map/all_gather | solution.py:21
  43.0 2.4 %constant_dynamic-slice_fusion = bf16[128,4096]{1,0:T(8,128)(2,1)} fusion(bf16[256,4096]{1,0:T(8,128)(2,1)} %all-gather.3.cloned.1.call-done, s32[]{:T(128)S(6)} %select_n.28), kind=kLoop, calls=%fused_computation.115 | loop fusion | bytes 2097156 | tf_op jit(solution)/shard_map/dynamic_slice | solution.py:27
  45.6 0.6 fusion.74
  46.6 0.4 compare_reduce_fusion
  47.0 1.6 fusion.8
  48.7 3.4 %fusion.4 = (bf16[256,2048]{1,0:T(8,128)(2,1)}, bf16[256,2048]{1,0:T(8,128)(2,1)}, bf16[256,2048]{1,0:T(8,128)(2,1)}, bf16[256,2048]{1,0:T(8,128)(2,1)}, bf16[25...) fusion(f32[2048]{0:T(1024)S(1)} %get-tuple-element.30, f32[2048]{0:T(1024)S(1)} %get-tuple-element.31, ...), kind=kLoop, calls=%fused_computation.28 | loop fusion | flops 13631488 | bytes 8437760 | tf_op jit(solution)/shard_map/convert.6
  52.1 45.5 %all-gather.5.cloned.1.call-done = bf16[512,4096]{1,0:T(8,128)(2,1)} async-done(((bf16[128,4096]{1,0:T(8,128)(2,1)}), bf16[512,4096]{1,0:T(8,128)(2,1)}) %all-gather.5.cloned.1.call-update) | async-done | bytes 4194320 | tf_op jit(solution)/shard_map/all_gather | solution.py:28
  97.6 2.7 %fusion.24 = f32[256,128]{1,0:T(8,128)S(1)} fusion(bf16[256,2048]{1,0:T(8,128)(2,1)} %get-tuple-element.11, bf16[256,2048]{1,0:T(8,128)(2,1)} %get-tuple-element.10, bf16[512,4096]{1,0:T(8,128)(2,1)} %all-gather.5.cloned.1.call-done, s32[]{:T(128)S(6)} %select_n.30), kind=kOutput, calls=%fused_computation.61 | convolution fusion | flops 272662528 | bytes 3276804 | tf_op jit(solution)/shard_map/dot_general | solution.py:56
  100.3 2.7 %fusion.22 = f32[128,4096]{1,0:T(8,128)S(1)} fusion(bf16[256,2048]{1,0:T(8,128)(2,1)} %get-tuple-element.11, bf16[256,2048]{1,0:T(8,128)(2,1)} %get-tuple-element.10, f32[256,128]{1,0:T(8,128)S(1)} %fusion.24, pred[256,128]{1,0:T(8,128)(4,1)S(1)} %compare_reduce_fusion, f32[]{:T(128)} %bitcast.4), kind=kOutput, calls=%fused_computation.59 | convolution fusion | flops 272728064 | bytes 4358148 | tf_op jit(solution)/shard_map/dot_general | solution.py:75
  103.0 0.7 fusion.25
  103.8 1.3 convolution_add_fusion.2
  105.3 0.7 fusion.26
  106.0 1.3 convolution_add_fusion.1
  107.6 0.7 fusion.27
  108.3 2.5 %fusion = f32[128,4096]{1,0:T(8,128)} fusion(f32[128,4096]{1,0:T(8,128)S(1)} %convolution_add_fusion.1, bf16[256,2048]{1,0:T(8,128)(2,1)S(1)} %copy-done.4, bf16[256,2048]{1,0:T(8,128)(2,1)S(1)} %copy-done.5, f32[256,128]{1,0:T(8,128)S(1)} %fusion.27, pred[256,128]{1,0:T(8,128)(4,1)S(1)} %compare_reduce_fusion, f32[]{:T(128)} %bitcast.7), kind=kOutput, calls=%fused_computation.21 | convolution fusion | flops 273776640 | bytes 6455300 | tf_op jit(solution)/shard_map/dot_general | solution.py:75
  111.1 2.5 %convolution_multiply_fusion.3 = f32[256,4096]{1,0:T(8,128)S(1)} fusion(bf16[512,4096]{1,0:T(8,128)(2,1)} %all-gather.5.cloned.1.call-done, s32[]{:T(128)S(6)} %select_n.30, f32[256,128]{1,0:T(8,128)S(1)} %fusion.24, pred[256,128]{1,0:T(8,128)(4,1)S(1)} %compare_reduce_fusion, f32[]{:T(128)} %bitcast.4), kind=kOutput, calls=%fused_computation.19 | convolution fusion | flops 269582336 | bytes 5407236 | tf_op jit(solution)/shard_map/dot_general | solution.py:63
  113.6 0.6 multiply_add_fusion.3
  114.2 1.6 copy-done.3
  115.8 1.3 convolution_multiply_fusion.1
  117.1 0.6 multiply_add_fusion.1
  117.7 1.3 convolution_multiply_fusion
  119.1 1.3 convolution_multiply_fusion.2
  120.4 0.6 multiply_add_fusion
  121.0 0.6 multiply_add_fusion.2
  121.6 2.5 %fusion.2 = f32[256,4096]{1,0:T(8,128)} fusion(f32[256,2048]{1,0:T(8,128)S(1)} %get-tuple-element.9, f32[256,2048]{1,0:T(8,128)S(1)} %get-tuple-element.8, f32[256,2048]{1,0:T(8,128)S(1)} %get-tuple-element.7, f32[256,2048]{1,0:T(8,128)S(1)} %get-tuple-element.6, f32[256,2048]{1,0:T(8,128)S(1)} %get-tuple-element.5, f32[256,2048]{1,0:T(8,128)S(1)} %get-tuple-element.4, ...), kind=kLoop, calls=%fused_computation.26 | loop fusion | flops 7340032 | bytes 20971520 | tf_op jit(solution)/shard_map/add | solution.py:66
  124.2 56.3 %all-reduce.2.cloned.1.call-done = f32[128,4096]{1,0:T(8,128)} async-done(((f32[128,4096]{1,0:T(8,128)}), f32[128,4096]{1,0:T(8,128)}) %all-reduce.2.cloned.1.call-update) | async-done | bytes 2097168 | tf_op jit(solution)/shard_map/psum | solution.py:80
  180.5 3.8 %add_dynamic-update-slice_fusion = f32[256,4096]{1,0:T(8,128)} fusion(f32[256,4096]{1,0:T(8,128)} %fusion.2, s32[]{:T(128)S(6)} %select_n.28, f32[128,4096]{1,0:T(8,128)} %all-reduce.2.cloned.1.call-done, f32[]{:T(128)S(6)} %convert_element_type.40), kind=kLoop, calls=%fused_computation.47 | loop fusion | flops 1048576 | bytes 6291464 | tf_op jit(solution)/shard_map/add | solution.py:85
  184.3 0.8 pad_maximum_fusion.20
  185.2 49.3 %reduce-scatter.2.cloned.1.call-done = f32[32,4096]{1,0:T(8,128)} async-done(((f32[256,4096]{1,0:T(8,128)}), f32[32,4096]{1,0:T(8,128)}) %reduce-scatter.2.cloned.1.call-update) | async-done | bytes 524304 | tf_op jit(solution)/shard_map/reduce_scatter | solution.py:85
  (35 shorter events, 1.3 us)
Async XLA Ops:
  7.2 35.8 %all-gather.3.cloned.1.call-start = ((), (), s32[]{:S(2)}) async-start(), calls=%async_computation.1 | async-start | bytes 2359296 | tf_op jit(solution)/shard_map/all_gather | solution.py:21
  8.0 37.6 %copy-start.8 = (f32[4]{0:T(128)S(1)}, f32[4]{0:T(128)}, u32[]{:S(2)}) copy-start(f32[4]{0:T(128)} %param.6) | copy-start | bytes 52
  9.1 37.5 %copy-start.9 = (s32[8]{0:T(128)S(1)}, s32[8]{0:T(128)}, u32[]{:S(2)}) copy-start(s32[8]{0:T(128)} %param.7) | copy-start | bytes 100
  10.9 86.6 %all-gather.5.cloned.1.call-start = ((), (), s32[]{:S(2)}) async-start(), calls=%async_computation.2 | async-start | bytes 5242880 | tf_op jit(solution)/shard_map/all_gather | solution.py:28
  43.0 4.0 %copy-start = (bf16[256,4096]{1,0:T(8,128)(2,1)S(1)}, bf16[256,4096]{1,0:T(8,128)(2,1)}, u32[]{:S(2)}) copy-start(bf16[256,4096]{1,0:T(8,128)(2,1)} %all-gather.3.cloned.1.call-done) | copy-start | bytes 6291460
  45.5 135.0 %all-reduce.2.cloned.1.call-start = ((), (), s32[]{:S(2)}) async-start(), calls=%async_computation.3 | async-start | bytes 4194304 | tf_op jit(solution)/shard_map/psum | solution.py:80
  97.6 5.4 %copy-start.2 = (bf16[512,4096]{1,0:T(8,128)(2,1)S(1)}, bf16[512,4096]{1,0:T(8,128)(2,1)}, u32[]{:S(2)}) copy-start(bf16[512,4096]{1,0:T(8,128)(2,1)} %all-gather.5.cloned.1.call-done) | copy-start | bytes 12582916
  100.3 2.7 %copy-start.1 = (bf16[256,2048]{1,0:T(8,128)(2,1)S(1)}, bf16[256,2048]{1,0:T(8,128)(2,1)}, u32[]{:S(2)}) copy-start(bf16[256,2048]{1,0:T(8,128)(2,1)} %get-tuple-element.13) | copy-start | bytes 3145732
  103.8 1.3 copy-start.6
  103.8 1.5 copy-start.7
  106.0 1.3 copy-start.4
  106.0 1.5 copy-start.5
  110.9 123.6 %reduce-scatter.2.cloned.1.call-start = ((), (), s32[]{:S(2)}) async-start(), calls=%async_computation.4 | async-start | bytes 4718592 | tf_op jit(solution)/shard_map/reduce_scatter | solution.py:85
  113.6 2.2 copy-start.3
Sparse Core Ops, SparseCore 0:
  11.1 31.8 all-gather.2
  45.6 51.9 all-gather.4
  111.0 69.4 all-reduce.1
  184.5 49.9 reduce-scatter.1
where the time goes:
time: 241 us
  waiting for transfers between devices  183 us (76%)
  matrix products  19.2 us (8%)
  other arithmetic  19.1 us (8%)
  between operations  14.1 us (6%)
  local copies, waits for them, and re-layouts  5.18 us (2%)
    psum x1, waiting for transfers between devices, per_device(): col_total = lax.psum(col_grad, 'rows')  56.3 us
    reduce_scatter x1, waiting for transfers between devices, per_device(): lax.psum_scatter(row_grad + addition, 'cols', scatter_dimension=0, tiled=...  49.3 us
    all_gather x1, waiting for transfers between devices, per_device(): stacked = lax.all_gather(own_piece, 'rows', axis=0, tiled=True)  45.5 us
    all_gather x1, waiting for transfers between devices, per_device(): row_tile = lax.all_gather(whitened, 'cols', axis=0, tiled=True)  32 us
    dot_general x4, matrix products, per_device(): lax.dot_general(adjoint, rotated, (((0,), (0,)), ((), ())), preferred_ele...  7.8 us
    dot_general x4, matrix products, per_device(): jnp.dot(adjoint, col_tile, preferred_element_type=jnp.float32) * norm_scale  6.53 us
    another operation x2, other arithmetic  5.08 us
    dot_general x4, matrix products, per_device(): lax.dot_general(rotated, col_tile, (((1,), (1,)), ((), ())), preferred_el...  4.84 us
  transfers between devices with their start and end apart: 4, of which 4 were waited for; matrix products, arithmetic and copies ran while one was open for 8% of the time, Pallas kernels for 0%

commit v1 on v0

v1 whole, which is shorter than its diff:
```python
import functools
import numpy as np
import jax
import jax.numpy as jnp
from jax import lax
from jax.experimental import pallas as pl
from jax.experimental.pallas import tpu as pltpu
from jax.sharding import PartitionSpec as P

LAGS = 4
LAG_STEP = 8
BIN = 128
PAIR = 2
CHUNK = 512

LAG_SHIFTS = [(lag - LAGS // 2) * LAG_STEP for lag in range(LAGS)]
SHIFTS = sorted({s for t in LAG_SHIFTS for s in (t, -t)})
TABLE = sorted({abs(s) for s in SHIFTS if s != 0})

NT = (((1,), (1,)), ((), ()))


def phase_table(freqs):
    index = np.arange(freqs, dtype=np.float64)
    rows = []
    for shift in TABLE:
        theta = np.pi * index * shift / freqs
        rows += [np.cos(theta), np.sin(theta)]
    return jnp.asarray(np.stack(rows), jnp.float32)


def phase(table_ref, shift, cols):
    at = TABLE.index(abs(shift))
    cosine = table_ref[2 * at : 2 * at + 1, cols]
    sine = table_ref[2 * at + 1 : 2 * at + 2, cols]
    return cosine, (sine if shift > 0 else -sine)


def reverse_bits(value, n_bits):
    return sum(((value >> b) & 1) << (n_bits - 1 - b) for b in range(n_bits))


def whiten_kernel(raw_ref, gain_ref, out_ref):
    freqs = gain_ref.shape[1]
    raw = raw_ref[...].astype(jnp.float32)
    power = jnp.mean(raw * raw, axis=1, keepdims=True)
    factor = lax.rsqrt(power + 1e-05)
    gain = gain_ref[...]
    out_ref[:, :freqs] = (raw[:, :freqs] * factor * gain).astype(jnp.bfloat16)
    out_ref[:, freqs:] = (raw[:, freqs:] * factor * gain).astype(jnp.bfloat16)


def rotate_into(out_ref, row, source, table_ref, shift):
    rows, width = source.shape
    freqs = width // 2
    if shift == 0:
        out_ref[row : row + rows, :] = source[...]
        return
    for start in range(0, freqs, CHUNK):
        cols = slice(start, start + CHUNK)
        high = slice(freqs + start, freqs + start + CHUNK)
        cosine, sine = phase(table_ref, shift, cols)
        real = source[:, cols].astype(jnp.float32)
        imag = source[:, high].astype(jnp.float32)
        out_ref[row : row + rows, cols] = (real * cosine - imag * sine).astype(jnp.bfloat16)
        out_ref[row : row + rows, high] = (imag * cosine + real * sine).astype(jnp.bfloat16)


def rotate_kernel(table_ref, own_ref, out_ref):
    rows = own_ref.shape[0]
    for at, shift in enumerate(SHIFTS):
        rotate_into(out_ref, at * rows, own_ref, table_ref, shift)


def main_kernel(sizes, bins_ref, lag_ref, table_ref, turned_ref, *refs):
    n_rows, n_cols, count = sizes
    own_tiles = refs[:count]
    swapped_tiles = refs[count : 2 * count]
    corr_ref, grad_ref, total_ref, col_ref, turned_col_ref = refs[2 * count :]
    n_lines = n_cols // PAIR
    n_bits = n_rows.bit_length() - 1
    block, width = own_tiles[0].shape
    freqs = width // 2
    norm = 1.0 / np.sqrt(np.float32(width))
    row = lax.axis_index("rows")
    col = lax.axis_index("cols")
    line, core = col // PAIR, col % PAIR
    first = (row * n_cols + col) * block
    ratio = n_cols // n_rows
    owner = col // ratio
    col_base = (col % ratio) * n_rows

    def place(dz, slot, plane):
        in_core = core ^ plane
        dr = jnp.where(in_core == 0, slot, reverse_bits(slot, n_bits))
        return row ^ dr, (line ^ dz) * PAIR + in_core

    for dz in range(n_lines):
        tiles, spots = [], []
        for plane, group in enumerate((own_tiles, swapped_tiles)):
            for slot in range(n_rows):
                tiles.append(group[dz * n_rows + slot])
                spots.append(place(dz, slot, plane))
        span = len(tiles) * block
        for tile, (from_row, from_col) in zip(tiles, spots):
            inside = (from_col >= col_base) & (from_col < col_base + n_rows)

            @pl.when((from_row == owner) & inside)
            def _():
                start = pl.multiple_of((from_col - col_base) * block, block)
                col_ref[pl.ds(start, block), :] = tile[...]

        scores = jnp.zeros((len(SHIFTS) * block, span), jnp.float32)
        for start in range(0, width, CHUNK):
            cols = slice(start, start + CHUNK)
            stacked = jnp.concatenate([tile[:, cols] for tile in tiles], axis=0)
            scores += lax.dot_general(turned_ref[:, cols], stacked, NT, preferred_element_type=jnp.float32)
        scores = scores * norm
        lane = lax.broadcasted_iota(jnp.int32, (block, span), 1)
        mine = first + lax.broadcasted_iota(jnp.int32, (block, span), 0)
        other = jnp.zeros((block, span), jnp.int32)
        for at, (from_row, from_col) in enumerate(spots):
            base = (from_row * n_cols + from_col) * block - at * block
            other = jnp.where(lane >= at * block, base + lane, other)
        distance = jnp.abs(mine - other) // BIN
        chosen = distance == bins_ref[0]
        for entry in range(1, bins_ref.shape[0]):
            chosen = chosen | (distance == bins_ref[entry])
        selected = chosen.astype(jnp.float32)
        weights = []
        for at, shift in enumerate(SHIFTS):
            factor = 0.0
            for lag, lag_shift in enumerate(LAG_SHIFTS):
                for sign in (1, -1):
                    if sign * lag_shift == shift:
                        factor = factor + lag_ref[lag]
            part = scores[at * block : (at + 1) * block, :]
            weights.append((factor * selected * part).astype(jnp.bfloat16))
        weights = jnp.concatenate(weights, axis=0)
        for start in range(0, width, CHUNK):
            cols = slice(start, start + CHUNK)
            stacked = jnp.concatenate([tile[:, cols] for tile in tiles], axis=0)
            term = jnp.dot(weights, stacked, preferred_element_type=jnp.float32)
            if dz == 0:
                total_ref[:, cols] = term
            else:
                total_ref[:, cols] += term

    for start in range(0, freqs, CHUNK):
        cols = slice(start, start + CHUNK)
        high = slice(freqs + start, freqs + start + CHUNK)
        real_sum = jnp.zeros((block, CHUNK), jnp.float32)
        imag_sum = jnp.zeros((block, CHUNK), jnp.float32)
        for at, shift in enumerate(SHIFTS):
            real = total_ref[at * block : (at + 1) * block, cols]
            imag = total_ref[at * block : (at + 1) * block, high]
            if shift == 0:
                real_sum, imag_sum = real_sum + real, imag_sum + imag
            else:
                cosine, sine = phase(table_ref, shift, cols)
                real_sum += real * cosine + imag * sine
                imag_sum += imag * cosine - real * sine
        grad_ref[:, cols] = real_sum * norm
        grad_ref[:, high] = imag_sum * norm

    n_col = col_ref.shape[0]
    for lag, shift in enumerate(LAG_SHIFTS):
        rotate_into(turned_col_ref, lag * n_col, col_ref, table_ref, -shift)
    for plane, group in enumerate((own_tiles, swapped_tiles)):
        for dz in range(n_lines):
            _, from_col = place(dz, 0, plane)
            spot = pl.multiple_of(from_col * block, block)
            part = lax.dot_general(
                group[dz * n_rows][...], turned_col_ref[...], NT, preferred_element_type=jnp.float32
            )
            for lag in range(LAGS):
                corr_ref[lag, pl.ds(spot, block), :] = part[:, lag * n_col : (lag + 1) * n_col] * norm


def per_device(spectra, band_weights, lag_weights, selected_bins):
    n_rows = lax.axis_size("rows")
    n_cols = lax.axis_size("cols")
    n_lines = n_cols // PAIR
    n_bits = n_rows.bit_length() - 1
    block, width = spectra.shape
    freqs = width // 2
    vmem = pl.BlockSpec(memory_space=pltpu.VMEM)
    smem = pl.BlockSpec(memory_space=pltpu.SMEM)
    table = phase_table(freqs)

    def send(value, move):
        pairs = []
        for r in range(n_rows):
            for c in range(n_cols):
                to_row, to_line, to_core = move(r, c // PAIR, c % PAIR)
                pairs.append((r * n_cols + c, to_row * n_cols + to_line * PAIR + to_core))
        return lax.ppermute(value, ("rows", "cols"), pairs)

    def send_row(value, bit):
        return send(value, lambda r, z, k: (r ^ (1 << (bit if k == 0 else n_bits - 1 - bit)), z, k))

    def send_line(value, step):
        return send(value, lambda r, z, k: (r, z ^ step, k))

    def swap(value):
        return send(value, lambda r, z, k: (r, z, k ^ 1))

    whitened = pl.pallas_call(
        whiten_kernel,
        out_shape=jax.ShapeDtypeStruct((block, width), jnp.bfloat16),
        in_specs=[vmem, vmem],
        out_specs=vmem,
    )(spectra, band_weights[None, :])
    lines = [whitened]
    for dz in range(1, n_lines):
        low = dz & -dz
        lines.append(send_line(lines[dz ^ low], low))
    tiles = []
    for dz in range(n_lines):
        group = [lines[dz]]
        for slot in range(1, n_rows):
            high = slot.bit_length() - 1
            group.append(send_row(group[slot ^ (1 << high)], high))
        tiles += group
    swapped = [swap(tile) for tile in tiles]
    turned = pl.pallas_call(
        rotate_kernel,
        out_shape=jax.ShapeDtypeStruct((len(SHIFTS) * block, width), jnp.bfloat16),
        in_specs=[vmem, vmem],
        out_specs=vmem,
    )(table, whitened)
    count = len(tiles)
    n_row, n_col = n_cols * block, n_rows * block
    correlations, gradient = pl.pallas_call(
        functools.partial(main_kernel, (n_rows, n_cols, count)),
        out_shape=(
            jax.ShapeDtypeStruct((LAGS, n_row, n_col), jnp.float32),
            jax.ShapeDtypeStruct((block, width), jnp.float32),
        ),
        in_specs=[smem, smem, vmem, vmem] + [vmem] * (2 * count),
        out_specs=(vmem, vmem),
        scratch_shapes=[
            pltpu.VMEM((len(SHIFTS) * block, width), jnp.float32),
            pltpu.VMEM((n_col, width), jnp.bfloat16),
            pltpu.VMEM((LAGS * n_col, width), jnp.bfloat16),
        ],
    )(selected_bins, lag_weights, table, turned, *tiles, *swapped)
    return correlations, gradient


def solution(mesh):
    placed = (P(("rows", "cols"), None), P(), P(), P())
    return jax.shard_map(
        per_device,
        mesh=mesh,
        in_specs=placed,
        out_specs=(P(None, "rows", "cols"), P(("rows", "cols"), None)),
        check_vma=False,
    )
```

time: 241 us -> 80.5 us (0.33)
  waiting for transfers between devices: 183 us -> 28.2 us
  Pallas kernels: 0 us -> 26.5 us
  starting transfers between devices: 0.35 us -> 24.5 us
  matrix products: 19.2 us -> 0 us
  other arithmetic: 19.1 us -> 0 us
  between operations: 14.1 us -> 1.07 us
  local copies, waits for them, and re-layouts: 5.18 us -> 0.08 us
    all_gather x2 -> x0, waiting for transfers between devices: 77.4 us -> none  [the longest x1 45.5 us: per_device(): stacked = lax.all_gather(own_piece, 'rows', axis=0, tiled=True)]
    psum x1 -> x0, waiting for transfers between devices: 56.3 us -> none  [per_device(): col_total = lax.psum(col_grad, 'rows')]
    reduce_scatter x1 -> x0, waiting for transfers between devices: 49.3 us -> none  [per_device(): lax.psum_scatter(row_grad + addition, 'cols', scatter_dimension=0, tiled=...]
    ppermute x0 -> x31, waiting for transfers between devices: none -> 28.2 us  [send(): return lax.ppermute(value, ('rows', 'cols'), pairs)]
    pallas_call x0 -> x3, Pallas kernels: none -> 26.5 us  [the longest x1 22.2 us: per_device(): pl.pallas_call(functools.partial(main_kernel, (n_rows, n_cols, count)), o...]
    ppermute x0 -> x31, starting transfers between devices: none -> 24.5 us  [send(): return lax.ppermute(value, ('rows', 'cols'), pairs)]
    dot_general x12 -> x0, matrix products: 19.2 us -> none  [the longest x4 7.8 us: per_device(): lax.dot_general(adjoint, rotated, (((0,), (0,)), ((), ())), preferred_ele...]
    add x8 -> x0, other arithmetic: 8.7 us -> none  [the longest x1 3.81 us: per_device(): row_grad + addition]
  transfers between devices with their start and end apart: 4 -> 31, of which waited for: 4 -> 9; matrix products, arithmetic and copies ran while one was open for 8% -> 0% of each run, Pallas kernels for 0% -> 3%
where the time goes in v1:
time: 80.5 us; the launch traced here: 80.3 us
  waiting for transfers between devices  28.2 us (35%)
  Pallas kernels  26.5 us (33%)
  starting transfers between devices  24.5 us (30%)
  between operations  1.07 us (1%)
    ppermute x31, waiting for transfers between devices, send(): return lax.ppermute(value, ('rows', 'cols'), pairs)  28.2 us
    ppermute x31, starting transfers between devices, send(): return lax.ppermute(value, ('rows', 'cols'), pairs)  24.5 us
    pallas_call x1, Pallas kernels, per_device(): pl.pallas_call(functools.partial(main_kernel, (n_rows, n_cols, count)), o...  22.2 us
    pallas_call x1, Pallas kernels, per_device(): pl.pallas_call(rotate_kernel, out_shape=jax.ShapeDtypeStruct((len(SHIFTS)...  2.4 us
    pallas_call x1, Pallas kernels, per_device(): pl.pallas_call(whiten_kernel, out_shape=jax.ShapeDtypeStruct((block, widt...  1.84 us
  transfers between devices with their start and end apart: 31, of which 9 were waited for; matrix products, arithmetic and copies ran while one was open for 0% of the time, Pallas kernels for 3%

profile of v1, /device:TPU:0, one launch (start us, length us, event | category | flops | bytes accessed | tf_op | source)
XLA Modules:
  0.0 80.3 jit_solution(15579468674657747613)
XLA Ops:
  0.6 1.8 %shard_map.68.own_ref.refs_0_ = bf16[32,4096]{1,0:T(8,128)(2,1)} custom-call(bf16[32,4096]{1,0:T(8,128)(2,1)} %raw_ref.1, f32[1,2048]{1,0:T(1,128)} %bitcast.1), custom_call_target="tpu_custom_call" | custom-call | tf_op jit(solution)/shard_map/pallas_call | solution.py:208
  2.5 4.1 %collective-permute-start.7 = (bf16[32,4096]{1,0:T(8,128)(2,1)}, bf16[32,4096]{1,0:T(8,128)(2,1)S(1)}, u32[]{:S(2)}, u32[]{:S(2)}) collective-permute-start(bf16[32,4096]{1,0:T(8,128)(2,1)} %shard_map.68.own_ref.refs_0_), channel_id=1, source_target_pairs={{0,4},{1,5},{2,6},{3,7},{4,0},{5,1},{6,2},{7,3},{8,12},{9,13},{10,... | collective-permute-start | bytes 786440 | tf_op jit(solution)/shard_map/ppermute | solution.py:197
  6.5 1.6 %collective-permute-start.3 = (bf16[32,4096]{1,0:T(8,128)(2,1)}, bf16[32,4096]{1,0:T(8,128)(2,1)S(1)}, u32[]{:S(2)}, u32[]{:S(2)}) collective-permute-start(bf16[32,4096]{1,0:T(8,128)(2,1)} %shard_map.68.own_ref.refs_0_), channel_id=1, source_target_pairs={{0,2},{1,3},{2,0},{3,1},{4,6},{5,7},{6,4},{7,5},{8,10},{9,11},{10,... | collective-permute-start | bytes 786440 | tf_op jit(solution)/shard_map/ppermute | solution.py:197
  8.1 1.5 %collective-permute-start.1 = (bf16[32,4096]{1,0:T(8,128)(2,1)}, bf16[32,4096]{1,0:T(8,128)(2,1)S(1)}, u32[]{:S(2)}, u32[]{:S(2)}) collective-permute-start(bf16[32,4096]{1,0:T(8,128)(2,1)} %shard_map.68.own_ref.refs_0_), channel_id=1, source_target_pairs={{0,16},{1,9},{2,18},{3,11},{4,20},{5,13},{6,22},{7,15},{8,24},{9,1... | collective-permute-start | bytes 786440 | tf_op jit(solution)/shard_map/ppermute | solution.py:197
  9.6 1.5 %collective-permute-start = (bf16[32,4096]{1,0:T(8,128)(2,1)}, bf16[32,4096]{1,0:T(8,128)(2,1)S(1)}, u32[]{:S(2)}, u32[]{:S(2)}) collective-permute-start(bf16[32,4096]{1,0:T(8,128)(2,1)} %shard_map.68.own_ref.refs_0_), channel_id=1, source_target_pairs={{0,8},{1,17},{2,10},{3,19},{4,12},{5,21},{6,14},{7,23},{8,0},{9,25... | collective-permute-start | bytes 786440 | tf_op jit(solution)/shard_map/ppermute | solution.py:197
  11.1 7.6 %collective-permute-done.7.refs_8_ = bf16[32,4096]{1,0:T(8,128)(2,1)S(1)} collective-permute-done((bf16[32,4096]{1,0:T(8,128)(2,1)}, bf16[32,4096]{1,0:T(8,128)(2,1)S(1)}, u32[]{:S(2)}, u32[]{:S(2)}) %collective-permute-start.7) | collective-permute-done | bytes 262176 | tf_op jit(solution)/shard_map/ppermute | solution.py:197
  18.8 0.8 %collective-permute-start.11 = (bf16[32,4096]{1,0:T(8,128)(2,1)S(1)}, bf16[32,4096]{1,0:T(8,128)(2,1)S(1)}, u32[]{:S(2)}, u32[]{:S(2)}) collective-permute-start(bf16[32,4096]{1,0:T(8,128)(2,1)S(1)} %collective-permute-done.7.refs_8_), channel_id=1, source_target_pairs={{0,2},{1,3},{2,0},{3,1},{4,6},{5,7},{6,4},{7,5},{8,10},{9,11},{10,... | collective-permute-start | bytes 786440 | tf_op jit(solution)/shard_map/ppermute | solution.py:197
  19.6 0.3 collective-permute-done.3.refs_4_
  19.9 1.6 %collective-permute-start.9 = (bf16[32,4096]{1,0:T(8,128)(2,1)S(1)}, bf16[32,4096]{1,0:T(8,128)(2,1)S(1)}, u32[]{:S(2)}, u32[]{:S(2)}) collective-permute-start(bf16[32,4096]{1,0:T(8,128)(2,1)S(1)} %collective-permute-done.7.refs_8_), channel_id=1, source_target_pairs={{0,16},{1,9},{2,18},{3,11},{4,20},{5,13},{6,22},{7,15},{8,24},{9,1... | collective-permute-start | bytes 786440 | tf_op jit(solution)/shard_map/ppermute | solution.py:197
  21.5 1.5 %collective-permute-start.8 = (bf16[32,4096]{1,0:T(8,128)(2,1)S(1)}, bf16[32,4096]{1,0:T(8,128)(2,1)S(1)}, u32[]{:S(2)}, u32[]{:S(2)}) collective-permute-start(bf16[32,4096]{1,0:T(8,128)(2,1)S(1)} %collective-permute-done.7.refs_8_), channel_id=1, source_target_pairs={{0,8},{1,17},{2,10},{3,19},{4,12},{5,21},{6,14},{7,23},{8,0},{9,25... | collective-permute-start | bytes 786440 | tf_op jit(solution)/shard_map/ppermute | solution.py:197
  23.0 0.6 collective-permute-start.5
  23.6 3.9 %collective-permute-done.11.refs_12_ = bf16[32,4096]{1,0:T(8,128)(2,1)S(1)} collective-permute-done((bf16[32,4096]{1,0:T(8,128)(2,1)S(1)}, bf16[32,4096]{1,0:T(8,128)(2,1)S(1)}, u32[]{:S(2)}, u32[]{:S(2)}) %collective-permute-start.11) | collective-permute-done | bytes 262176 | tf_op jit(solution)/shard_map/ppermute | solution.py:197
  27.5 1.5 %collective-permute-start.4 = (bf16[32,4096]{1,0:T(8,128)(2,1)S(1)}, bf16[32,4096]{1,0:T(8,128)(2,1)S(1)}, u32[]{:S(2)}, u32[]{:S(2)}) collective-permute-start(bf16[32,4096]{1,0:T(8,128)(2,1)S(1)} %collective-permute-done.3.refs_4_), channel_id=1, source_target_pairs={{0,8},{1,17},{2,10},{3,19},{4,12},{5,21},{6,14},{7,23},{8,0},{9,25... | collective-permute-start | bytes 786440 | tf_op jit(solution)/shard_map/ppermute | solution.py:197
  29.1 0.8 %collective-permute-done.8.refs_9_ = bf16[32,4096]{1,0:T(8,128)(2,1)S(1)} collective-permute-done((bf16[32,4096]{1,0:T(8,128)(2,1)S(1)}, bf16[32,4096]{1,0:T(8,128)(2,1)S(1)}, u32[]{:S(2)}, u32[]{:S(2)}) %collective-permute-start.8) | collective-permute-done | bytes 262176 | tf_op jit(solution)/shard_map/ppermute | solution.py:197
  29.9 1.3 %collective-permute-start.2 = (bf16[32,4096]{1,0:T(8,128)(2,1)S(1)}, bf16[32,4096]{1,0:T(8,128)(2,1)S(1)}, u32[]{:S(2)}, u32[]{:S(2)}) collective-permute-start(bf16[32,4096]{1,0:T(8,128)(2,1)S(1)} %collective-permute-done.refs_1_), channel_id=1, source_target_pairs={{0,16},{1,9},{2,18},{3,11},{4,20},{5,13},{6,22},{7,15},{8,24},{9,1... | collective-permute-start | bytes 786440 | tf_op jit(solution)/shard_map/ppermute | solution.py:197
  31.2 2.9 %collective-permute-done.5.refs_6_ = bf16[32,4096]{1,0:T(8,128)(2,1)S(1)} collective-permute-done((bf16[32,4096]{1,0:T(8,128)(2,1)S(1)}, bf16[32,4096]{1,0:T(8,128)(2,1)S(1)}, u32[]{:S(2)}, u32[]{:S(2)}) %collective-permute-start.5) | collective-permute-done | bytes 262176 | tf_op jit(solution)/shard_map/ppermute | solution.py:197
  34.2 2.4 %collective-permute-start.13 = (bf16[32,4096]{1,0:T(8,128)(2,1)S(1)}, bf16[32,4096]{1,0:T(8,128)(2,1)}, u32[]{:S(2)}, u32[]{:S(2)}) collective-permute-start(bf16[32,4096]{1,0:T(8,128)(2,1)S(1)} %collective-permute-done.11.refs_12_), channel_id=1, source_target_pairs={{0,16},{1,9},{2,18},{3,11},{4,20},{5,13},{6,22},{7,15},{8,24},{9,1... | collective-permute-start | bytes 786440 | tf_op jit(solution)/shard_map/ppermute | solution.py:197
  36.7 1.4 %collective-permute-start.12 = (bf16[32,4096]{1,0:T(8,128)(2,1)S(1)}, bf16[32,4096]{1,0:T(8,128)(2,1)}, u32[]{:S(2)}, u32[]{:S(2)}) collective-permute-start(bf16[32,4096]{1,0:T(8,128)(2,1)S(1)} %collective-permute-done.11.refs_12_), channel_id=1, source_target_pairs={{0,8},{1,17},{2,10},{3,19},{4,12},{5,21},{6,14},{7,23},{8,0},{9,25... | collective-permute-start | bytes 786440 | tf_op jit(solution)/shard_map/ppermute | solution.py:197
  38.1 0.5 collective-permute-start.24
  38.6 0.6 collective-permute-start.10
  39.2 4.7 %collective-permute-done.13.refs_14_ = bf16[32,4096]{1,0:T(8,128)(2,1)} collective-permute-done((bf16[32,4096]{1,0:T(8,128)(2,1)S(1)}, bf16[32,4096]{1,0:T(8,128)(2,1)}, u32[]{:S(2)}, u32[]{:S(2)}) %collective-permute-start.13) | collective-permute-done | bytes 262176 | tf_op jit(solution)/shard_map/ppermute | solution.py:197
  43.9 2.1 %collective-permute-done.12.refs_13_ = bf16[32,4096]{1,0:T(8,128)(2,1)} collective-permute-done((bf16[32,4096]{1,0:T(8,128)(2,1)S(1)}, bf16[32,4096]{1,0:T(8,128)(2,1)}, u32[]{:S(2)}, u32[]{:S(2)}) %collective-permute-start.12) | collective-permute-done | bytes 262176 | tf_op jit(solution)/shard_map/ppermute | solution.py:197
  46.0 0.2 collective-permute-start.6
  46.1 1.3 %collective-permute-start.18 = (bf16[32,4096]{1,0:T(8,128)(2,1)S(1)}, bf16[32,4096]{1,0:T(8,128)(2,1)S(1)}, u32[]{:S(2)}, u32[]{:S(2)}) collective-permute-start(bf16[32,4096]{1,0:T(8,128)(2,1)S(1)} %collective-permute-done.2.refs_3_), channel_id=1, source_target_pairs={{0,1},{1,0},{2,3},{3,2},{4,5},{5,4},{6,7},{7,6},{8,9},{9,8},{10,11... | collective-permute-start | bytes 786440 | tf_op jit(solution)/shard_map/ppermute | solution.py:197
  47.4 1.0 %collective-permute-start.14 = (bf16[32,4096]{1,0:T(8,128)(2,1)}, bf16[32,4096]{1,0:T(8,128)(2,1)}, u32[]{:S(2)}, u32[]{:S(2)}) collective-permute-start(bf16[32,4096]{1,0:T(8,128)(2,1)} %collective-permute-done.12.refs_13_), channel_id=1, source_target_pairs={{0,16},{1,9},{2,18},{3,11},{4,20},{5,13},{6,22},{7,15},{8,24},{9,1... | collective-permute-start | bytes 786440 | tf_op jit(solution)/shard_map/ppermute | solution.py:197
  48.4 0.5 collective-permute-start.29
  48.9 3.6 %collective-permute-done.6.refs_7_ = bf16[32,4096]{1,0:T(8,128)(2,1)} collective-permute-done((bf16[32,4096]{1,0:T(8,128)(2,1)S(1)}, bf16[32,4096]{1,0:T(8,128)(2,1)}, u32[]{:S(2)}, u32[]{:S(2)}) %collective-permute-start.6) | collective-permute-done | bytes 262176 | tf_op jit(solution)/shard_map/ppermute | solution.py:197
  52.5 0.6 collective-permute-start.22
  53.1 2.2 %collective-permute-done.14.refs_15_ = bf16[32,4096]{1,0:T(8,128)(2,1)} collective-permute-done((bf16[32,4096]{1,0:T(8,128)(2,1)}, bf16[32,4096]{1,0:T(8,128)(2,1)}, u32[]{:S(2)}, u32[]{:S(2)}) %collective-permute-start.14) | collective-permute-done | bytes 262176 | tf_op jit(solution)/shard_map/ppermute | solution.py:197
  55.3 0.1 collective-permute-start.30
  55.4 2.4 %shard_map.69.turned_ref = bf16[160,4096]{1,0:T(8,128)(2,1)} custom-call(f32[4,2048]{1,0:T(4,128)} %constant.2.clone.table_ref, bf16[32,4096]{1,0:T(8,128)(2,1)} %shard_map.68.own_ref.refs_0_), custom_call_target="tpu_custom_call" | custom-call | tf_op jit(solution)/shard_map/pallas_call | solution.py:226
  58.0 22.2 %shard_map.70 = (f32[4,256,128]{2,1,0:T(8,128)}, f32[32,4096]{1,0:T(8,128)}) custom-call(s32[8]{0:T(128)} %bins_ref.1, f32[4]{0:T(128)} %lag_ref.1, f32[4,2048]{1,0:T(4,128)} %constant.2.clone.table_ref, bf16[160,4096]{1,0:T(8,128)(2,1)} %shard_map.69.turned_ref, bf16[32,4096]{1,0:T(8,128)(2,1)} %shard_map.68.own_ref.refs_0_, bf16[32,4096]{1,0:T(8,128)(2,1)} %copy-done.4, ...), custom_call_target="tpu_custom_call" | custom-call | tf_op jit(solution)/shard_map/pallas_call | solution.py:234
  (75 shorter events, 0.2 us)
Async XLA Ops:
  2.5 16.3 %collective-permute-start.7 = (bf16[32,4096]{1,0:T(8,128)(2,1)}, bf16[32,4096]{1,0:T(8,128)(2,1)S(1)}, u32[]{:S(2)}, u32[]{:S(2)}) collective-permute-start(bf16[32,4096]{1,0:T(8,128)(2,1)} %shard_map.68.own_ref.refs_0_), channel_id=1, source_target_pairs={{0,4},{1,5},{2,6},{3,7},{4,0},{5,1},{6,2},{7,3},{8,12},{9,13},{10,... | collective-permute-start | bytes 786440 | tf_op jit(solution)/shard_map/ppermute | solution.py:197
  6.5 12.2 %collective-permute-start.15 = (bf16[32,4096]{1,0:T(8,128)(2,1)}, bf16[32,4096]{1,0:T(8,128)(2,1)S(1)}, u32[]{:S(2)}, u32[]{:S(2)}) collective-permute-start(bf16[32,4096]{1,0:T(8,128)(2,1)} %shard_map.68.own_ref.refs_0_), channel_id=1, source_target_pairs={{0,1},{1,0},{2,3},{3,2},{4,5},{5,4},{6,7},{7,6},{8,9},{9,8},{10,11... | collective-permute-start | bytes 786440 | tf_op jit(solution)/shard_map/ppermute | solution.py:197
  6.5 13.4 %collective-permute-start.3 = (bf16[32,4096]{1,0:T(8,128)(2,1)}, bf16[32,4096]{1,0:T(8,128)(2,1)S(1)}, u32[]{:S(2)}, u32[]{:S(2)}) collective-permute-start(bf16[32,4096]{1,0:T(8,128)(2,1)} %shard_map.68.own_ref.refs_0_), channel_id=1, source_target_pairs={{0,2},{1,3},{2,0},{3,1},{4,6},{5,7},{6,4},{7,5},{8,10},{9,11},{10,... | collective-permute-start | bytes 786440 | tf_op jit(solution)/shard_map/ppermute | solution.py:197
  8.1 13.4 %collective-permute-start.1 = (bf16[32,4096]{1,0:T(8,128)(2,1)}, bf16[32,4096]{1,0:T(8,128)(2,1)S(1)}, u32[]{:S(2)}, u32[]{:S(2)}) collective-permute-start(bf16[32,4096]{1,0:T(8,128)(2,1)} %shard_map.68.own_ref.refs_0_), channel_id=1, source_target_pairs={{0,16},{1,9},{2,18},{3,11},{4,20},{5,13},{6,22},{7,15},{8,24},{9,1... | collective-permute-start | bytes 786440 | tf_op jit(solution)/shard_map/ppermute | solution.py:197
  9.6 13.4 %collective-permute-start = (bf16[32,4096]{1,0:T(8,128)(2,1)}, bf16[32,4096]{1,0:T(8,128)(2,1)S(1)}, u32[]{:S(2)}, u32[]{:S(2)}) collective-permute-start(bf16[32,4096]{1,0:T(8,128)(2,1)} %shard_map.68.own_ref.refs_0_), channel_id=1, source_target_pairs={{0,8},{1,17},{2,10},{3,19},{4,12},{5,21},{6,14},{7,23},{8,0},{9,25... | collective-permute-start | bytes 786440 | tf_op jit(solution)/shard_map/ppermute | solution.py:197
  18.8 39.1 %copy-start = (bf16[32,4096]{1,0:T(8,128)(2,1)}, bf16[32,4096]{1,0:T(8,128)(2,1)S(1)}, u32[]{:S(2)}) copy-start(bf16[32,4096]{1,0:T(8,128)(2,1)S(1)} %collective-permute-done.7.refs_8_) | copy-start | bytes 786436
  18.8 4.2 %collective-permute-start.23 = (bf16[32,4096]{1,0:T(8,128)(2,1)S(1)}, bf16[32,4096]{1,0:T(8,128)(2,1)S(1)}, u32[]{:S(2)}, u32[]{:S(2)}) collective-permute-start(bf16[32,4096]{1,0:T(8,128)(2,1)S(1)} %collective-permute-done.7.refs_8_), channel_id=1, source_target_pairs={{0,1},{1,0},{2,3},{3,2},{4,5},{5,4},{6,7},{7,6},{8,9},{9,8},{10,11... | collective-permute-start | bytes 786440 | tf_op jit(solution)/shard_map/ppermute | solution.py:197
  18.8 8.7 %collective-permute-start.11 = (bf16[32,4096]{1,0:T(8,128)(2,1)S(1)}, bf16[32,4096]{1,0:T(8,128)(2,1)S(1)}, u32[]{:S(2)}, u32[]{:S(2)}) collective-permute-start(bf16[32,4096]{1,0:T(8,128)(2,1)S(1)} %collective-permute-done.7.refs_8_), channel_id=1, source_target_pairs={{0,2},{1,3},{2,0},{3,1},{4,6},{5,7},{6,4},{7,5},{8,10},{9,11},{10,... | collective-permute-start | bytes 786440 | tf_op jit(solution)/shard_map/ppermute | solution.py:197
  19.9 9.1 %collective-permute-start.9 = (bf16[32,4096]{1,0:T(8,128)(2,1)S(1)}, bf16[32,4096]{1,0:T(8,128)(2,1)S(1)}, u32[]{:S(2)}, u32[]{:S(2)}) collective-permute-start(bf16[32,4096]{1,0:T(8,128)(2,1)S(1)} %collective-permute-done.7.refs_8_), channel_id=1, source_target_pairs={{0,16},{1,9},{2,18},{3,11},{4,20},{5,13},{6,22},{7,15},{8,24},{9,1... | collective-permute-start | bytes 786440 | tf_op jit(solution)/shard_map/ppermute | solution.py:197
  21.5 8.4 %collective-permute-start.8 = (bf16[32,4096]{1,0:T(8,128)(2,1)S(1)}, bf16[32,4096]{1,0:T(8,128)(2,1)S(1)}, u32[]{:S(2)}, u32[]{:S(2)}) collective-permute-start(bf16[32,4096]{1,0:T(8,128)(2,1)S(1)} %collective-permute-done.7.refs_8_), channel_id=1, source_target_pairs={{0,8},{1,17},{2,10},{3,19},{4,12},{5,21},{6,14},{7,23},{8,0},{9,25... | collective-permute-start | bytes 786440 | tf_op jit(solution)/shard_map/ppermute | solution.py:197
  23.0 6.9 %collective-permute-start.19 = (bf16[32,4096]{1,0:T(8,128)(2,1)S(1)}, bf16[32,4096]{1,0:T(8,128)(2,1)S(1)}, u32[]{:S(2)}, u32[]{:S(2)}) collective-permute-start(bf16[32,4096]{1,0:T(8,128)(2,1)S(1)} %collective-permute-done.3.refs_4_), channel_id=1, source_target_pairs={{0,1},{1,0},{2,3},{3,2},{4,5},{5,4},{6,7},{7,6},{8,9},{9,8},{10,11... | collective-permute-start | bytes 786440 | tf_op jit(solution)/shard_map/ppermute | solution.py:197
  23.0 11.1 %collective-permute-start.5 = (bf16[32,4096]{1,0:T(8,128)(2,1)S(1)}, bf16[32,4096]{1,0:T(8,128)(2,1)S(1)}, u32[]{:S(2)}, u32[]{:S(2)}) collective-permute-start(bf16[32,4096]{1,0:T(8,128)(2,1)S(1)} %collective-permute-done.3.refs_4_), channel_id=1, source_target_pairs={{0,16},{1,9},{2,18},{3,11},{4,20},{5,13},{6,22},{7,15},{8,24},{9,1... | collective-permute-start | bytes 786440 | tf_op jit(solution)/shard_map/ppermute | solution.py:197
  27.5 6.7 %collective-permute-start.4 = (bf16[32,4096]{1,0:T(8,128)(2,1)S(1)}, bf16[32,4096]{1,0:T(8,128)(2,1)S(1)}, u32[]{:S(2)}, u32[]{:S(2)}) collective-permute-start(bf16[32,4096]{1,0:T(8,128)(2,1)S(1)} %collective-permute-done.3.refs_4_), channel_id=1, source_target_pairs={{0,8},{1,17},{2,10},{3,19},{4,12},{5,21},{6,14},{7,23},{8,0},{9,25... | collective-permute-start | bytes 786440 | tf_op jit(solution)/shard_map/ppermute | solution.py:197
  29.0 7.6 %collective-permute-start.17 = (bf16[32,4096]{1,0:T(8,128)(2,1)S(1)}, bf16[32,4096]{1,0:T(8,128)(2,1)S(1)}, u32[]{:S(2)}, u32[]{:S(2)}) collective-permute-start(bf16[32,4096]{1,0:T(8,128)(2,1)S(1)} %collective-permute-done.1.refs_2_), channel_id=1, source_target_pairs={{0,1},{1,0},{2,3},{3,2},{4,5},{5,4},{6,7},{7,6},{8,9},{9,8},{10,11... | collective-permute-start | bytes 786440 | tf_op jit(solution)/shard_map/ppermute | solution.py:197
  29.9 8.2 %collective-permute-start.16 = (bf16[32,4096]{1,0:T(8,128)(2,1)S(1)}, bf16[32,4096]{1,0:T(8,128)(2,1)S(1)}, u32[]{:S(2)}, u32[]{:S(2)}) collective-permute-start(bf16[32,4096]{1,0:T(8,128)(2,1)S(1)} %collective-permute-done.refs_1_), channel_id=1, source_target_pairs={{0,1},{1,0},{2,3},{3,2},{4,5},{5,4},{6,7},{7,6},{8,9},{9,8},{10,11... | collective-permute-start | bytes 786440 | tf_op jit(solution)/shard_map/ppermute | solution.py:197
  29.9 8.2 %collective-permute-start.2 = (bf16[32,4096]{1,0:T(8,128)(2,1)S(1)}, bf16[32,4096]{1,0:T(8,128)(2,1)S(1)}, u32[]{:S(2)}, u32[]{:S(2)}) collective-permute-start(bf16[32,4096]{1,0:T(8,128)(2,1)S(1)} %collective-permute-done.refs_1_), channel_id=1, source_target_pairs={{0,16},{1,9},{2,18},{3,11},{4,20},{5,13},{6,22},{7,15},{8,24},{9,1... | collective-permute-start | bytes 786440 | tf_op jit(solution)/shard_map/ppermute | solution.py:197
  34.2 4.5 %collective-permute-start.27 = (bf16[32,4096]{1,0:T(8,128)(2,1)S(1)}, bf16[32,4096]{1,0:T(8,128)(2,1)S(1)}, u32[]{:S(2)}, u32[]{:S(2)}) collective-permute-start(bf16[32,4096]{1,0:T(8,128)(2,1)S(1)} %collective-permute-done.11.refs_12_), channel_id=1, source_target_pairs={{0,1},{1,0},{2,3},{3,2},{4,5},{5,4},{6,7},{7,6},{8,9},{9,8},{10,11... | collective-permute-start | bytes 786440 | tf_op jit(solution)/shard_map/ppermute | solution.py:197
  34.2 9.7 %collective-permute-start.13 = (bf16[32,4096]{1,0:T(8,128)(2,1)S(1)}, bf16[32,4096]{1,0:T(8,128)(2,1)}, u32[]{:S(2)}, u32[]{:S(2)}) collective-permute-start(bf16[32,4096]{1,0:T(8,128)(2,1)S(1)} %collective-permute-done.11.refs_12_), channel_id=1, source_target_pairs={{0,16},{1,9},{2,18},{3,11},{4,20},{5,13},{6,22},{7,15},{8,24},{9,1... | collective-permute-start | bytes 786440 | tf_op jit(solution)/shard_map/ppermute | solution.py:197
  36.7 9.3 %collective-permute-start.12 = (bf16[32,4096]{1,0:T(8,128)(2,1)S(1)}, bf16[32,4096]{1,0:T(8,128)(2,1)}, u32[]{:S(2)}, u32[]{:S(2)}) collective-permute-start(bf16[32,4096]{1,0:T(8,128)(2,1)S(1)} %collective-permute-done.11.refs_12_), channel_id=1, source_target_pairs={{0,8},{1,17},{2,10},{3,19},{4,12},{5,21},{6,14},{7,23},{8,0},{9,25... | collective-permute-start | bytes 786440 | tf_op jit(solution)/shard_map/ppermute | solution.py:197
  38.1 7.8 %collective-permute-start.25 = (bf16[32,4096]{1,0:T(8,128)(2,1)S(1)}, bf16[32,4096]{1,0:T(8,128)(2,1)S(1)}, u32[]{:S(2)}, u32[]{:S(2)}) collective-permute-start(bf16[32,4096]{1,0:T(8,128)(2,1)S(1)} %collective-permute-done.9.refs_10_), channel_id=1, source_target_pairs={{0,1},{1,0},{2,3},{3,2},{4,5},{5,4},{6,7},{7,6},{8,9},{9,8},{10,11... | collective-permute-start | bytes 786440 | tf_op jit(solution)/shard_map/ppermute | solution.py:197
  38.1 8.0 %collective-permute-start.24 = (bf16[32,4096]{1,0:T(8,128)(2,1)S(1)}, bf16[32,4096]{1,0:T(8,128)(2,1)S(1)}, u32[]{:S(2)}, u32[]{:S(2)}) collective-permute-start(bf16[32,4096]{1,0:T(8,128)(2,1)S(1)} %collective-permute-done.8.refs_9_), channel_id=1, source_target_pairs={{0,1},{1,0},{2,3},{3,2},{4,5},{5,4},{6,7},{7,6},{8,9},{9,8},{10,11... | collective-permute-start | bytes 786440 | tf_op jit(solution)/shard_map/ppermute | solution.py:197
  38.6 8.8 %collective-permute-start.10 = (bf16[32,4096]{1,0:T(8,128)(2,1)S(1)}, bf16[32,4096]{1,0:T(8,128)(2,1)}, u32[]{:S(2)}, u32[]{:S(2)}) collective-permute-start(bf16[32,4096]{1,0:T(8,128)(2,1)S(1)} %collective-permute-done.8.refs_9_), channel_id=1, source_target_pairs={{0,16},{1,9},{2,18},{3,11},{4,20},{5,13},{6,22},{7,15},{8,24},{9,1... | collective-permute-start | bytes 786440 | tf_op jit(solution)/shard_map/ppermute | solution.py:197
  43.9 4.6 %collective-permute-start.21 = (bf16[32,4096]{1,0:T(8,128)(2,1)S(1)}, bf16[32,4096]{1,0:T(8,128)(2,1)S(1)}, u32[]{:S(2)}, u32[]{:S(2)}) collective-permute-start(bf16[32,4096]{1,0:T(8,128)(2,1)S(1)} %collective-permute-done.5.refs_6_), channel_id=1, source_target_pairs={{0,1},{1,0},{2,3},{3,2},{4,5},{5,4},{6,7},{7,6},{8,9},{9,8},{10,11... | collective-permute-start | bytes 786440 | tf_op jit(solution)/shard_map/ppermute | solution.py:197
  45.9 2.5 %collective-permute-start.20 = (bf16[32,4096]{1,0:T(8,128)(2,1)S(1)}, bf16[32,4096]{1,0:T(8,128)(2,1)S(1)}, u32[]{:S(2)}, u32[]{:S(2)}) collective-permute-start(bf16[32,4096]{1,0:T(8,128)(2,1)S(1)} %collective-permute-done.4.refs_5_), channel_id=1, source_target_pairs={{0,1},{1,0},{2,3},{3,2},{4,5},{5,4},{6,7},{7,6},{8,9},{9,8},{10,11... | collective-permute-start | bytes 786440 | tf_op jit(solution)/shard_map/ppermute | solution.py:197
  46.0 6.5 %collective-permute-start.6 = (bf16[32,4096]{1,0:T(8,128)(2,1)S(1)}, bf16[32,4096]{1,0:T(8,128)(2,1)}, u32[]{:S(2)}, u32[]{:S(2)}) collective-permute-start(bf16[32,4096]{1,0:T(8,128)(2,1)S(1)} %collective-permute-done.4.refs_5_), channel_id=1, source_target_pairs={{0,16},{1,9},{2,18},{3,11},{4,20},{5,13},{6,22},{7,15},{8,24},{9,1... | collective-permute-start | bytes 786440 | tf_op jit(solution)/shard_map/ppermute | solution.py:197
  46.1 6.4 %collective-permute-start.18 = (bf16[32,4096]{1,0:T(8,128)(2,1)S(1)}, bf16[32,4096]{1,0:T(8,128)(2,1)S(1)}, u32[]{:S(2)}, u32[]{:S(2)}) collective-permute-start(bf16[32,4096]{1,0:T(8,128)(2,1)S(1)} %collective-permute-done.2.refs_3_), channel_id=1, source_target_pairs={{0,1},{1,0},{2,3},{3,2},{4,5},{5,4},{6,7},{7,6},{8,9},{9,8},{10,11... | collective-permute-start | bytes 786440 | tf_op jit(solution)/shard_map/ppermute | solution.py:197
  47.4 7.9 %collective-permute-start.14 = (bf16[32,4096]{1,0:T(8,128)(2,1)}, bf16[32,4096]{1,0:T(8,128)(2,1)}, u32[]{:S(2)}, u32[]{:S(2)}) collective-permute-start(bf16[32,4096]{1,0:T(8,128)(2,1)} %collective-permute-done.12.refs_13_), channel_id=1, source_target_pairs={{0,16},{1,9},{2,18},{3,11},{4,20},{5,13},{6,22},{7,15},{8,24},{9,1... | collective-permute-start | bytes 786440 | tf_op jit(solution)/shard_map/ppermute | solution.py:197
  48.4 9.4 %collective-permute-start.28 = (bf16[32,4096]{1,0:T(8,128)(2,1)}, bf16[32,4096]{1,0:T(8,128)(2,1)}, u32[]{:S(2)}, u32[]{:S(2)}) collective-permute-start(bf16[32,4096]{1,0:T(8,128)(2,1)} %collective-permute-done.12.refs_13_), channel_id=1, source_target_pairs={{0,1},{1,0},{2,3},{3,2},{4,5},{5,4},{6,7},{7,6},{8,9},{9,8},{10,11... | collective-permute-start | bytes 786440 | tf_op jit(solution)/shard_map/ppermute | solution.py:197
  48.4 9.4 %collective-permute-start.29 = (bf16[32,4096]{1,0:T(8,128)(2,1)}, bf16[32,4096]{1,0:T(8,128)(2,1)}, u32[]{:S(2)}, u32[]{:S(2)}) collective-permute-start(bf16[32,4096]{1,0:T(8,128)(2,1)} %collective-permute-done.13.refs_14_), channel_id=1, source_target_pairs={{0,1},{1,0},{2,3},{3,2},{4,5},{5,4},{6,7},{7,6},{8,9},{9,8},{10,11... | collective-permute-start | bytes 786440 | tf_op jit(solution)/shard_map/ppermute | solution.py:197
  52.5 5.3 %collective-permute-start.26 = (bf16[32,4096]{1,0:T(8,128)(2,1)}, bf16[32,4096]{1,0:T(8,128)(2,1)}, u32[]{:S(2)}, u32[]{:S(2)}) collective-permute-start(bf16[32,4096]{1,0:T(8,128)(2,1)} %collective-permute-done.10.refs_11_), channel_id=1, source_target_pairs={{0,1},{1,0},{2,3},{3,2},{4,5},{5,4},{6,7},{7,6},{8,9},{9,8},{10,11... | collective-permute-start | bytes 786440 | tf_op jit(solution)/shard_map/ppermute | solution.py:197
  52.5 5.3 %collective-permute-start.22 = (bf16[32,4096]{1,0:T(8,128)(2,1)}, bf16[32,4096]{1,0:T(8,128)(2,1)}, u32[]{:S(2)}, u32[]{:S(2)}) collective-permute-start(bf16[32,4096]{1,0:T(8,128)(2,1)} %collective-permute-done.6.refs_7_), channel_id=1, source_target_pairs={{0,1},{1,0},{2,3},{3,2},{4,5},{5,4},{6,7},{7,6},{8,9},{9,8},{10,11... | collective-permute-start | bytes 786440 | tf_op jit(solution)/shard_map/ppermute | solution.py:197
  55.3 2.5 %collective-permute-start.30 = (bf16[32,4096]{1,0:T(8,128)(2,1)}, bf16[32,4096]{1,0:T(8,128)(2,1)}, u32[]{:S(2)}, u32[]{:S(2)}) collective-permute-start(bf16[32,4096]{1,0:T(8,128)(2,1)} %collective-permute-done.14.refs_15_), channel_id=1, source_target_pairs={{0,1},{1,0},{2,3},{3,2},{4,5},{5,4},{6,7},{7,6},{8,9},{9,8},{10,11... | collective-permute-start | bytes 786440 | tf_op jit(solution)/shard_map/ppermute | solution.py:197
  (20 other events, 442.9 us)

commit v2 on v1

v2 whole, which is shorter than its diff:
```python
import functools
import numpy as np
import jax
import jax.numpy as jnp
from jax import lax
from jax.experimental import pallas as pl
from jax.experimental.pallas import tpu as pltpu
from jax.sharding import PartitionSpec as P


LAGS = 4
LAG_STEP = 8
BIN = 128
PAIR = 2
CHUNK = 512

LAG_SHIFTS = [(lag - LAGS // 2) * LAG_STEP for lag in range(LAGS)]
SHIFTS = sorted({s for t in LAG_SHIFTS for s in (t, -t)})
TABLE = sorted({abs(s) for s in SHIFTS if s != 0})

NT = (((1,), (1,)), ((), ()))


def phase_table(freqs):
    index = np.arange(freqs, dtype=np.float64)
    rows = []
    for shift in TABLE:
        theta = np.pi * index * shift / freqs
        rows += [np.cos(theta), np.sin(theta)]
    return jnp.asarray(np.stack(rows), jnp.float32)


def phase(table_ref, shift, cols):
    at = TABLE.index(abs(shift))
    cosine = table_ref[2 * at : 2 * at + 1, cols]
    sine = table_ref[2 * at + 1 : 2 * at + 2, cols]
    return cosine, (sine if shift > 0 else -sine)


def reverse_bits(value, n_bits):
    return sum(((value >> b) & 1) << (n_bits - 1 - b) for b in range(n_bits))


def whiten_kernel(raw_ref, gain_ref, out_ref):
    freqs = gain_ref.shape[1]
    raw = raw_ref[...].astype(jnp.float32)
    power = jnp.mean(raw * raw, axis=1, keepdims=True)
    factor = lax.rsqrt(power + 1e-05)
    gain = gain_ref[...]
    out_ref[:, :freqs] = (raw[:, :freqs] * factor * gain).astype(jnp.bfloat16)
    out_ref[:, freqs:] = (raw[:, freqs:] * factor * gain).astype(jnp.bfloat16)


def rotate_into(out_ref, row, source, table_ref, shift):
    rows, width = source.shape
    freqs = width // 2
    if shift == 0:
        out_ref[row : row + rows, :] = source[...]
        return
    for start in range(0, freqs, CHUNK):
        cols = slice(start, start + CHUNK)
        high = slice(freqs + start, freqs + start + CHUNK)
        cosine, sine = phase(table_ref, shift, cols)
        real = source[:, cols].astype(jnp.float32)
        imag = source[:, high].astype(jnp.float32)
        out_ref[row : row + rows, cols] = (real * cosine - imag * sine).astype(jnp.bfloat16)
        out_ref[row : row + rows, high] = (imag * cosine + real * sine).astype(jnp.bfloat16)


def rotate_kernel(table_ref, own_ref, out_ref):
    rows = own_ref.shape[0]
    for at, shift in enumerate(SHIFTS):
        rotate_into(out_ref, at * rows, own_ref, table_ref, shift)


class Place:
    def __init__(self, n_rows, n_cols, block):
        self.n_rows, self.n_cols, self.block = n_rows, n_cols, block
        self.n_bits = n_rows.bit_length() - 1
        self.row = lax.axis_index("rows")
        self.col = lax.axis_index("cols")
        self.line, self.core = self.col // PAIR, self.col % PAIR
        self.first = (self.row * n_cols + self.col) * block
        ratio = n_cols // n_rows
        self.owner = self.col // ratio
        self.col_base = (self.col % ratio) * n_rows

    def inside(self, dz):
        from_col = (self.line ^ dz) * PAIR
        return (from_col >= self.col_base) & (from_col < self.col_base + self.n_rows)

    def half(self, dz):
        return ((self.line ^ dz) * PAIR - self.col_base) // PAIR

    def of(self, dz, slot, plane):
        in_core = self.core ^ plane
        dr = jnp.where(in_core == 0, slot, reverse_bits(slot, self.n_bits))
        return self.row ^ dr, (self.line ^ dz) * PAIR + in_core


def gather_weights(place, dz, scores, bins_ref, lag_ref):
    block = place.block
    span = scores.shape[1]
    lane = lax.broadcasted_iota(jnp.int32, (block, span), 1)
    mine = place.first + lax.broadcasted_iota(jnp.int32, (block, span), 0)
    other = jnp.zeros((block, span), jnp.int32)
    spots = [place.of(dz, slot, plane) for plane in range(PAIR) for slot in range(place.n_rows)]
    for at, (from_row, from_col) in enumerate(spots):
        base = (from_row * place.n_cols + from_col) * block - at * block
        other = jnp.where(lane >= at * block, base + lane, other)
    distance = jnp.abs(mine - other) // BIN
    chosen = distance == bins_ref[0]
    for entry in range(1, bins_ref.shape[0]):
        chosen = chosen | (distance == bins_ref[entry])
    selected = chosen.astype(jnp.float32)
    weights = []
    for at, shift in enumerate(SHIFTS):
        factor = 0.0
        for lag, lag_shift in enumerate(LAG_SHIFTS):
            for sign in (1, -1):
                if sign * lag_shift == shift:
                    factor = factor + lag_ref[lag]
        part = scores[at * block : (at + 1) * block, :]
        weights.append((factor * selected * part).astype(jnp.bfloat16))
    return jnp.concatenate(weights, axis=0)


def stack(tiles, cols):
    return jnp.concatenate([tile[:, cols] for tile in tiles], axis=0)


def bundle_step(place, dz, tiles, bins_ref, lag_ref, turned_ref, old_ref, new_ref):
    width = tiles[0].shape[1]
    norm = 1.0 / np.sqrt(np.float32(width))
    scores = jnp.zeros((turned_ref.shape[0], len(tiles) * place.block), jnp.float32)
    for start in range(0, width, CHUNK):
        cols = slice(start, start + CHUNK)
        scores += lax.dot_general(
            turned_ref[:, cols], stack(tiles, cols), NT, preferred_element_type=jnp.float32
        )
    weights = gather_weights(place, dz, scores * norm, bins_ref, lag_ref)
    for start in range(0, width, CHUNK):
        cols = slice(start, start + CHUNK)
        term = jnp.dot(weights, stack(tiles, cols), preferred_element_type=jnp.float32)
        new_ref[:, cols] = term if old_ref is None else old_ref[:, cols] + term


def pick_step(place, dz, tiles, table_ref, staged_ref, picked_ref):
    block, n_rows = place.block, place.n_rows

    @pl.when(place.inside(dz))
    def _():
        for plane in range(PAIR):
            for slot in range(n_rows):
                from_row, from_col = place.of(dz, slot, plane)
                start = pl.multiple_of((from_col % PAIR) * block, block)

                @pl.when(from_row == place.owner)
                def _():
                    staged_ref[pl.ds(start, block), :] = tiles[plane * n_rows + slot][...]

        for lag, shift in enumerate(LAG_SHIFTS):
            rotate_into(picked_ref, lag * PAIR * block, staged_ref, table_ref, -shift)


def corr_step(place, dz, lines, picked_ref, part_ref):
    block = place.block

    @pl.when(place.inside(dz))
    def _():
        for at, tile in enumerate(lines):
            _, from_col = place.of(at // PAIR, 0, at % PAIR)
            spot = pl.multiple_of(from_col * block, block)
            part_ref[pl.ds(place.half(dz), 1), pl.ds(spot, block), :] = lax.dot_general(
                tile[...], picked_ref[...], NT, preferred_element_type=jnp.float32
            )[None]


def bundle_kernel(sizes, dz, fresh, bins_ref, lag_ref, table_ref, turned_ref, *refs):
    n_rows, n_cols = sizes
    tiles = refs[: PAIR * n_rows]
    total_ref, picked_ref, staged_ref = refs[-3:]
    place = Place(n_rows, n_cols, tiles[0].shape[0])
    pick_step(place, dz, tiles, table_ref, staged_ref, picked_ref)
    old_ref = None if fresh else refs[PAIR * n_rows]
    bundle_step(place, dz, tiles, bins_ref, lag_ref, turned_ref, old_ref, total_ref)


def corr_kernel(sizes, *refs):
    n_rows, n_cols = sizes
    lines, picked, part_ref = refs[:n_cols], refs[n_cols:-1], refs[-1]
    place = Place(n_rows, n_cols, lines[0].shape[0])
    for dz, picked_ref in enumerate(picked):
        corr_step(place, dz, lines, picked_ref, part_ref)


def end_kernel(sizes, dz, bins_ref, lag_ref, table_ref, turned_ref, *refs):
    n_rows, n_cols = sizes
    count = PAIR * n_rows
    tiles, lines = refs[:count], refs[count : count + n_cols]
    old_ref, old_part_ref, corr_ref, grad_ref, total_ref, staged_ref, picked_ref, part_ref = refs[count + n_cols :]
    block, width = tiles[0].shape
    freqs = width // 2
    norm = 1.0 / np.sqrt(np.float32(width))
    place = Place(n_rows, n_cols, block)
    bundle_step(place, dz, tiles, bins_ref, lag_ref, turned_ref, old_ref, total_ref)

    for start in range(0, freqs, CHUNK):
        cols = slice(start, start + CHUNK)
        high = slice(freqs + start, freqs + start + CHUNK)
        real_sum = jnp.zeros((block, CHUNK), jnp.float32)
        imag_sum = jnp.zeros((block, CHUNK), jnp.float32)
        for at, shift in enumerate(SHIFTS):
            real = total_ref[at * block : (at + 1) * block, cols]
            imag = total_ref[at * block : (at + 1) * block, high]
            if shift == 0:
                real_sum, imag_sum = real_sum + real, imag_sum + imag
            else:
                cosine, sine = phase(table_ref, shift, cols)
                real_sum += real * cosine + imag * sine
                imag_sum += imag * cosine - real * sine
        grad_ref[:, cols] = real_sum * norm
        grad_ref[:, high] = imag_sum * norm

    pick_step(place, dz, tiles, table_ref, staged_ref, picked_ref)
    corr_step(place, dz, lines, picked_ref, part_ref)
    here = place.inside(dz)
    wide = PAIR * block
    for lag in range(LAGS):
        cols = slice(lag * wide, (lag + 1) * wide)
        halves = []
        for half in range(part_ref.shape[0]):
            fresh = here & (place.half(dz) == half)
            halves.append(jnp.where(fresh, part_ref[half, :, cols], old_part_ref[half, :, cols]))
        corr_ref[lag] = jnp.concatenate(halves, axis=1) * norm


def per_device(spectra, band_weights, lag_weights, selected_bins):
    n_rows = lax.axis_size("rows")
    n_cols = lax.axis_size("cols")
    n_lines = n_cols // PAIR
    n_bits = n_rows.bit_length() - 1
    block, width = spectra.shape
    freqs = width // 2
    vmem = pl.BlockSpec(memory_space=pltpu.VMEM)
    smem = pl.BlockSpec(memory_space=pltpu.SMEM)
    table = phase_table(freqs)

    def send(value, move):
        pairs = []
        for r in range(n_rows):
            for c in range(n_cols):
                to_row, to_line, to_core = move(r, c // PAIR, c % PAIR)
                pairs.append((r * n_cols + c, to_row * n_cols + to_line * PAIR + to_core))
        return lax.ppermute(value, ("rows", "cols"), pairs)

    def send_row(value, bit):
        return send(value, lambda r, z, k: (r ^ (1 << (bit if k == 0 else n_bits - 1 - bit)), z, k))

    def send_line(value, step):
        return send(value, lambda r, z, k: (r, z ^ step, k))

    def call(kernel, outs, operands, specs, limit, **more):
        return pl.pallas_call(
            kernel,
            out_shape=outs,
            in_specs=specs,
            out_specs=jax.tree.map(lambda _: vmem, outs),
            compiler_params=pltpu.CompilerParams(vmem_limit_bytes=limit << 20),
            **more,
        )(*operands)

    def shape(rows, dtype, *last):
        return jax.ShapeDtypeStruct((rows, *(last or (width,))), dtype)

    whitened = call(
        whiten_kernel, shape(block, jnp.bfloat16), (spectra, band_weights[None, :]), [vmem] * 2, 4
    )
    turned = call(
        rotate_kernel, shape(len(SHIFTS) * block, jnp.bfloat16), (table, whitened), [vmem] * 2, 8
    )
    lines = [whitened]
    for dz in range(1, n_lines):
        low = dz & -dz
        lines.append(send_line(lines[dz ^ low], low))
    groups = []
    for dz in range(n_lines):
        group = [lines[dz]]
        for slot in range(1, n_rows):
            if dz % 2 and slot == n_rows - 1:
                group.append(send_line(groups[dz ^ 1][slot], 1))
            else:
                high = slot.bit_length() - 1
                group.append(send_row(group[slot ^ (1 << high)], high))
        groups.append(group)
    swapped = [[send(tile, lambda r, z, k: (r, z, k ^ 1)) for tile in group] for group in groups]
    n_row, n_col = n_cols * block, n_rows * block
    sizes = (n_rows, n_cols)
    total = shape(len(SHIFTS) * block, jnp.float32)
    picked_shape = shape(LAGS * PAIR * block, jnp.bfloat16)
    staged = pltpu.VMEM((PAIR * block, width), jnp.bfloat16)
    part_shape = (n_rows // PAIR, n_row, LAGS * PAIR * block)
    state, picked = [], []
    for dz in range(n_lines - 1):
        operands = [selected_bins, lag_weights, table, turned, *groups[dz], *swapped[dz]]
        base = len(operands)
        operands += state
        new_state, new_picked = call(
            functools.partial(bundle_kernel, sizes, dz, not state),
            (total, picked_shape),
            operands,
            [smem] * 2 + [vmem] * (len(operands) - 2),
            20,
            scratch_shapes=[staged],
            input_output_aliases={base: 0} if state else {},
        )
        state = [new_state]
        picked.append(new_picked)
    last = n_lines - 1
    lines = [pair[dz][0] for dz in range(n_lines) for pair in (groups, swapped)]
    parts = call(
        functools.partial(corr_kernel, sizes),
        shape(part_shape[0], jnp.float32, *part_shape[1:]),
        [*lines, *picked],
        [vmem] * (n_cols + n_lines - 1),
        20 if n_lines <= n_rows else 40,
    )
    operands = [selected_bins, lag_weights, table, turned, *groups[last], *swapped[last], *lines, *state, parts]
    correlations, gradient = call(
        functools.partial(end_kernel, sizes, last),
        (shape(LAGS, jnp.float32, n_row, n_col), shape(block, jnp.float32)),
        operands,
        [smem] * 2 + [vmem] * (len(operands) - 2),
        36,
        scratch_shapes=[
            pltpu.VMEM(total.shape, total.dtype),
            staged,
            pltpu.VMEM(picked_shape.shape, picked_shape.dtype),
            pltpu.VMEM(part_shape, jnp.float32),
        ],
    )
    return correlations, gradient


def solution(mesh):
    placed = (P(("rows", "cols"), None), P(), P(), P())
    return jax.shard_map(
        per_device,
        mesh=mesh,
        in_specs=placed,
        out_specs=(P(None, "rows", "cols"), P(("rows", "cols"), None)),
        check_vma=False,
    )
```

time: 80.5 us -> 78.7 us (0.978)
  Pallas kernels: 26.5 us -> 22.7 us
  local copies, waits for them, and re-layouts: 0.08 us -> 2.42 us
  starting transfers between devices: 24.5 us -> 22.8 us
  waiting for transfers between devices: 28.2 us -> 29.8 us
    pallas_call x3 -> x7, Pallas kernels: 26.5 us -> 22.7 us  [call(): pl.pallas_call(kernel, out_shape=outs, in_specs=specs, out_specs=jax.tree...]
    unnamed x42 -> x10, local copies, waits for them, and re-layouts: 0.08 us -> 2.42 us
    ppermute x31, starting transfers between devices: 24.5 us -> 22.8 us  [send(): return lax.ppermute(value, ('rows', 'cols'), pairs)]
    ppermute x31, waiting for transfers between devices: 28.2 us -> 29.8 us  [send(): return lax.ppermute(value, ('rows', 'cols'), pairs)]
  transfers between devices with their start and end apart: 31 -> 31, of which waited for: 9 -> 9; matrix products, arithmetic and copies ran while one was open for 0% -> 0% of each run, Pallas kernels for 3% -> 24%
where the time goes in v2:
time: 78.7 us; the launch traced here: 78.5 us
  waiting for transfers between devices  29.8 us (38%)
  starting transfers between devices  22.8 us (29%)
  Pallas kernels  22.7 us (29%)
  local copies, waits for them, and re-layouts  2.42 us (3%)
    ppermute x31, waiting for transfers between devices, send(): return lax.ppermute(value, ('rows', 'cols'), pairs)  29.8 us
    ppermute x31, starting transfers between devices, send(): return lax.ppermute(value, ('rows', 'cols'), pairs)  22.8 us
    pallas_call x7, Pallas kernels, call(): pl.pallas_call(kernel, out_shape=outs, in_specs=specs, out_specs=jax.tree...  22.7 us
    unnamed x10, local copies, waits for them, and re-layouts  2.42 us
  transfers between devices with their start and end apart: 31, of which 9 were waited for; matrix products, arithmetic and copies ran while one was open for 0% of the time, Pallas kernels for 24%

profile of v2, /device:TPU:0, one launch (start us, length us, event | category | flops | bytes accessed | tf_op | source)
XLA Modules:
  0.0 78.5 jit_solution(10833101549442063654)
XLA Ops:
  0.7 1.0 %copy-done.1 = bf16[32,4096]{1,0:T(8,128)(2,1)S(1)} copy-done((bf16[32,4096]{1,0:T(8,128)(2,1)S(1)}, bf16[32,4096]{1,0:T(8,128)(2,1)}, u32[]{:S(2)}) %copy-start.1) | copy-done | bytes 262168
  1.6 0.7 copy-done.2
  2.5 3.0 %collective-permute-start.21 = (bf16[32,4096]{1,0:T(8,128)(2,1)S(1)}, bf16[32,4096]{1,0:T(8,128)(2,1)S(1)}, u32[]{:S(2)}, u32[]{:S(2)}) collective-permute-start(bf16[32,4096]{1,0:T(8,128)(2,1)S(1)} %shard_map.68.own_ref.refs_0_.refs_8_), channel_id=1, source_target_pairs={{0,8},{1,17},{2,10},{3,19},{4,12},{5,21},{6,14},{7,23},{8,0},{9,25... | collective-permute-start | bytes 786440 | tf_op jit(solution)/shard_map/ppermute | solution.py:255
  5.5 1.5 %collective-permute-start.27 = (bf16[32,4096]{1,0:T(8,128)(2,1)S(1)}, bf16[32,4096]{1,0:T(8,128)(2,1)S(1)}, u32[]{:S(2)}, u32[]{:S(2)}) collective-permute-start(bf16[32,4096]{1,0:T(8,128)(2,1)S(1)} %shard_map.68.own_ref.refs_0_.refs_8_), channel_id=1, source_target_pairs={{0,16},{1,9},{2,18},{3,11},{4,20},{5,13},{6,22},{7,15},{8,24},{9,1... | collective-permute-start | bytes 786440 | tf_op jit(solution)/shard_map/ppermute | solution.py:255
  7.0 1.6 %collective-permute-start.12 = (bf16[32,4096]{1,0:T(8,128)(2,1)S(1)}, bf16[32,4096]{1,0:T(8,128)(2,1)S(1)}, u32[]{:S(2)}, u32[]{:S(2)}) collective-permute-start(bf16[32,4096]{1,0:T(8,128)(2,1)S(1)} %shard_map.68.own_ref.refs_0_.refs_8_), channel_id=1, source_target_pairs={{0,2},{1,3},{2,0},{3,1},{4,6},{5,7},{6,4},{7,5},{8,10},{9,11},{10,... | collective-permute-start | bytes 786440 | tf_op jit(solution)/shard_map/ppermute | solution.py:255
  8.6 2.6 %collective-permute-start = (bf16[32,4096]{1,0:T(8,128)(2,1)S(1)}, bf16[32,4096]{1,0:T(8,128)(2,1)S(1)}, u32[]{:S(2)}, u32[]{:S(2)}) collective-permute-start(bf16[32,4096]{1,0:T(8,128)(2,1)S(1)} %shard_map.68.own_ref.refs_0_.refs_8_), channel_id=1, source_target_pairs={{0,4},{1,5},{2,6},{3,7},{4,0},{5,1},{6,2},{7,3},{8,12},{9,13},{10,... | collective-permute-start | bytes 786440 | tf_op jit(solution)/shard_map/ppermute | solution.py:255
  11.2 0.9 %collective-permute-done.21.refs_1_ = bf16[32,4096]{1,0:T(8,128)(2,1)S(1)} collective-permute-done((bf16[32,4096]{1,0:T(8,128)(2,1)S(1)}, bf16[32,4096]{1,0:T(8,128)(2,1)S(1)}, u32[]{:S(2)}, u32[]{:S(2)}) %collective-permute-start.21) | collective-permute-done | bytes 262176 | tf_op jit(solution)/shard_map/ppermute | solution.py:255
  12.1 1.6 %collective-permute-start.22 = (bf16[32,4096]{1,0:T(8,128)(2,1)S(1)}, bf16[32,4096]{1,0:T(8,128)(2,1)S(1)}, u32[]{:S(2)}, u32[]{:S(2)}) collective-permute-start(bf16[32,4096]{1,0:T(8,128)(2,1)S(1)} %collective-permute-done.21.refs_1_), channel_id=1, source_target_pairs={{0,16},{1,9},{2,18},{3,11},{4,20},{5,13},{6,22},{7,15},{8,24},{9,1... | collective-permute-start | bytes 786440 | tf_op jit(solution)/shard_map/ppermute | solution.py:255
  14.2 5.8 %collective-permute-done.12.refs_0_.refs_2_.refs_10_ = bf16[32,4096]{1,0:T(8,128)(2,1)S(1)} collective-permute-done((bf16[32,4096]{1,0:T(8,128)(2,1)S(1)}, bf16[32,4096]{1,0:T(8,128)(2,1)S(1)}, u32[]{:S(2)}, u32[]{:S(2)}) %collective-permute-start.12) | collective-permute-done | bytes 262176 | tf_op jit(solution)/shard_map/ppermute | solution.py:255
  20.0 2.4 %collective-permute-done.refs_0_.refs_4_.refs_12_ = bf16[32,4096]{1,0:T(8,128)(2,1)S(1)} collective-permute-done((bf16[32,4096]{1,0:T(8,128)(2,1)S(1)}, bf16[32,4096]{1,0:T(8,128)(2,1)S(1)}, u32[]{:S(2)}, u32[]{:S(2)}) %collective-permute-start) | collective-permute-done | bytes 262176 | tf_op jit(solution)/shard_map/ppermute | solution.py:255
  22.4 1.5 %collective-permute-start.19 = (bf16[32,4096]{1,0:T(8,128)(2,1)S(1)}, bf16[32,4096]{1,0:T(8,128)(2,1)S(1)}, u32[]{:S(2)}, u32[]{:S(2)}) collective-permute-start(bf16[32,4096]{1,0:T(8,128)(2,1)S(1)} %collective-permute-done.12.refs_0_.refs_2_.refs_10_), channel_id=1, source_target_pairs={{0,8},{1,17},{2,10},{3,19},{4,12},{5,21},{6,14},{7,23},{8,0},{9,25... | collective-permute-start | bytes 786440 | tf_op jit(solution)/shard_map/ppermute | solution.py:255
  23.8 1.5 %collective-permute-start.20 = (bf16[32,4096]{1,0:T(8,128)(2,1)S(1)}, bf16[32,4096]{1,0:T(8,128)(2,1)S(1)}, u32[]{:S(2)}, u32[]{:S(2)}) collective-permute-start(bf16[32,4096]{1,0:T(8,128)(2,1)S(1)} %collective-permute-done.12.refs_0_.refs_2_.refs_10_), channel_id=1, source_target_pairs={{0,16},{1,9},{2,18},{3,11},{4,20},{5,13},{6,22},{7,15},{8,24},{9,1... | collective-permute-start | bytes 786440 | tf_op jit(solution)/shard_map/ppermute | solution.py:255
  25.4 0.5 collective-permute-start.4
  25.9 0.6 collective-permute-start.15
  26.5 4.4 %collective-permute-done.19.refs_1_ = bf16[32,4096]{1,0:T(8,128)(2,1)S(1)} collective-permute-done((bf16[32,4096]{1,0:T(8,128)(2,1)S(1)}, bf16[32,4096]{1,0:T(8,128)(2,1)S(1)}, u32[]{:S(2)}, u32[]{:S(2)}) %collective-permute-start.19) | collective-permute-done | bytes 262176 | tf_op jit(solution)/shard_map/ppermute | solution.py:255
  30.9 1.1 %collective-permute-start.1 = (bf16[32,4096]{1,0:T(8,128)(2,1)S(1)}, bf16[32,4096]{1,0:T(8,128)(2,1)S(1)}, u32[]{:S(2)}, u32[]{:S(2)}) collective-permute-start(bf16[32,4096]{1,0:T(8,128)(2,1)S(1)} %collective-permute-done.refs_0_.refs_4_.refs_12_), channel_id=1, source_target_pairs={{0,2},{1,3},{2,0},{3,1},{4,6},{5,7},{6,4},{7,5},{8,10},{9,11},{10,... | collective-permute-start | bytes 786440 | tf_op jit(solution)/shard_map/ppermute | solution.py:255
  32.0 3.6 %collective-permute-done.4.refs_1_ = bf16[32,4096]{1,0:T(8,128)(2,1)S(1)} collective-permute-done((bf16[32,4096]{1,0:T(8,128)(2,1)S(1)}, bf16[32,4096]{1,0:T(8,128)(2,1)S(1)}, u32[]{:S(2)}, u32[]{:S(2)}) %collective-permute-start.4) | collective-permute-done | bytes 262176 | tf_op jit(solution)/shard_map/ppermute | solution.py:255
  35.6 0.5 collective-permute-start.25
  36.1 1.8 %collective-permute-start.23 = (bf16[32,4096]{1,0:T(8,128)(2,1)S(1)}, bf16[32,4096]{1,0:T(8,128)(2,1)S(1)}, u32[]{:S(2)}, u32[]{:S(2)}) collective-permute-start(bf16[32,4096]{1,0:T(8,128)(2,1)S(1)} %collective-permute-done.22.refs_3_), channel_id=1, source_target_pairs={{0,2},{1,3},{2,0},{3,1},{4,6},{5,7},{6,4},{7,5},{8,10},{9,11},{10,... | collective-permute-start | bytes 786440 | tf_op jit(solution)/shard_map/ppermute | solution.py:255
  38.2 0.9 %collective-permute-start.16 = (bf16[32,4096]{1,0:T(8,128)(2,1)S(1)}, bf16[32,4096]{1,0:T(8,128)(2,1)S(1)}, u32[]{:S(2)}, u32[]{:S(2)}) collective-permute-start(bf16[32,4096]{1,0:T(8,128)(2,1)S(1)} %collective-permute-done.4.refs_1_), channel_id=1, source_target_pairs={{0,1},{1,0},{2,3},{3,2},{4,5},{5,4},{6,7},{7,6},{8,9},{9,8},{10,11... | collective-permute-start | bytes 786440 | tf_op jit(solution)/shard_map/ppermute | solution.py:255
  39.2 1.3 %collective-permute-start.2 = (bf16[32,4096]{1,0:T(8,128)(2,1)S(1)}, bf16[32,4096]{1,0:T(8,128)(2,1)S(1)}, u32[]{:S(2)}, u32[]{:S(2)}) collective-permute-start(bf16[32,4096]{1,0:T(8,128)(2,1)S(1)} %collective-permute-done.1.refs_6_.refs_0_.refs_14_), channel_id=1, source_target_pairs={{0,8},{1,17},{2,10},{3,19},{4,12},{5,21},{6,14},{7,23},{8,0},{9,25... | collective-permute-start | bytes 786440 | tf_op jit(solution)/shard_map/ppermute | solution.py:255
  40.5 4.0 %collective-permute-done.23.refs_3_ = bf16[32,4096]{1,0:T(8,128)(2,1)S(1)} collective-permute-done((bf16[32,4096]{1,0:T(8,128)(2,1)S(1)}, bf16[32,4096]{1,0:T(8,128)(2,1)S(1)}, u32[]{:S(2)}, u32[]{:S(2)}) %collective-permute-start.23) | collective-permute-done | bytes 262176 | tf_op jit(solution)/shard_map/ppermute | solution.py:255
  44.9 1.4 %collective-permute-done.5.refs_3_ = bf16[32,4096]{1,0:T(8,128)(2,1)S(1)} collective-permute-done((bf16[32,4096]{1,0:T(8,128)(2,1)S(1)}, bf16[32,4096]{1,0:T(8,128)(2,1)S(1)}, u32[]{:S(2)}, u32[]{:S(2)}) %collective-permute-start.5) | collective-permute-done | bytes 262176 | tf_op jit(solution)/shard_map/ppermute | solution.py:255
  47.3 3.5 %collective-permute-done.3.refs_2_ = bf16[32,4096]{1,0:T(8,128)(2,1)S(1)} collective-permute-done((bf16[32,4096]{1,0:T(8,128)(2,1)S(1)}, bf16[32,4096]{1,0:T(8,128)(2,1)S(1)}, u32[]{:S(2)}, u32[]{:S(2)}) %collective-permute-start.3) | collective-permute-done | bytes 262176 | tf_op jit(solution)/shard_map/ppermute | solution.py:255
  50.8 0.5 collective-permute-start.9
  51.3 3.8 %collective-permute-done.6.refs_3_ = bf16[32,4096]{1,0:T(8,128)(2,1)S(1)} collective-permute-done((bf16[32,4096]{1,0:T(8,128)(2,1)S(1)}, bf16[32,4096]{1,0:T(8,128)(2,1)S(1)}, u32[]{:S(2)}, u32[]{:S(2)}) %collective-permute-start.6) | collective-permute-done | bytes 262176 | tf_op jit(solution)/shard_map/ppermute | solution.py:255
  55.1 0.8 copy-done
  56.2 3.0 %shard_map.70 = (f32[160,4096]{1,0:T(8,128)S(1)}, bf16[256,4096]{1,0:T(8,128)(2,1)S(1)}) custom-call(s32[8]{0:T(128)S(1)} %copy-done.3, f32[4]{0:T(128)S(1)} %copy-done.4, f32[4,2048]{1,0:T(4,128)S(1)} %copy-done, bf16[160,4096]{1,0:T(8,128)(2,1)S(1)} %shard_map.69.turned_ref, bf16[32,4096]{1,0:T(8,128)(2,1)S(1)} %shard_map.68.own_ref.refs_0_.refs_8_, ...), custom_call_target="tpu_custom_call" | custom-call | tf_op jit(solution)/shard_map/pallas_call | solution.py:264
  59.2 3.2 %shard_map.71 = (f32[160,4096]{1,0:T(8,128)S(1)}, bf16[256,4096]{1,0:T(8,128)(2,1)S(1)}) custom-call(s32[8]{0:T(128)S(1)} %copy-done.3, f32[4]{0:T(128)S(1)} %copy-done.4, f32[4,2048]{1,0:T(4,128)S(1)} %copy-done, bf16[160,4096]{1,0:T(8,128)(2,1)S(1)} %shard_map.69.turned_ref, ...), custom_call_target="tpu_custom_call", output_to_operand_aliasing={{0}: (12, {})} | custom-call | tf_op jit(solution)/shard_map/pallas_call | solution.py:264
  62.4 2.5 %shard_map.72 = (f32[160,4096]{1,0:T(8,128)S(1)}, bf16[256,4096]{1,0:T(8,128)(2,1)S(1)}) custom-call(s32[8]{0:T(128)S(1)} %copy-done.3, f32[4]{0:T(128)S(1)} %copy-done.4, f32[4,2048]{1,0:T(4,128)S(1)} %copy-done, bf16[160,4096]{1,0:T(8,128)(2,1)S(1)} %shard_map.69.turned_ref, ...), custom_call_target="tpu_custom_call", output_to_operand_aliasing={{0}: (12, {})} | custom-call | tf_op jit(solution)/shard_map/pallas_call | solution.py:264
  65.0 9.8 %shard_map.73.refs_17_ = f32[2,256,256]{2,1,0:T(8,128)S(1)} custom-call(bf16[32,4096]{1,0:T(8,128)(2,1)S(1)} %shard_map.68.own_ref.refs_0_.refs_8_, bf16[32,4096]{1,0:T(8,128)(2,1)S(1)} %collective-permute-done.11.refs_4_.refs_1_.refs_9_, bf16[32,4096]{1,0:T(8,128)(2,1)S(1)} %collective-permute-done.12.refs_0_.refs_2_.refs_10_, ...), custom_call_target="tpu_custom_call" | custom-call | tf_op jit(solution)/shard_map/pallas_call | solution.py:264
  74.9 3.6 %shard_map.74 = (f32[4,256,128]{2,1,0:T(8,128)}, f32[32,4096]{1,0:T(8,128)}) custom-call(s32[8]{0:T(128)S(1)} %copy-done.3, f32[4]{0:T(128)S(1)} %copy-done.4, f32[4,2048]{1,0:T(4,128)S(1)} %copy-done, bf16[160,4096]{1,0:T(8,128)(2,1)S(1)} %shard_map.69.turned_ref, bf16[32,4096]{1,0:T(8,128)(2,1)S(1)} %collective-permute-done.1.refs_6_.refs_0_.refs_14_, ...), custom_call_target="tpu_custom_call" | custom-call | tf_op jit(solution)/shard_map/pallas_call | solution.py:264
  (47 shorter events, 2.9 us)
Async XLA Ops:
  0.6 55.6 %copy-start.4 = (f32[4]{0:T(128)S(1)}, f32[4]{0:T(128)}, u32[]{:S(2)}) copy-start(f32[4]{0:T(128)} %lag_ref.7) | copy-start | bytes 52
  2.5 9.6 %collective-permute-start.21 = (bf16[32,4096]{1,0:T(8,128)(2,1)S(1)}, bf16[32,4096]{1,0:T(8,128)(2,1)S(1)}, u32[]{:S(2)}, u32[]{:S(2)}) collective-permute-start(bf16[32,4096]{1,0:T(8,128)(2,1)S(1)} %shard_map.68.own_ref.refs_0_.refs_8_), channel_id=1, source_target_pairs={{0,8},{1,17},{2,10},{3,19},{4,12},{5,21},{6,14},{7,23},{8,0},{9,25... | collective-permute-start | bytes 786440 | tf_op jit(solution)/shard_map/ppermute | solution.py:255
  5.5 8.2 %collective-permute-start.11 = (bf16[32,4096]{1,0:T(8,128)(2,1)S(1)}, bf16[32,4096]{1,0:T(8,128)(2,1)S(1)}, u32[]{:S(2)}, u32[]{:S(2)}) collective-permute-start(bf16[32,4096]{1,0:T(8,128)(2,1)S(1)} %shard_map.68.own_ref.refs_0_.refs_8_), channel_id=1, source_target_pairs={{0,1},{1,0},{2,3},{3,2},{4,5},{5,4},{6,7},{7,6},{8,9},{9,8},{10,11... | collective-permute-start | bytes 786440 | tf_op jit(solution)/shard_map/ppermute | solution.py:255
  5.5 8.2 %collective-permute-start.27 = (bf16[32,4096]{1,0:T(8,128)(2,1)S(1)}, bf16[32,4096]{1,0:T(8,128)(2,1)S(1)}, u32[]{:S(2)}, u32[]{:S(2)}) collective-permute-start(bf16[32,4096]{1,0:T(8,128)(2,1)S(1)} %shard_map.68.own_ref.refs_0_.refs_8_), channel_id=1, source_target_pairs={{0,16},{1,9},{2,18},{3,11},{4,20},{5,13},{6,22},{7,15},{8,24},{9,1... | collective-permute-start | bytes 786440 | tf_op jit(solution)/shard_map/ppermute | solution.py:255
  7.0 13.0 %collective-permute-start.12 = (bf16[32,4096]{1,0:T(8,128)(2,1)S(1)}, bf16[32,4096]{1,0:T(8,128)(2,1)S(1)}, u32[]{:S(2)}, u32[]{:S(2)}) collective-permute-start(bf16[32,4096]{1,0:T(8,128)(2,1)S(1)} %shard_map.68.own_ref.refs_0_.refs_8_), channel_id=1, source_target_pairs={{0,2},{1,3},{2,0},{3,1},{4,6},{5,7},{6,4},{7,5},{8,10},{9,11},{10,... | collective-permute-start | bytes 786440 | tf_op jit(solution)/shard_map/ppermute | solution.py:255
  8.6 13.8 %collective-permute-start = (bf16[32,4096]{1,0:T(8,128)(2,1)S(1)}, bf16[32,4096]{1,0:T(8,128)(2,1)S(1)}, u32[]{:S(2)}, u32[]{:S(2)}) collective-permute-start(bf16[32,4096]{1,0:T(8,128)(2,1)S(1)} %shard_map.68.own_ref.refs_0_.refs_8_), channel_id=1, source_target_pairs={{0,4},{1,5},{2,6},{3,7},{4,0},{5,1},{6,2},{7,3},{8,12},{9,13},{10,... | collective-permute-start | bytes 786440 | tf_op jit(solution)/shard_map/ppermute | solution.py:255
  12.1 11.7 %collective-permute-start.22 = (bf16[32,4096]{1,0:T(8,128)(2,1)S(1)}, bf16[32,4096]{1,0:T(8,128)(2,1)S(1)}, u32[]{:S(2)}, u32[]{:S(2)}) collective-permute-start(bf16[32,4096]{1,0:T(8,128)(2,1)S(1)} %collective-permute-done.21.refs_1_), channel_id=1, source_target_pairs={{0,16},{1,9},{2,18},{3,11},{4,20},{5,13},{6,22},{7,15},{8,24},{9,1... | collective-permute-start | bytes 786440 | tf_op jit(solution)/shard_map/ppermute | solution.py:255
  13.7 11.7 %collective-permute-start.28 = (bf16[32,4096]{1,0:T(8,128)(2,1)S(1)}, bf16[32,4096]{1,0:T(8,128)(2,1)S(1)}, u32[]{:S(2)}, u32[]{:S(2)}) collective-permute-start(bf16[32,4096]{1,0:T(8,128)(2,1)S(1)} %collective-permute-done.21.refs_1_), channel_id=1, source_target_pairs={{0,1},{1,0},{2,3},{3,2},{4,5},{5,4},{6,7},{7,6},{8,9},{9,8},{10,11... | collective-permute-start | bytes 786440 | tf_op jit(solution)/shard_map/ppermute | solution.py:255
  13.7 12.2 %collective-permute-start.29 = (bf16[32,4096]{1,0:T(8,128)(2,1)S(1)}, bf16[32,4096]{1,0:T(8,128)(2,1)S(1)}, u32[]{:S(2)}, u32[]{:S(2)}) collective-permute-start(bf16[32,4096]{1,0:T(8,128)(2,1)S(1)} %collective-permute-done.27.refs_2_), channel_id=1, source_target_pairs={{0,1},{1,0},{2,3},{3,2},{4,5},{5,4},{6,7},{7,6},{8,9},{9,8},{10,11... | collective-permute-start | bytes 786440 | tf_op jit(solution)/shard_map/ppermute | solution.py:255
  20.0 5.9 %collective-permute-start.13 = (bf16[32,4096]{1,0:T(8,128)(2,1)S(1)}, bf16[32,4096]{1,0:T(8,128)(2,1)S(1)}, u32[]{:S(2)}, u32[]{:S(2)}) collective-permute-start(bf16[32,4096]{1,0:T(8,128)(2,1)S(1)} %collective-permute-done.12.refs_0_.refs_2_.refs_10_), channel_id=1, source_target_pairs={{0,1},{1,0},{2,3},{3,2},{4,5},{5,4},{6,7},{7,6},{8,9},{9,8},{10,11... | collective-permute-start | bytes 786440 | tf_op jit(solution)/shard_map/ppermute | solution.py:255
  22.4 8.5 %collective-permute-start.19 = (bf16[32,4096]{1,0:T(8,128)(2,1)S(1)}, bf16[32,4096]{1,0:T(8,128)(2,1)S(1)}, u32[]{:S(2)}, u32[]{:S(2)}) collective-permute-start(bf16[32,4096]{1,0:T(8,128)(2,1)S(1)} %collective-permute-done.12.refs_0_.refs_2_.refs_10_), channel_id=1, source_target_pairs={{0,8},{1,17},{2,10},{3,19},{4,12},{5,21},{6,14},{7,23},{8,0},{9,25... | collective-permute-start | bytes 786440 | tf_op jit(solution)/shard_map/ppermute | solution.py:255
  23.8 8.2 %collective-permute-start.20 = (bf16[32,4096]{1,0:T(8,128)(2,1)S(1)}, bf16[32,4096]{1,0:T(8,128)(2,1)S(1)}, u32[]{:S(2)}, u32[]{:S(2)}) collective-permute-start(bf16[32,4096]{1,0:T(8,128)(2,1)S(1)} %collective-permute-done.12.refs_0_.refs_2_.refs_10_), channel_id=1, source_target_pairs={{0,16},{1,9},{2,18},{3,11},{4,20},{5,13},{6,22},{7,15},{8,24},{9,1... | collective-permute-start | bytes 786440 | tf_op jit(solution)/shard_map/ppermute | solution.py:255
  25.4 10.2 %collective-permute-start.4 = (bf16[32,4096]{1,0:T(8,128)(2,1)S(1)}, bf16[32,4096]{1,0:T(8,128)(2,1)S(1)}, u32[]{:S(2)}, u32[]{:S(2)}) collective-permute-start(bf16[32,4096]{1,0:T(8,128)(2,1)S(1)} %collective-permute-done.refs_0_.refs_4_.refs_12_), channel_id=1, source_target_pairs={{0,8},{1,17},{2,10},{3,19},{4,12},{5,21},{6,14},{7,23},{8,0},{9,25... | collective-permute-start | bytes 786440 | tf_op jit(solution)/shard_map/ppermute | solution.py:255
  25.9 9.7 %collective-permute-start.14 = (bf16[32,4096]{1,0:T(8,128)(2,1)S(1)}, bf16[32,4096]{1,0:T(8,128)(2,1)S(1)}, u32[]{:S(2)}, u32[]{:S(2)}) collective-permute-start(bf16[32,4096]{1,0:T(8,128)(2,1)S(1)} %collective-permute-done.refs_0_.refs_4_.refs_12_), channel_id=1, source_target_pairs={{0,1},{1,0},{2,3},{3,2},{4,5},{5,4},{6,7},{7,6},{8,9},{9,8},{10,11... | collective-permute-start | bytes 786440 | tf_op jit(solution)/shard_map/ppermute | solution.py:255
  25.9 10.2 %collective-permute-start.15 = (bf16[32,4096]{1,0:T(8,128)(2,1)S(1)}, bf16[32,4096]{1,0:T(8,128)(2,1)S(1)}, u32[]{:S(2)}, u32[]{:S(2)}) collective-permute-start(bf16[32,4096]{1,0:T(8,128)(2,1)S(1)} %collective-permute-done.refs_0_.refs_4_.refs_12_), channel_id=1, source_target_pairs={{0,16},{1,9},{2,18},{3,11},{4,20},{5,13},{6,22},{7,15},{8,24},{9,1... | collective-permute-start | bytes 786440 | tf_op jit(solution)/shard_map/ppermute | solution.py:255
  30.9 7.0 %collective-permute-start.1 = (bf16[32,4096]{1,0:T(8,128)(2,1)S(1)}, bf16[32,4096]{1,0:T(8,128)(2,1)S(1)}, u32[]{:S(2)}, u32[]{:S(2)}) collective-permute-start(bf16[32,4096]{1,0:T(8,128)(2,1)S(1)} %collective-permute-done.refs_0_.refs_4_.refs_12_), channel_id=1, source_target_pairs={{0,2},{1,3},{2,0},{3,1},{4,6},{5,7},{6,4},{7,5},{8,10},{9,11},{10,... | collective-permute-start | bytes 786440 | tf_op jit(solution)/shard_map/ppermute | solution.py:255
  32.0 6.2 %collective-permute-start.30 = (bf16[32,4096]{1,0:T(8,128)(2,1)S(1)}, bf16[32,4096]{1,0:T(8,128)(2,1)S(1)}, u32[]{:S(2)}, u32[]{:S(2)}) collective-permute-start(bf16[32,4096]{1,0:T(8,128)(2,1)S(1)} %collective-permute-done.22.refs_3_), channel_id=1, source_target_pairs={{0,1},{1,0},{2,3},{3,2},{4,5},{5,4},{6,7},{7,6},{8,9},{9,8},{10,11... | collective-permute-start | bytes 786440 | tf_op jit(solution)/shard_map/ppermute | solution.py:255
  35.6 3.5 %collective-permute-start.24 = (bf16[32,4096]{1,0:T(8,128)(2,1)S(1)}, bf16[32,4096]{1,0:T(8,128)(2,1)S(1)}, u32[]{:S(2)}, u32[]{:S(2)}) collective-permute-start(bf16[32,4096]{1,0:T(8,128)(2,1)S(1)} %collective-permute-done.19.refs_1_), channel_id=1, source_target_pairs={{0,1},{1,0},{2,3},{3,2},{4,5},{5,4},{6,7},{7,6},{8,9},{9,8},{10,11... | collective-permute-start | bytes 786440 | tf_op jit(solution)/shard_map/ppermute | solution.py:255
  35.6 3.6 %collective-permute-start.25 = (bf16[32,4096]{1,0:T(8,128)(2,1)S(1)}, bf16[32,4096]{1,0:T(8,128)(2,1)S(1)}, u32[]{:S(2)}, u32[]{:S(2)}) collective-permute-start(bf16[32,4096]{1,0:T(8,128)(2,1)S(1)} %collective-permute-done.20.refs_2_), channel_id=1, source_target_pairs={{0,1},{1,0},{2,3},{3,2},{4,5},{5,4},{6,7},{7,6},{8,9},{9,8},{10,11... | collective-permute-start | bytes 786440 | tf_op jit(solution)/shard_map/ppermute | solution.py:255
  36.1 8.3 %collective-permute-start.23 = (bf16[32,4096]{1,0:T(8,128)(2,1)S(1)}, bf16[32,4096]{1,0:T(8,128)(2,1)S(1)}, u32[]{:S(2)}, u32[]{:S(2)}) collective-permute-start(bf16[32,4096]{1,0:T(8,128)(2,1)S(1)} %collective-permute-done.22.refs_3_), channel_id=1, source_target_pairs={{0,2},{1,3},{2,0},{3,1},{4,6},{5,7},{6,4},{7,5},{8,10},{9,11},{10,... | collective-permute-start | bytes 786440 | tf_op jit(solution)/shard_map/ppermute | solution.py:255
  37.9 8.5 %collective-permute-start.5 = (bf16[32,4096]{1,0:T(8,128)(2,1)S(1)}, bf16[32,4096]{1,0:T(8,128)(2,1)S(1)}, u32[]{:S(2)}, u32[]{:S(2)}) collective-permute-start(bf16[32,4096]{1,0:T(8,128)(2,1)S(1)} %collective-permute-done.4.refs_1_), channel_id=1, source_target_pairs={{0,16},{1,9},{2,18},{3,11},{4,20},{5,13},{6,22},{7,15},{8,24},{9,1... | collective-permute-start | bytes 786440 | tf_op jit(solution)/shard_map/ppermute | solution.py:255
  38.2 8.2 %collective-permute-start.16 = (bf16[32,4096]{1,0:T(8,128)(2,1)S(1)}, bf16[32,4096]{1,0:T(8,128)(2,1)S(1)}, u32[]{:S(2)}, u32[]{:S(2)}) collective-permute-start(bf16[32,4096]{1,0:T(8,128)(2,1)S(1)} %collective-permute-done.4.refs_1_), channel_id=1, source_target_pairs={{0,1},{1,0},{2,3},{3,2},{4,5},{5,4},{6,7},{7,6},{8,9},{9,8},{10,11... | collective-permute-start | bytes 786440 | tf_op jit(solution)/shard_map/ppermute | solution.py:255
  39.1 7.7 %collective-permute-start.17 = (bf16[32,4096]{1,0:T(8,128)(2,1)S(1)}, bf16[32,4096]{1,0:T(8,128)(2,1)S(1)}, u32[]{:S(2)}, u32[]{:S(2)}) collective-permute-start(bf16[32,4096]{1,0:T(8,128)(2,1)S(1)} %collective-permute-done.15.refs_2_), channel_id=1, source_target_pairs={{0,1},{1,0},{2,3},{3,2},{4,5},{5,4},{6,7},{7,6},{8,9},{9,8},{10,11... | collective-permute-start | bytes 786440 | tf_op jit(solution)/shard_map/ppermute | solution.py:255
  39.2 7.8 %collective-permute-start.2 = (bf16[32,4096]{1,0:T(8,128)(2,1)S(1)}, bf16[32,4096]{1,0:T(8,128)(2,1)S(1)}, u32[]{:S(2)}, u32[]{:S(2)}) collective-permute-start(bf16[32,4096]{1,0:T(8,128)(2,1)S(1)} %collective-permute-done.1.refs_6_.refs_0_.refs_14_), channel_id=1, source_target_pairs={{0,8},{1,17},{2,10},{3,19},{4,12},{5,21},{6,14},{7,23},{8,0},{9,25... | collective-permute-start | bytes 786440 | tf_op jit(solution)/shard_map/ppermute | solution.py:255
  44.4 6.4 %collective-permute-start.3 = (bf16[32,4096]{1,0:T(8,128)(2,1)S(1)}, bf16[32,4096]{1,0:T(8,128)(2,1)S(1)}, u32[]{:S(2)}, u32[]{:S(2)}) collective-permute-start(bf16[32,4096]{1,0:T(8,128)(2,1)S(1)} %collective-permute-done.1.refs_6_.refs_0_.refs_14_), channel_id=1, source_target_pairs={{0,16},{1,9},{2,18},{3,11},{4,20},{5,13},{6,22},{7,15},{8,24},{9,1... | collective-permute-start | bytes 786440 | tf_op jit(solution)/shard_map/ppermute | solution.py:255
  46.4 4.5 %collective-permute-start.26 = (bf16[32,4096]{1,0:T(8,128)(2,1)S(1)}, bf16[32,4096]{1,0:T(8,128)(2,1)S(1)}, u32[]{:S(2)}, u32[]{:S(2)}) collective-permute-start(bf16[32,4096]{1,0:T(8,128)(2,1)S(1)} %collective-permute-done.23.refs_3_), channel_id=1, source_target_pairs={{0,1},{1,0},{2,3},{3,2},{4,5},{5,4},{6,7},{7,6},{8,9},{9,8},{10,11... | collective-permute-start | bytes 786440 | tf_op jit(solution)/shard_map/ppermute | solution.py:255
  46.4 8.7 %collective-permute-start.6 = (bf16[32,4096]{1,0:T(8,128)(2,1)S(1)}, bf16[32,4096]{1,0:T(8,128)(2,1)S(1)}, u32[]{:S(2)}, u32[]{:S(2)}) collective-permute-start(bf16[32,4096]{1,0:T(8,128)(2,1)S(1)} %collective-permute-done.5.refs_3_), channel_id=1, source_target_pairs={{0,2},{1,3},{2,0},{3,1},{4,6},{5,7},{6,4},{7,5},{8,10},{9,11},{10,... | collective-permute-start | bytes 786440 | tf_op jit(solution)/shard_map/ppermute | solution.py:255
  46.8 15.6 %collective-permute-start.18 = (bf16[32,4096]{1,0:T(8,128)(2,1)S(1)}, bf16[32,4096]{1,0:T(8,128)(2,1)S(1)}, u32[]{:S(2)}, u32[]{:S(2)}) collective-permute-start(bf16[32,4096]{1,0:T(8,128)(2,1)S(1)} %collective-permute-done.5.refs_3_), channel_id=1, source_target_pairs={{0,1},{1,0},{2,3},{3,2},{4,5},{5,4},{6,7},{7,6},{8,9},{9,8},{10,11... | collective-permute-start | bytes 786440 | tf_op jit(solution)/shard_map/ppermute | solution.py:255
  47.0 18.0 %collective-permute-start.7 = (bf16[32,4096]{1,0:T(8,128)(2,1)S(1)}, bf16[32,4096]{1,0:T(8,128)(2,1)S(1)}, u32[]{:S(2)}, u32[]{:S(2)}) collective-permute-start(bf16[32,4096]{1,0:T(8,128)(2,1)S(1)} %collective-permute-done.1.refs_6_.refs_0_.refs_14_), channel_id=1, source_target_pairs={{0,1},{1,0},{2,3},{3,2},{4,5},{5,4},{6,7},{7,6},{8,9},{9,8},{10,11... | collective-permute-start | bytes 786440 | tf_op jit(solution)/shard_map/ppermute | solution.py:255
  50.8 24.0 %collective-permute-start.8 = (bf16[32,4096]{1,0:T(8,128)(2,1)S(1)}, bf16[32,4096]{1,0:T(8,128)(2,1)S(1)}, u32[]{:S(2)}, u32[]{:S(2)}) collective-permute-start(bf16[32,4096]{1,0:T(8,128)(2,1)S(1)} %collective-permute-done.2.refs_1_), channel_id=1, source_target_pairs={{0,1},{1,0},{2,3},{3,2},{4,5},{5,4},{6,7},{7,6},{8,9},{9,8},{10,11... | collective-permute-start | bytes 786440 | tf_op jit(solution)/shard_map/ppermute | solution.py:255
  50.8 24.0 %collective-permute-start.9 = (bf16[32,4096]{1,0:T(8,128)(2,1)S(1)}, bf16[32,4096]{1,0:T(8,128)(2,1)S(1)}, u32[]{:S(2)}, u32[]{:S(2)}) collective-permute-start(bf16[32,4096]{1,0:T(8,128)(2,1)S(1)} %collective-permute-done.3.refs_2_), channel_id=1, source_target_pairs={{0,1},{1,0},{2,3},{3,2},{4,5},{5,4},{6,7},{7,6},{8,9},{9,8},{10,11... | collective-permute-start | bytes 786440 | tf_op jit(solution)/shard_map/ppermute | solution.py:255
  55.1 19.8 %collective-permute-start.10 = (bf16[32,4096]{1,0:T(8,128)(2,1)S(1)}, bf16[32,4096]{1,0:T(8,128)(2,1)S(1)}, u32[]{:S(2)}, u32[]{:S(2)}) collective-permute-start(bf16[32,4096]{1,0:T(8,128)(2,1)S(1)} %collective-permute-done.6.refs_3_), channel_id=1, source_target_pairs={{0,1},{1,0},{2,3},{3,2},{4,5},{5,4},{6,7},{7,6},{8,9},{9,8},{10,11... | collective-permute-start | bytes 786440 | tf_op jit(solution)/shard_map/ppermute | solution.py:255
  (4 other events, 58.0 us)

commit v3 on v2

--- a/solution.py
+++ b/solution.py
@@ -41,7 +41,15 @@
     return sum(((value >> b) & 1) << (n_bits - 1 - b) for b in range(n_bits))
 
 
-def whiten_kernel(raw_ref, gain_ref, out_ref):
+def whiten_kernel(raw_hbm, gain_hbm, out_ref, raw_ref, gain_ref, sems):
+    copies = [
+        pltpu.make_async_copy(raw_hbm, raw_ref, sems.at[0]),
+        pltpu.make_async_copy(gain_hbm, gain_ref, sems.at[1]),
+    ]
+    for copy in copies:
+        copy.start()
+    for copy in copies:
+        copy.wait()
     freqs = gain_ref.shape[1]
     raw = raw_ref[...].astype(jnp.float32)
     power = jnp.mean(raw * raw, axis=1, keepdims=True)
@@ -165,15 +173,20 @@
 
 def corr_step(place, dz, lines, picked_ref, part_ref):
     block = place.block
+    width = picked_ref.shape[1]
 
     @pl.when(place.inside(dz))
     def _():
-        for at, tile in enumerate(lines):
+        part = jnp.zeros((len(lines) * block, picked_ref.shape[0]), jnp.float32)
+        for start in range(0, width, CHUNK):
+            cols = slice(start, start + CHUNK)
+            part += lax.dot_general(
+                stack(lines, cols), picked_ref[:, cols], NT, preferred_element_type=jnp.float32
+            )
+        for at in range(len(lines)):
             _, from_col = place.of(at // PAIR, 0, at % PAIR)
             spot = pl.multiple_of(from_col * block, block)
-            part_ref[pl.ds(place.half(dz), 1), pl.ds(spot, block), :] = lax.dot_general(
-                tile[...], picked_ref[...], NT, preferred_element_type=jnp.float32
-            )[None]
+            part_ref[pl.ds(place.half(dz), 1), pl.ds(spot, block), :] = part[at * block : (at + 1) * block][None]
 
 
 def bundle_kernel(sizes, dz, fresh, bins_ref, lag_ref, table_ref, turned_ref, *refs):
@@ -274,7 +287,16 @@
         return jax.ShapeDtypeStruct((rows, *(last or (width,))), dtype)
 
     whitened = call(
-        whiten_kernel, shape(block, jnp.bfloat16), (spectra, band_weights[None, :]), [vmem] * 2, 4
+        whiten_kernel,
+        shape(block, jnp.bfloat16),
+        (spectra, band_weights[None, :]),
+        [pl.BlockSpec(memory_space=pltpu.HBM)] * 2,
+        4,
+        scratch_shapes=[
+            pltpu.VMEM((block, width), spectra.dtype),
+            pltpu.VMEM((1, freqs), jnp.float32),
+            pltpu.SemaphoreType.DMA((2,)),
+        ],
     )
     turned = call(
         rotate_kernel, shape(len(SHIFTS) * block, jnp.bfloat16), (table, whitened), [vmem] * 2, 8

time: 78.7 us -> 70.6 us (0.90)
  Pallas kernels: 22.7 us -> 14.6 us
    pallas_call x7, Pallas kernels: 22.7 us -> 14.6 us  [call(): pl.pallas_call(kernel, out_shape=outs, in_specs=specs, out_specs=jax.tree...]
  transfers between devices with their start and end apart: 31 -> 31, of which waited for: 9 -> 9; matrix products, arithmetic and copies ran while one was open for 0% -> 0% of each run, Pallas kernels for 24% -> 15%
where the time goes in v3:
time: 70.6 us; the launch traced here: 70.4 us
  waiting for transfers between devices  29.8 us (42%)
  starting transfers between devices  22.8 us (32%)
  Pallas kernels  14.6 us (21%)
  local copies, waits for them, and re-layouts  2.42 us (3%)
  between operations  0.79 us (1%)
    ppermute x31, waiting for transfers between devices, send(): return lax.ppermute(value, ('rows', 'cols'), pairs)  29.8 us
    ppermute x31, starting transfers between devices, send(): return lax.ppermute(value, ('rows', 'cols'), pairs)  22.8 us
    pallas_call x7, Pallas kernels, call(): pl.pallas_call(kernel, out_shape=outs, in_specs=specs, out_specs=jax.tree...  14.6 us
    unnamed x10, local copies, waits for them, and re-layouts  2.42 us
  transfers between devices with their start and end apart: 31, of which 9 were waited for; matrix products, arithmetic and copies ran while one was open for 0% of the time, Pallas kernels for 15%

profile of v3, /device:TPU:0, one launch (start us, length us, event | category | flops | bytes accessed | tf_op | source)
XLA Modules:
  0.0 70.4 jit_solution(7117173424166691809)
XLA Ops:
  0.7 1.0 %copy-done.1 = bf16[32,4096]{1,0:T(8,128)(2,1)S(1)} copy-done((bf16[32,4096]{1,0:T(8,128)(2,1)S(1)}, bf16[32,4096]{1,0:T(8,128)(2,1)}, u32[]{:S(2)}) %copy-start.1) | copy-done | bytes 262168
  1.6 0.7 copy-done.2
  2.5 3.0 %collective-permute-start.21 = (bf16[32,4096]{1,0:T(8,128)(2,1)S(1)}, bf16[32,4096]{1,0:T(8,128)(2,1)S(1)}, u32[]{:S(2)}, u32[]{:S(2)}) collective-permute-start(bf16[32,4096]{1,0:T(8,128)(2,1)S(1)} %shard_map.68.own_ref.refs_0_.refs_8_), channel_id=1, source_target_pairs={{0,8},{1,17},{2,10},{3,19},{4,12},{5,21},{6,14},{7,23},{8,0},{9,25... | collective-permute-start | bytes 786440 | tf_op jit(solution)/shard_map/ppermute | solution.py:268
  5.6 1.5 %collective-permute-start.27 = (bf16[32,4096]{1,0:T(8,128)(2,1)S(1)}, bf16[32,4096]{1,0:T(8,128)(2,1)S(1)}, u32[]{:S(2)}, u32[]{:S(2)}) collective-permute-start(bf16[32,4096]{1,0:T(8,128)(2,1)S(1)} %shard_map.68.own_ref.refs_0_.refs_8_), channel_id=1, source_target_pairs={{0,16},{1,9},{2,18},{3,11},{4,20},{5,13},{6,22},{7,15},{8,24},{9,1... | collective-permute-start | bytes 786440 | tf_op jit(solution)/shard_map/ppermute | solution.py:268
  7.1 1.6 %collective-permute-start.12 = (bf16[32,4096]{1,0:T(8,128)(2,1)S(1)}, bf16[32,4096]{1,0:T(8,128)(2,1)S(1)}, u32[]{:S(2)}, u32[]{:S(2)}) collective-permute-start(bf16[32,4096]{1,0:T(8,128)(2,1)S(1)} %shard_map.68.own_ref.refs_0_.refs_8_), channel_id=1, source_target_pairs={{0,2},{1,3},{2,0},{3,1},{4,6},{5,7},{6,4},{7,5},{8,10},{9,11},{10,... | collective-permute-start | bytes 786440 | tf_op jit(solution)/shard_map/ppermute | solution.py:268
  8.7 2.6 %collective-permute-start = (bf16[32,4096]{1,0:T(8,128)(2,1)S(1)}, bf16[32,4096]{1,0:T(8,128)(2,1)S(1)}, u32[]{:S(2)}, u32[]{:S(2)}) collective-permute-start(bf16[32,4096]{1,0:T(8,128)(2,1)S(1)} %shard_map.68.own_ref.refs_0_.refs_8_), channel_id=1, source_target_pairs={{0,4},{1,5},{2,6},{3,7},{4,0},{5,1},{6,2},{7,3},{8,12},{9,13},{10,... | collective-permute-start | bytes 786440 | tf_op jit(solution)/shard_map/ppermute | solution.py:268
  11.3 0.9 %collective-permute-done.21.refs_1_ = bf16[32,4096]{1,0:T(8,128)(2,1)S(1)} collective-permute-done((bf16[32,4096]{1,0:T(8,128)(2,1)S(1)}, bf16[32,4096]{1,0:T(8,128)(2,1)S(1)}, u32[]{:S(2)}, u32[]{:S(2)}) %collective-permute-start.21) | collective-permute-done | bytes 262176 | tf_op jit(solution)/shard_map/ppermute | solution.py:268
  12.2 1.6 %collective-permute-start.22 = (bf16[32,4096]{1,0:T(8,128)(2,1)S(1)}, bf16[32,4096]{1,0:T(8,128)(2,1)S(1)}, u32[]{:S(2)}, u32[]{:S(2)}) collective-permute-start(bf16[32,4096]{1,0:T(8,128)(2,1)S(1)} %collective-permute-done.21.refs_1_), channel_id=1, source_target_pairs={{0,16},{1,9},{2,18},{3,11},{4,20},{5,13},{6,22},{7,15},{8,24},{9,1... | collective-permute-start | bytes 786440 | tf_op jit(solution)/shard_map/ppermute | solution.py:268
  14.3 5.8 %collective-permute-done.12.refs_0_.refs_2_.refs_10_ = bf16[32,4096]{1,0:T(8,128)(2,1)S(1)} collective-permute-done((bf16[32,4096]{1,0:T(8,128)(2,1)S(1)}, bf16[32,4096]{1,0:T(8,128)(2,1)S(1)}, u32[]{:S(2)}, u32[]{:S(2)}) %collective-permute-start.12) | collective-permute-done | bytes 262176 | tf_op jit(solution)/shard_map/ppermute | solution.py:268
  20.1 2.4 %collective-permute-done.refs_0_.refs_4_.refs_12_ = bf16[32,4096]{1,0:T(8,128)(2,1)S(1)} collective-permute-done((bf16[32,4096]{1,0:T(8,128)(2,1)S(1)}, bf16[32,4096]{1,0:T(8,128)(2,1)S(1)}, u32[]{:S(2)}, u32[]{:S(2)}) %collective-permute-start) | collective-permute-done | bytes 262176 | tf_op jit(solution)/shard_map/ppermute | solution.py:268
  22.4 1.5 %collective-permute-start.19 = (bf16[32,4096]{1,0:T(8,128)(2,1)S(1)}, bf16[32,4096]{1,0:T(8,128)(2,1)S(1)}, u32[]{:S(2)}, u32[]{:S(2)}) collective-permute-start(bf16[32,4096]{1,0:T(8,128)(2,1)S(1)} %collective-permute-done.12.refs_0_.refs_2_.refs_10_), channel_id=1, source_target_pairs={{0,8},{1,17},{2,10},{3,19},{4,12},{5,21},{6,14},{7,23},{8,0},{9,25... | collective-permute-start | bytes 786440 | tf_op jit(solution)/shard_map/ppermute | solution.py:268
  23.9 1.5 %collective-permute-start.20 = (bf16[32,4096]{1,0:T(8,128)(2,1)S(1)}, bf16[32,4096]{1,0:T(8,128)(2,1)S(1)}, u32[]{:S(2)}, u32[]{:S(2)}) collective-permute-start(bf16[32,4096]{1,0:T(8,128)(2,1)S(1)} %collective-permute-done.12.refs_0_.refs_2_.refs_10_), channel_id=1, source_target_pairs={{0,16},{1,9},{2,18},{3,11},{4,20},{5,13},{6,22},{7,15},{8,24},{9,1... | collective-permute-start | bytes 786440 | tf_op jit(solution)/shard_map/ppermute | solution.py:268
  25.4 0.5 collective-permute-start.4
  26.0 0.6 collective-permute-start.15
  26.6 4.4 %collective-permute-done.19.refs_1_ = bf16[32,4096]{1,0:T(8,128)(2,1)S(1)} collective-permute-done((bf16[32,4096]{1,0:T(8,128)(2,1)S(1)}, bf16[32,4096]{1,0:T(8,128)(2,1)S(1)}, u32[]{:S(2)}, u32[]{:S(2)}) %collective-permute-start.19) | collective-permute-done | bytes 262176 | tf_op jit(solution)/shard_map/ppermute | solution.py:268
  31.0 1.1 %collective-permute-start.1 = (bf16[32,4096]{1,0:T(8,128)(2,1)S(1)}, bf16[32,4096]{1,0:T(8,128)(2,1)S(1)}, u32[]{:S(2)}, u32[]{:S(2)}) collective-permute-start(bf16[32,4096]{1,0:T(8,128)(2,1)S(1)} %collective-permute-done.refs_0_.refs_4_.refs_12_), channel_id=1, source_target_pairs={{0,2},{1,3},{2,0},{3,1},{4,6},{5,7},{6,4},{7,5},{8,10},{9,11},{10,... | collective-permute-start | bytes 786440 | tf_op jit(solution)/shard_map/ppermute | solution.py:268
  32.1 3.6 %collective-permute-done.4.refs_1_ = bf16[32,4096]{1,0:T(8,128)(2,1)S(1)} collective-permute-done((bf16[32,4096]{1,0:T(8,128)(2,1)S(1)}, bf16[32,4096]{1,0:T(8,128)(2,1)S(1)}, u32[]{:S(2)}, u32[]{:S(2)}) %collective-permute-start.4) | collective-permute-done | bytes 262176 | tf_op jit(solution)/shard_map/ppermute | solution.py:268
  35.6 0.5 collective-permute-start.25
  36.1 1.8 %collective-permute-start.23 = (bf16[32,4096]{1,0:T(8,128)(2,1)S(1)}, bf16[32,4096]{1,0:T(8,128)(2,1)S(1)}, u32[]{:S(2)}, u32[]{:S(2)}) collective-permute-start(bf16[32,4096]{1,0:T(8,128)(2,1)S(1)} %collective-permute-done.22.refs_3_), channel_id=1, source_target_pairs={{0,2},{1,3},{2,0},{3,1},{4,6},{5,7},{6,4},{7,5},{8,10},{9,11},{10,... | collective-permute-start | bytes 786440 | tf_op jit(solution)/shard_map/ppermute | solution.py:268
  38.2 0.9 %collective-permute-start.16 = (bf16[32,4096]{1,0:T(8,128)(2,1)S(1)}, bf16[32,4096]{1,0:T(8,128)(2,1)S(1)}, u32[]{:S(2)}, u32[]{:S(2)}) collective-permute-start(bf16[32,4096]{1,0:T(8,128)(2,1)S(1)} %collective-permute-done.4.refs_1_), channel_id=1, source_target_pairs={{0,1},{1,0},{2,3},{3,2},{4,5},{5,4},{6,7},{7,6},{8,9},{9,8},{10,11... | collective-permute-start | bytes 786440 | tf_op jit(solution)/shard_map/ppermute | solution.py:268
  39.2 1.3 %collective-permute-start.2 = (bf16[32,4096]{1,0:T(8,128)(2,1)S(1)}, bf16[32,4096]{1,0:T(8,128)(2,1)S(1)}, u32[]{:S(2)}, u32[]{:S(2)}) collective-permute-start(bf16[32,4096]{1,0:T(8,128)(2,1)S(1)} %collective-permute-done.1.refs_6_.refs_0_.refs_14_), channel_id=1, source_target_pairs={{0,8},{1,17},{2,10},{3,19},{4,12},{5,21},{6,14},{7,23},{8,0},{9,25... | collective-permute-start | bytes 786440 | tf_op jit(solution)/shard_map/ppermute | solution.py:268
  40.5 4.0 %collective-permute-done.23.refs_3_ = bf16[32,4096]{1,0:T(8,128)(2,1)S(1)} collective-permute-done((bf16[32,4096]{1,0:T(8,128)(2,1)S(1)}, bf16[32,4096]{1,0:T(8,128)(2,1)S(1)}, u32[]{:S(2)}, u32[]{:S(2)}) %collective-permute-start.23) | collective-permute-done | bytes 262176 | tf_op jit(solution)/shard_map/ppermute | solution.py:268
  45.0 1.4 %collective-permute-done.5.refs_3_ = bf16[32,4096]{1,0:T(8,128)(2,1)S(1)} collective-permute-done((bf16[32,4096]{1,0:T(8,128)(2,1)S(1)}, bf16[32,4096]{1,0:T(8,128)(2,1)S(1)}, u32[]{:S(2)}, u32[]{:S(2)}) %collective-permute-start.5) | collective-permute-done | bytes 262176 | tf_op jit(solution)/shard_map/ppermute | solution.py:268
  47.4 3.5 %collective-permute-done.3.refs_2_ = bf16[32,4096]{1,0:T(8,128)(2,1)S(1)} collective-permute-done((bf16[32,4096]{1,0:T(8,128)(2,1)S(1)}, bf16[32,4096]{1,0:T(8,128)(2,1)S(1)}, u32[]{:S(2)}, u32[]{:S(2)}) %collective-permute-start.3) | collective-permute-done | bytes 262176 | tf_op jit(solution)/shard_map/ppermute | solution.py:268
  50.9 0.5 collective-permute-start.9
  51.4 3.8 %collective-permute-done.6.refs_3_ = bf16[32,4096]{1,0:T(8,128)(2,1)S(1)} collective-permute-done((bf16[32,4096]{1,0:T(8,128)(2,1)S(1)}, bf16[32,4096]{1,0:T(8,128)(2,1)S(1)}, u32[]{:S(2)}, u32[]{:S(2)}) %collective-permute-start.6) | collective-permute-done | bytes 262176 | tf_op jit(solution)/shard_map/ppermute | solution.py:268
  55.1 0.8 %copy-done = f32[4,2048]{1,0:T(4,128)S(1)} copy-done((f32[4,2048]{1,0:T(4,128)S(1)}, f32[4,2048]{1,0:T(4,128)}, u32[]{:S(2)}) %copy-start) | copy-done | bytes 32792
  56.2 3.0 %shard_map.70 = (f32[160,4096]{1,0:T(8,128)S(1)}, bf16[256,4096]{1,0:T(8,128)(2,1)S(1)}) custom-call(s32[8]{0:T(128)S(1)} %copy-done.3, f32[4]{0:T(128)S(1)} %copy-done.4, f32[4,2048]{1,0:T(4,128)S(1)} %copy-done, bf16[160,4096]{1,0:T(8,128)(2,1)S(1)} %shard_map.69.turned_ref, bf16[32,4096]{1,0:T(8,128)(2,1)S(1)} %shard_map.68.own_ref.refs_0_.refs_8_, ...), custom_call_target="tpu_custom_call" | custom-call | tf_op jit(solution)/shard_map/pallas_call | solution.py:277
  59.3 3.2 %shard_map.71 = (f32[160,4096]{1,0:T(8,128)S(1)}, bf16[256,4096]{1,0:T(8,128)(2,1)S(1)}) custom-call(s32[8]{0:T(128)S(1)} %copy-done.3, f32[4]{0:T(128)S(1)} %copy-done.4, f32[4,2048]{1,0:T(4,128)S(1)} %copy-done, bf16[160,4096]{1,0:T(8,128)(2,1)S(1)} %shard_map.69.turned_ref, ...), custom_call_target="tpu_custom_call", output_to_operand_aliasing={{0}: (12, {})} | custom-call | tf_op jit(solution)/shard_map/pallas_call | solution.py:277
  62.5 2.5 %shard_map.72 = (f32[160,4096]{1,0:T(8,128)S(1)}, bf16[256,4096]{1,0:T(8,128)(2,1)S(1)}) custom-call(s32[8]{0:T(128)S(1)} %copy-done.3, f32[4]{0:T(128)S(1)} %copy-done.4, f32[4,2048]{1,0:T(4,128)S(1)} %copy-done, bf16[160,4096]{1,0:T(8,128)(2,1)S(1)} %shard_map.69.turned_ref, ...), custom_call_target="tpu_custom_call", output_to_operand_aliasing={{0}: (12, {})} | custom-call | tf_op jit(solution)/shard_map/pallas_call | solution.py:277
  65.0 1.7 %shard_map.73.refs_17_ = f32[2,256,256]{2,1,0:T(8,128)S(1)} custom-call(bf16[32,4096]{1,0:T(8,128)(2,1)S(1)} %shard_map.68.own_ref.refs_0_.refs_8_, bf16[32,4096]{1,0:T(8,128)(2,1)S(1)} %collective-permute-done.11.refs_4_.refs_1_.refs_9_, bf16[32,4096]{1,0:T(8,128)(2,1)S(1)} %collective-permute-done.12.refs_0_.refs_2_.refs_10_, ...), custom_call_target="tpu_custom_call" | custom-call | tf_op jit(solution)/shard_map/pallas_call | solution.py:277
  66.7 3.6 %shard_map.74 = (f32[4,256,128]{2,1,0:T(8,128)}, f32[32,4096]{1,0:T(8,128)}) custom-call(s32[8]{0:T(128)S(1)} %copy-done.3, f32[4]{0:T(128)S(1)} %copy-done.4, f32[4,2048]{1,0:T(4,128)S(1)} %copy-done, bf16[160,4096]{1,0:T(8,128)(2,1)S(1)} %shard_map.69.turned_ref, bf16[32,4096]{1,0:T(8,128)(2,1)S(1)} %collective-permute-done.1.refs_6_.refs_0_.refs_14_, ...), custom_call_target="tpu_custom_call" | custom-call | tf_op jit(solution)/shard_map/pallas_call | solution.py:277
  (47 shorter events, 2.9 us)
Async XLA Ops:
  0.6 55.6 %copy-start.4 = (f32[4]{0:T(128)S(1)}, f32[4]{0:T(128)}, u32[]{:S(2)}) copy-start(f32[4]{0:T(128)} %lag_ref.7) | copy-start | bytes 52
  2.5 9.6 %collective-permute-start.21 = (bf16[32,4096]{1,0:T(8,128)(2,1)S(1)}, bf16[32,4096]{1,0:T(8,128)(2,1)S(1)}, u32[]{:S(2)}, u32[]{:S(2)}) collective-permute-start(bf16[32,4096]{1,0:T(8,128)(2,1)S(1)} %shard_map.68.own_ref.refs_0_.refs_8_), channel_id=1, source_target_pairs={{0,8},{1,17},{2,10},{3,19},{4,12},{5,21},{6,14},{7,23},{8,0},{9,25... | collective-permute-start | bytes 786440 | tf_op jit(solution)/shard_map/ppermute | solution.py:268
  5.6 8.2 %collective-permute-start.11 = (bf16[32,4096]{1,0:T(8,128)(2,1)S(1)}, bf16[32,4096]{1,0:T(8,128)(2,1)S(1)}, u32[]{:S(2)}, u32[]{:S(2)}) collective-permute-start(bf16[32,4096]{1,0:T(8,128)(2,1)S(1)} %shard_map.68.own_ref.refs_0_.refs_8_), channel_id=1, source_target_pairs={{0,1},{1,0},{2,3},{3,2},{4,5},{5,4},{6,7},{7,6},{8,9},{9,8},{10,11... | collective-permute-start | bytes 786440 | tf_op jit(solution)/shard_map/ppermute | solution.py:268
  5.6 8.2 %collective-permute-start.27 = (bf16[32,4096]{1,0:T(8,128)(2,1)S(1)}, bf16[32,4096]{1,0:T(8,128)(2,1)S(1)}, u32[]{:S(2)}, u32[]{:S(2)}) collective-permute-start(bf16[32,4096]{1,0:T(8,128)(2,1)S(1)} %shard_map.68.own_ref.refs_0_.refs_8_), channel_id=1, source_target_pairs={{0,16},{1,9},{2,18},{3,11},{4,20},{5,13},{6,22},{7,15},{8,24},{9,1... | collective-permute-start | bytes 786440 | tf_op jit(solution)/shard_map/ppermute | solution.py:268
  7.1 13.0 %collective-permute-start.12 = (bf16[32,4096]{1,0:T(8,128)(2,1)S(1)}, bf16[32,4096]{1,0:T(8,128)(2,1)S(1)}, u32[]{:S(2)}, u32[]{:S(2)}) collective-permute-start(bf16[32,4096]{1,0:T(8,128)(2,1)S(1)} %shard_map.68.own_ref.refs_0_.refs_8_), channel_id=1, source_target_pairs={{0,2},{1,3},{2,0},{3,1},{4,6},{5,7},{6,4},{7,5},{8,10},{9,11},{10,... | collective-permute-start | bytes 786440 | tf_op jit(solution)/shard_map/ppermute | solution.py:268
  8.7 13.8 %collective-permute-start = (bf16[32,4096]{1,0:T(8,128)(2,1)S(1)}, bf16[32,4096]{1,0:T(8,128)(2,1)S(1)}, u32[]{:S(2)}, u32[]{:S(2)}) collective-permute-start(bf16[32,4096]{1,0:T(8,128)(2,1)S(1)} %shard_map.68.own_ref.refs_0_.refs_8_), channel_id=1, source_target_pairs={{0,4},{1,5},{2,6},{3,7},{4,0},{5,1},{6,2},{7,3},{8,12},{9,13},{10,... | collective-permute-start | bytes 786440 | tf_op jit(solution)/shard_map/ppermute | solution.py:268
  12.2 11.7 %collective-permute-start.22 = (bf16[32,4096]{1,0:T(8,128)(2,1)S(1)}, bf16[32,4096]{1,0:T(8,128)(2,1)S(1)}, u32[]{:S(2)}, u32[]{:S(2)}) collective-permute-start(bf16[32,4096]{1,0:T(8,128)(2,1)S(1)} %collective-permute-done.21.refs_1_), channel_id=1, source_target_pairs={{0,16},{1,9},{2,18},{3,11},{4,20},{5,13},{6,22},{7,15},{8,24},{9,1... | collective-permute-start | bytes 786440 | tf_op jit(solution)/shard_map/ppermute | solution.py:268
  13.7 11.7 %collective-permute-start.28 = (bf16[32,4096]{1,0:T(8,128)(2,1)S(1)}, bf16[32,4096]{1,0:T(8,128)(2,1)S(1)}, u32[]{:S(2)}, u32[]{:S(2)}) collective-permute-start(bf16[32,4096]{1,0:T(8,128)(2,1)S(1)} %collective-permute-done.21.refs_1_), channel_id=1, source_target_pairs={{0,1},{1,0},{2,3},{3,2},{4,5},{5,4},{6,7},{7,6},{8,9},{9,8},{10,11... | collective-permute-start | bytes 786440 | tf_op jit(solution)/shard_map/ppermute | solution.py:268
  13.7 12.2 %collective-permute-start.29 = (bf16[32,4096]{1,0:T(8,128)(2,1)S(1)}, bf16[32,4096]{1,0:T(8,128)(2,1)S(1)}, u32[]{:S(2)}, u32[]{:S(2)}) collective-permute-start(bf16[32,4096]{1,0:T(8,128)(2,1)S(1)} %collective-permute-done.27.refs_2_), channel_id=1, source_target_pairs={{0,1},{1,0},{2,3},{3,2},{4,5},{5,4},{6,7},{7,6},{8,9},{9,8},{10,11... | collective-permute-start | bytes 786440 | tf_op jit(solution)/shard_map/ppermute | solution.py:268
  20.1 5.9 %collective-permute-start.13 = (bf16[32,4096]{1,0:T(8,128)(2,1)S(1)}, bf16[32,4096]{1,0:T(8,128)(2,1)S(1)}, u32[]{:S(2)}, u32[]{:S(2)}) collective-permute-start(bf16[32,4096]{1,0:T(8,128)(2,1)S(1)} %collective-permute-done.12.refs_0_.refs_2_.refs_10_), channel_id=1, source_target_pairs={{0,1},{1,0},{2,3},{3,2},{4,5},{5,4},{6,7},{7,6},{8,9},{9,8},{10,11... | collective-permute-start | bytes 786440 | tf_op jit(solution)/shard_map/ppermute | solution.py:268
  22.4 8.5 %collective-permute-start.19 = (bf16[32,4096]{1,0:T(8,128)(2,1)S(1)}, bf16[32,4096]{1,0:T(8,128)(2,1)S(1)}, u32[]{:S(2)}, u32[]{:S(2)}) collective-permute-start(bf16[32,4096]{1,0:T(8,128)(2,1)S(1)} %collective-permute-done.12.refs_0_.refs_2_.refs_10_), channel_id=1, source_target_pairs={{0,8},{1,17},{2,10},{3,19},{4,12},{5,21},{6,14},{7,23},{8,0},{9,25... | collective-permute-start | bytes 786440 | tf_op jit(solution)/shard_map/ppermute | solution.py:268
  23.9 8.2 %collective-permute-start.20 = (bf16[32,4096]{1,0:T(8,128)(2,1)S(1)}, bf16[32,4096]{1,0:T(8,128)(2,1)S(1)}, u32[]{:S(2)}, u32[]{:S(2)}) collective-permute-start(bf16[32,4096]{1,0:T(8,128)(2,1)S(1)} %collective-permute-done.12.refs_0_.refs_2_.refs_10_), channel_id=1, source_target_pairs={{0,16},{1,9},{2,18},{3,11},{4,20},{5,13},{6,22},{7,15},{8,24},{9,1... | collective-permute-start | bytes 786440 | tf_op jit(solution)/shard_map/ppermute | solution.py:268
  25.4 10.2 %collective-permute-start.4 = (bf16[32,4096]{1,0:T(8,128)(2,1)S(1)}, bf16[32,4096]{1,0:T(8,128)(2,1)S(1)}, u32[]{:S(2)}, u32[]{:S(2)}) collective-permute-start(bf16[32,4096]{1,0:T(8,128)(2,1)S(1)} %collective-permute-done.refs_0_.refs_4_.refs_12_), channel_id=1, source_target_pairs={{0,8},{1,17},{2,10},{3,19},{4,12},{5,21},{6,14},{7,23},{8,0},{9,25... | collective-permute-start | bytes 786440 | tf_op jit(solution)/shard_map/ppermute | solution.py:268
  26.0 9.7 %collective-permute-start.14 = (bf16[32,4096]{1,0:T(8,128)(2,1)S(1)}, bf16[32,4096]{1,0:T(8,128)(2,1)S(1)}, u32[]{:S(2)}, u32[]{:S(2)}) collective-permute-start(bf16[32,4096]{1,0:T(8,128)(2,1)S(1)} %collective-permute-done.refs_0_.refs_4_.refs_12_), channel_id=1, source_target_pairs={{0,1},{1,0},{2,3},{3,2},{4,5},{5,4},{6,7},{7,6},{8,9},{9,8},{10,11... | collective-permute-start | bytes 786440 | tf_op jit(solution)/shard_map/ppermute | solution.py:268
  26.0 10.2 %collective-permute-start.15 = (bf16[32,4096]{1,0:T(8,128)(2,1)S(1)}, bf16[32,4096]{1,0:T(8,128)(2,1)S(1)}, u32[]{:S(2)}, u32[]{:S(2)}) collective-permute-start(bf16[32,4096]{1,0:T(8,128)(2,1)S(1)} %collective-permute-done.refs_0_.refs_4_.refs_12_), channel_id=1, source_target_pairs={{0,16},{1,9},{2,18},{3,11},{4,20},{5,13},{6,22},{7,15},{8,24},{9,1... | collective-permute-start | bytes 786440 | tf_op jit(solution)/shard_map/ppermute | solution.py:268
  31.0 7.0 %collective-permute-start.1 = (bf16[32,4096]{1,0:T(8,128)(2,1)S(1)}, bf16[32,4096]{1,0:T(8,128)(2,1)S(1)}, u32[]{:S(2)}, u32[]{:S(2)}) collective-permute-start(bf16[32,4096]{1,0:T(8,128)(2,1)S(1)} %collective-permute-done.refs_0_.refs_4_.refs_12_), channel_id=1, source_target_pairs={{0,2},{1,3},{2,0},{3,1},{4,6},{5,7},{6,4},{7,5},{8,10},{9,11},{10,... | collective-permute-start | bytes 786440 | tf_op jit(solution)/shard_map/ppermute | solution.py:268
  32.1 6.2 %collective-permute-start.30 = (bf16[32,4096]{1,0:T(8,128)(2,1)S(1)}, bf16[32,4096]{1,0:T(8,128)(2,1)S(1)}, u32[]{:S(2)}, u32[]{:S(2)}) collective-permute-start(bf16[32,4096]{1,0:T(8,128)(2,1)S(1)} %collective-permute-done.22.refs_3_), channel_id=1, source_target_pairs={{0,1},{1,0},{2,3},{3,2},{4,5},{5,4},{6,7},{7,6},{8,9},{9,8},{10,11... | collective-permute-start | bytes 786440 | tf_op jit(solution)/shard_map/ppermute | solution.py:268
  35.6 3.5 %collective-permute-start.24 = (bf16[32,4096]{1,0:T(8,128)(2,1)S(1)}, bf16[32,4096]{1,0:T(8,128)(2,1)S(1)}, u32[]{:S(2)}, u32[]{:S(2)}) collective-permute-start(bf16[32,4096]{1,0:T(8,128)(2,1)S(1)} %collective-permute-done.19.refs_1_), channel_id=1, source_target_pairs={{0,1},{1,0},{2,3},{3,2},{4,5},{5,4},{6,7},{7,6},{8,9},{9,8},{10,11... | collective-permute-start | bytes 786440 | tf_op jit(solution)/shard_map/ppermute | solution.py:268
  35.6 3.6 %collective-permute-start.25 = (bf16[32,4096]{1,0:T(8,128)(2,1)S(1)}, bf16[32,4096]{1,0:T(8,128)(2,1)S(1)}, u32[]{:S(2)}, u32[]{:S(2)}) collective-permute-start(bf16[32,4096]{1,0:T(8,128)(2,1)S(1)} %collective-permute-done.20.refs_2_), channel_id=1, source_target_pairs={{0,1},{1,0},{2,3},{3,2},{4,5},{5,4},{6,7},{7,6},{8,9},{9,8},{10,11... | collective-permute-start | bytes 786440 | tf_op jit(solution)/shard_map/ppermute | solution.py:268
  36.1 8.3 %collective-permute-start.23 = (bf16[32,4096]{1,0:T(8,128)(2,1)S(1)}, bf16[32,4096]{1,0:T(8,128)(2,1)S(1)}, u32[]{:S(2)}, u32[]{:S(2)}) collective-permute-start(bf16[32,4096]{1,0:T(8,128)(2,1)S(1)} %collective-permute-done.22.refs_3_), channel_id=1, source_target_pairs={{0,2},{1,3},{2,0},{3,1},{4,6},{5,7},{6,4},{7,5},{8,10},{9,11},{10,... | collective-permute-start | bytes 786440 | tf_op jit(solution)/shard_map/ppermute | solution.py:268
  38.0 8.5 %collective-permute-start.5 = (bf16[32,4096]{1,0:T(8,128)(2,1)S(1)}, bf16[32,4096]{1,0:T(8,128)(2,1)S(1)}, u32[]{:S(2)}, u32[]{:S(2)}) collective-permute-start(bf16[32,4096]{1,0:T(8,128)(2,1)S(1)} %collective-permute-done.4.refs_1_), channel_id=1, source_target_pairs={{0,16},{1,9},{2,18},{3,11},{4,20},{5,13},{6,22},{7,15},{8,24},{9,1... | collective-permute-start | bytes 786440 | tf_op jit(solution)/shard_map/ppermute | solution.py:268
  38.2 8.2 %collective-permute-start.16 = (bf16[32,4096]{1,0:T(8,128)(2,1)S(1)}, bf16[32,4096]{1,0:T(8,128)(2,1)S(1)}, u32[]{:S(2)}, u32[]{:S(2)}) collective-permute-start(bf16[32,4096]{1,0:T(8,128)(2,1)S(1)} %collective-permute-done.4.refs_1_), channel_id=1, source_target_pairs={{0,1},{1,0},{2,3},{3,2},{4,5},{5,4},{6,7},{7,6},{8,9},{9,8},{10,11... | collective-permute-start | bytes 786440 | tf_op jit(solution)/shard_map/ppermute | solution.py:268
  39.1 7.7 %collective-permute-start.17 = (bf16[32,4096]{1,0:T(8,128)(2,1)S(1)}, bf16[32,4096]{1,0:T(8,128)(2,1)S(1)}, u32[]{:S(2)}, u32[]{:S(2)}) collective-permute-start(bf16[32,4096]{1,0:T(8,128)(2,1)S(1)} %collective-permute-done.15.refs_2_), channel_id=1, source_target_pairs={{0,1},{1,0},{2,3},{3,2},{4,5},{5,4},{6,7},{7,6},{8,9},{9,8},{10,11... | collective-permute-start | bytes 786440 | tf_op jit(solution)/shard_map/ppermute | solution.py:268
  39.2 7.8 %collective-permute-start.2 = (bf16[32,4096]{1,0:T(8,128)(2,1)S(1)}, bf16[32,4096]{1,0:T(8,128)(2,1)S(1)}, u32[]{:S(2)}, u32[]{:S(2)}) collective-permute-start(bf16[32,4096]{1,0:T(8,128)(2,1)S(1)} %collective-permute-done.1.refs_6_.refs_0_.refs_14_), channel_id=1, source_target_pairs={{0,8},{1,17},{2,10},{3,19},{4,12},{5,21},{6,14},{7,23},{8,0},{9,25... | collective-permute-start | bytes 786440 | tf_op jit(solution)/shard_map/ppermute | solution.py:268
  44.5 6.4 %collective-permute-start.3 = (bf16[32,4096]{1,0:T(8,128)(2,1)S(1)}, bf16[32,4096]{1,0:T(8,128)(2,1)S(1)}, u32[]{:S(2)}, u32[]{:S(2)}) collective-permute-start(bf16[32,4096]{1,0:T(8,128)(2,1)S(1)} %collective-permute-done.1.refs_6_.refs_0_.refs_14_), channel_id=1, source_target_pairs={{0,16},{1,9},{2,18},{3,11},{4,20},{5,13},{6,22},{7,15},{8,24},{9,1... | collective-permute-start | bytes 786440 | tf_op jit(solution)/shard_map/ppermute | solution.py:268
  46.4 4.5 %collective-permute-start.26 = (bf16[32,4096]{1,0:T(8,128)(2,1)S(1)}, bf16[32,4096]{1,0:T(8,128)(2,1)S(1)}, u32[]{:S(2)}, u32[]{:S(2)}) collective-permute-start(bf16[32,4096]{1,0:T(8,128)(2,1)S(1)} %collective-permute-done.23.refs_3_), channel_id=1, source_target_pairs={{0,1},{1,0},{2,3},{3,2},{4,5},{5,4},{6,7},{7,6},{8,9},{9,8},{10,11... | collective-permute-start | bytes 786440 | tf_op jit(solution)/shard_map/ppermute | solution.py:268
  46.4 8.7 %collective-permute-start.6 = (bf16[32,4096]{1,0:T(8,128)(2,1)S(1)}, bf16[32,4096]{1,0:T(8,128)(2,1)S(1)}, u32[]{:S(2)}, u32[]{:S(2)}) collective-permute-start(bf16[32,4096]{1,0:T(8,128)(2,1)S(1)} %collective-permute-done.5.refs_3_), channel_id=1, source_target_pairs={{0,2},{1,3},{2,0},{3,1},{4,6},{5,7},{6,4},{7,5},{8,10},{9,11},{10,... | collective-permute-start | bytes 786440 | tf_op jit(solution)/shard_map/ppermute | solution.py:268
  46.8 15.6 %collective-permute-start.18 = (bf16[32,4096]{1,0:T(8,128)(2,1)S(1)}, bf16[32,4096]{1,0:T(8,128)(2,1)S(1)}, u32[]{:S(2)}, u32[]{:S(2)}) collective-permute-start(bf16[32,4096]{1,0:T(8,128)(2,1)S(1)} %collective-permute-done.5.refs_3_), channel_id=1, source_target_pairs={{0,1},{1,0},{2,3},{3,2},{4,5},{5,4},{6,7},{7,6},{8,9},{9,8},{10,11... | collective-permute-start | bytes 786440 | tf_op jit(solution)/shard_map/ppermute | solution.py:268
  47.0 18.0 %collective-permute-start.7 = (bf16[32,4096]{1,0:T(8,128)(2,1)S(1)}, bf16[32,4096]{1,0:T(8,128)(2,1)S(1)}, u32[]{:S(2)}, u32[]{:S(2)}) collective-permute-start(bf16[32,4096]{1,0:T(8,128)(2,1)S(1)} %collective-permute-done.1.refs_6_.refs_0_.refs_14_), channel_id=1, source_target_pairs={{0,1},{1,0},{2,3},{3,2},{4,5},{5,4},{6,7},{7,6},{8,9},{9,8},{10,11... | collective-permute-start | bytes 786440 | tf_op jit(solution)/shard_map/ppermute | solution.py:268
  50.9 15.9 %collective-permute-start.8 = (bf16[32,4096]{1,0:T(8,128)(2,1)S(1)}, bf16[32,4096]{1,0:T(8,128)(2,1)S(1)}, u32[]{:S(2)}, u32[]{:S(2)}) collective-permute-start(bf16[32,4096]{1,0:T(8,128)(2,1)S(1)} %collective-permute-done.2.refs_1_), channel_id=1, source_target_pairs={{0,1},{1,0},{2,3},{3,2},{4,5},{5,4},{6,7},{7,6},{8,9},{9,8},{10,11... | collective-permute-start | bytes 786440 | tf_op jit(solution)/shard_map/ppermute | solution.py:268
  50.9 15.9 %collective-permute-start.9 = (bf16[32,4096]{1,0:T(8,128)(2,1)S(1)}, bf16[32,4096]{1,0:T(8,128)(2,1)S(1)}, u32[]{:S(2)}, u32[]{:S(2)}) collective-permute-start(bf16[32,4096]{1,0:T(8,128)(2,1)S(1)} %collective-permute-done.3.refs_2_), channel_id=1, source_target_pairs={{0,1},{1,0},{2,3},{3,2},{4,5},{5,4},{6,7},{7,6},{8,9},{9,8},{10,11... | collective-permute-start | bytes 786440 | tf_op jit(solution)/shard_map/ppermute | solution.py:268
  55.1 11.6 %collective-permute-start.10 = (bf16[32,4096]{1,0:T(8,128)(2,1)S(1)}, bf16[32,4096]{1,0:T(8,128)(2,1)S(1)}, u32[]{:S(2)}, u32[]{:S(2)}) collective-permute-start(bf16[32,4096]{1,0:T(8,128)(2,1)S(1)} %collective-permute-done.6.refs_3_), channel_id=1, source_target_pairs={{0,1},{1,0},{2,3},{3,2},{4,5},{5,4},{6,7},{7,6},{8,9},{9,8},{10,11... | collective-permute-start | bytes 786440 | tf_op jit(solution)/shard_map/ppermute | solution.py:268
  (4 other events, 58.0 us)

commit v4 on v3

--- a/solution.py
+++ b/solution.py
@@ -106,13 +106,12 @@
         return self.row ^ dr, (self.line ^ dz) * PAIR + in_core
 
 
-def gather_weights(place, dz, scores, bins_ref, lag_ref):
+def gather_weights(place, spots, scores, bins_ref, lag_ref):
     block = place.block
     span = scores.shape[1]
     lane = lax.broadcasted_iota(jnp.int32, (block, span), 1)
     mine = place.first + lax.broadcasted_iota(jnp.int32, (block, span), 0)
     other = jnp.zeros((block, span), jnp.int32)
-    spots = [place.of(dz, slot, plane) for plane in range(PAIR) for slot in range(place.n_rows)]
     for at, (from_row, from_col) in enumerate(spots):
         base = (from_row * place.n_cols + from_col) * block - at * block
         other = jnp.where(lane >= at * block, base + lane, other)
@@ -137,7 +136,7 @@
     return jnp.concatenate([tile[:, cols] for tile in tiles], axis=0)
 
 
-def bundle_step(place, dz, tiles, bins_ref, lag_ref, turned_ref, old_ref, new_ref):
+def bundle_weights(place, dz, tiles, bins_ref, lag_ref, turned_ref, skip=0):
     width = tiles[0].shape[1]
     norm = 1.0 / np.sqrt(np.float32(width))
     scores = jnp.zeros((turned_ref.shape[0], len(tiles) * place.block), jnp.float32)
@@ -146,11 +145,8 @@
         scores += lax.dot_general(
             turned_ref[:, cols], stack(tiles, cols), NT, preferred_element_type=jnp.float32
         )
-    weights = gather_weights(place, dz, scores * norm, bins_ref, lag_ref)
-    for start in range(0, width, CHUNK):
-        cols = slice(start, start + CHUNK)
-        term = jnp.dot(weights, stack(tiles, cols), preferred_element_type=jnp.float32)
-        new_ref[:, cols] = term if old_ref is None else old_ref[:, cols] + term
+    spots = [place.of(dz, slot, plane) for plane in range(PAIR) for slot in range(place.n_rows)]
+    return gather_weights(place, spots[skip : skip + len(tiles)], scores * norm, bins_ref, lag_ref)
 
 
 def pick_step(place, dz, tiles, table_ref, staged_ref, picked_ref):
@@ -189,14 +185,19 @@
             part_ref[pl.ds(place.half(dz), 1), pl.ds(spot, block), :] = part[at * block : (at + 1) * block][None]
 
 
-def bundle_kernel(sizes, dz, fresh, bins_ref, lag_ref, table_ref, turned_ref, *refs):
+def bundle_kernel(sizes, dz, bins_ref, lag_ref, table_ref, turned_ref, *refs):
     n_rows, n_cols = sizes
-    tiles = refs[: PAIR * n_rows]
-    total_ref, picked_ref, staged_ref = refs[-3:]
+    weights_ref, picked_ref, staged_ref = refs[-3:]
+    tiles = refs[:-3]
     place = Place(n_rows, n_cols, tiles[0].shape[0])
     pick_step(place, dz, tiles, table_ref, staged_ref, picked_ref)
-    old_ref = None if fresh else refs[PAIR * n_rows]
-    bundle_step(place, dz, tiles, bins_ref, lag_ref, turned_ref, old_ref, total_ref)
+    weights_ref[...] = bundle_weights(place, dz, tiles, bins_ref, lag_ref, turned_ref)
+
+
+def partial_kernel(sizes, dz, bins_ref, lag_ref, turned_ref, *refs):
+    tiles, weights_ref = refs[:-1], refs[-1]
+    place = Place(*sizes, tiles[0].shape[0])
+    weights_ref[...] = bundle_weights(place, dz, tiles, bins_ref, lag_ref, turned_ref)
 
 
 def corr_kernel(sizes, *refs):
@@ -209,23 +210,32 @@
 
 def end_kernel(sizes, dz, bins_ref, lag_ref, table_ref, turned_ref, *refs):
     n_rows, n_cols = sizes
-    count = PAIR * n_rows
-    tiles, lines = refs[:count], refs[count : count + n_cols]
-    old_ref, old_part_ref, corr_ref, grad_ref, total_ref, staged_ref, picked_ref, part_ref = refs[count + n_cols :]
+    per_line = PAIR * n_rows
+    count = (n_cols // PAIR) * per_line
+    every, old_weights = refs[:count], refs[count : count + dz + 1]
+    old_part_ref, corr_ref, grad_ref, weights_ref, staged_ref, picked_ref, part_ref = refs[count + dz + 1 :]
+    tiles = every[dz * per_line :]
+    lines = every[::n_rows]
     block, width = tiles[0].shape
     freqs = width // 2
     norm = 1.0 / np.sqrt(np.float32(width))
     place = Place(n_rows, n_cols, block)
-    bundle_step(place, dz, tiles, bins_ref, lag_ref, turned_ref, old_ref, total_ref)
+    span = per_line * block
+    fresh = bundle_weights(place, dz, tiles[-1:], bins_ref, lag_ref, turned_ref, per_line - 1)
+    for at, old_ref in enumerate(old_weights[:-1]):
+        weights_ref[:, at * span : (at + 1) * span] = old_ref[...]
+    weights_ref[:, dz * span :] = jnp.concatenate([old_weights[-1][...], fresh], axis=1)
 
     for start in range(0, freqs, CHUNK):
         cols = slice(start, start + CHUNK)
         high = slice(freqs + start, freqs + start + CHUNK)
+        reals = jnp.dot(weights_ref[...], stack(every, cols), preferred_element_type=jnp.float32)
+        imags = jnp.dot(weights_ref[...], stack(every, high), preferred_element_type=jnp.float32)
         real_sum = jnp.zeros((block, CHUNK), jnp.float32)
         imag_sum = jnp.zeros((block, CHUNK), jnp.float32)
         for at, shift in enumerate(SHIFTS):
-            real = total_ref[at * block : (at + 1) * block, cols]
-            imag = total_ref[at * block : (at + 1) * block, high]
+            real = reals[at * block : (at + 1) * block]
+            imag = imags[at * block : (at + 1) * block]
             if shift == 0:
                 real_sum, imag_sum = real_sum + real, imag_sum + imag
             else:
@@ -273,13 +283,14 @@
     def send_line(value, step):
         return send(value, lambda r, z, k: (r, z ^ step, k))
 
-    def call(kernel, outs, operands, specs, limit, **more):
+    def call(kernel, outs, operands, specs, **more):
+        held = sum(x.size * x.dtype.itemsize for x in [*operands, *jax.tree.leaves(outs)])
         return pl.pallas_call(
             kernel,
             out_shape=outs,
             in_specs=specs,
             out_specs=jax.tree.map(lambda _: vmem, outs),
-            compiler_params=pltpu.CompilerParams(vmem_limit_bytes=limit << 20),
+            compiler_params=pltpu.CompilerParams(vmem_limit_bytes=min(held + (12 << 20), 60 << 20)),
             **more,
         )(*operands)
 
@@ -291,7 +302,6 @@
         shape(block, jnp.bfloat16),
         (spectra, band_weights[None, :]),
         [pl.BlockSpec(memory_space=pltpu.HBM)] * 2,
-        4,
         scratch_shapes=[
             pltpu.VMEM((block, width), spectra.dtype),
             pltpu.VMEM((1, freqs), jnp.float32),
@@ -299,7 +309,7 @@
         ],
     )
     turned = call(
-        rotate_kernel, shape(len(SHIFTS) * block, jnp.bfloat16), (table, whitened), [vmem] * 2, 8
+        rotate_kernel, shape(len(SHIFTS) * block, jnp.bfloat16), (table, whitened), [vmem] * 2
     )
     lines = [whitened]
     for dz in range(1, n_lines):
@@ -318,44 +328,49 @@
     swapped = [[send(tile, lambda r, z, k: (r, z, k ^ 1)) for tile in group] for group in groups]
     n_row, n_col = n_cols * block, n_rows * block
     sizes = (n_rows, n_cols)
-    total = shape(len(SHIFTS) * block, jnp.float32)
+    every = [[*groups[dz], *swapped[dz]] for dz in range(n_lines)]
+    weights_shape = shape(len(SHIFTS) * block, jnp.bfloat16, PAIR * n_rows * block)
     picked_shape = shape(LAGS * PAIR * block, jnp.bfloat16)
     staged = pltpu.VMEM((PAIR * block, width), jnp.bfloat16)
     part_shape = (n_rows // PAIR, n_row, LAGS * PAIR * block)
-    state, picked = [], []
+    common = [selected_bins, lag_weights, table, turned]
+    weights, picked = [], []
     for dz in range(n_lines - 1):
-        operands = [selected_bins, lag_weights, table, turned, *groups[dz], *swapped[dz]]
-        base = len(operands)
-        operands += state
-        new_state, new_picked = call(
-            functools.partial(bundle_kernel, sizes, dz, not state),
-            (total, picked_shape),
+        operands = [*common, *every[dz]]
+        new_weights, new_picked = call(
+            functools.partial(bundle_kernel, sizes, dz),
+            (weights_shape, picked_shape),
             operands,
             [smem] * 2 + [vmem] * (len(operands) - 2),
-            20,
             scratch_shapes=[staged],
-            input_output_aliases={base: 0} if state else {},
         )
-        state = [new_state]
+        weights.append(new_weights)
         picked.append(new_picked)
     last = n_lines - 1
-    lines = [pair[dz][0] for dz in range(n_lines) for pair in (groups, swapped)]
+    operands = [selected_bins, lag_weights, turned, *every[last][:-1]]
+    weights.append(
+        call(
+            functools.partial(partial_kernel, sizes, last),
+            shape(len(SHIFTS) * block, jnp.bfloat16, (PAIR * n_rows - 1) * block),
+            operands,
+            [smem] * 2 + [vmem] * (len(operands) - 2),
+        )
+    )
+    lines = [tile for group in every for tile in group[::n_rows]]
     parts = call(
         functools.partial(corr_kernel, sizes),
         shape(part_shape[0], jnp.float32, *part_shape[1:]),
         [*lines, *picked],
         [vmem] * (n_cols + n_lines - 1),
-        20 if n_lines <= n_rows else 40,
-    )
-    operands = [selected_bins, lag_weights, table, turned, *groups[last], *swapped[last], *lines, *state, parts]
+    )
+    operands = [*common, *(tile for group in every for tile in group), *weights, parts]
     correlations, gradient = call(
-        functools.partial(end_kernel, sizes, last),
+        functools.partial(end_kernel, sizes, n_lines - 1),
         (shape(LAGS, jnp.float32, n_row, n_col), shape(block, jnp.float32)),
         operands,
         [smem] * 2 + [vmem] * (len(operands) - 2),
-        36,
         scratch_shapes=[
-            pltpu.VMEM(total.shape, total.dtype),
+            pltpu.VMEM((len(SHIFTS) * block, n_rows * n_cols * block), jnp.bfloat16),
             staged,
             pltpu.VMEM(picked_shape.shape, picked_shape.dtype),
             pltpu.VMEM(part_shape, jnp.float32),

time: 70.6 us -> 69.7 us (0.987)
  waiting for transfers between devices: 29.8 us -> 32.9 us
  starting transfers between devices: 22.8 us -> 20.2 us
  Pallas kernels: 14.6 us -> 13.1 us
    ppermute x31, waiting for transfers between devices: 29.8 us -> 32.9 us  [send(): return lax.ppermute(value, ('rows', 'cols'), pairs)]
    ppermute x31, starting transfers between devices: 22.8 us -> 20.2 us  [send(): return lax.ppermute(value, ('rows', 'cols'), pairs)]
    pallas_call x7 -> x8, Pallas kernels: 14.6 us -> 13.1 us  [call(): pl.pallas_call(kernel, out_shape=outs, in_specs=specs, out_specs=jax.tree...]
    unnamed x10 -> x12, local copies, waits for them, and re-layouts: 2.42 us -> 2.42 us
  transfers between devices with their start and end apart: 31 -> 31, of which waited for: 9 -> 10; matrix products, arithmetic and copies ran while one was open for 0% -> 0% of each run, Pallas kernels for 15% -> 12%
where the time goes in v4:
time: 69.7 us; the launch traced here: 69.4 us
  waiting for transfers between devices  32.9 us (47%)
  starting transfers between devices  20.2 us (29%)
  Pallas kernels  13.1 us (19%)
  local copies, waits for them, and re-layouts  2.42 us (3%)
  between operations  0.8 us (1%)
    ppermute x31, waiting for transfers between devices, send(): return lax.ppermute(value, ('rows', 'cols'), pairs)  32.9 us
    ppermute x31, starting transfers between devices, send(): return lax.ppermute(value, ('rows', 'cols'), pairs)  20.2 us
    pallas_call x8, Pallas kernels, call(): pl.pallas_call(kernel, out_shape=outs, in_specs=specs, out_specs=jax.tree...  13.1 us
    unnamed x12, local copies, waits for them, and re-layouts  2.42 us
  transfers between devices with their start and end apart: 31, of which 10 were waited for; matrix products, arithmetic and copies ran while one was open for 0% of the time, Pallas kernels for 12%

profile of v4, /device:TPU:0, one launch (start us, length us, event | category | flops | bytes accessed | tf_op | source)
XLA Modules:
  0.0 69.4 jit_solution(2285056350882085852)
XLA Ops:
  0.7 1.0 %copy-done.2 = bf16[32,4096]{1,0:T(8,128)(2,1)S(1)} copy-done((bf16[32,4096]{1,0:T(8,128)(2,1)S(1)}, bf16[32,4096]{1,0:T(8,128)(2,1)}, u32[]{:S(2)}) %copy-start.2) | copy-done | bytes 262168
  1.6 0.7 %copy-done.5 = f32[2048]{0:T(1024)S(1)} copy-done((f32[2048]{0:T(1024)S(1)}, f32[2048]{0:T(1024)}, u32[]{:S(2)}) %copy-start.5) | copy-done | bytes 8216
  2.5 3.0 %collective-permute-start = (bf16[32,4096]{1,0:T(8,128)(2,1)S(1)}, bf16[32,4096]{1,0:T(8,128)(2,1)S(1)}, u32[]{:S(2)}, u32[]{:S(2)}) collective-permute-start(bf16[32,4096]{1,0:T(8,128)(2,1)S(1)} %shard_map.68.own_ref.refs_0_), channel_id=1, source_target_pairs={{0,8},{1,17},{2,10},{3,19},{4,12},{5,21},{6,14},{7,23},{8,0},{9,25... | collective-permute-start | bytes 786440 | tf_op jit(solution)/shard_map/ppermute | solution.py:278
  5.6 1.6 %collective-permute-start.7 = (bf16[32,4096]{1,0:T(8,128)(2,1)S(1)}, bf16[32,4096]{1,0:T(8,128)(2,1)S(1)}, u32[]{:S(2)}, u32[]{:S(2)}) collective-permute-start(bf16[32,4096]{1,0:T(8,128)(2,1)S(1)} %shard_map.68.own_ref.refs_0_), channel_id=1, source_target_pairs={{0,2},{1,3},{2,0},{3,1},{4,6},{5,7},{6,4},{7,5},{8,10},{9,11},{10,... | collective-permute-start | bytes 786440 | tf_op jit(solution)/shard_map/ppermute | solution.py:278
  7.1 2.6 %collective-permute-start.15 = (bf16[32,4096]{1,0:T(8,128)(2,1)S(1)}, bf16[32,4096]{1,0:T(8,128)(2,1)S(1)}, u32[]{:S(2)}, u32[]{:S(2)}) collective-permute-start(bf16[32,4096]{1,0:T(8,128)(2,1)S(1)} %shard_map.68.own_ref.refs_0_), channel_id=1, source_target_pairs={{0,4},{1,5},{2,6},{3,7},{4,0},{5,1},{6,2},{7,3},{8,12},{9,13},{10,... | collective-permute-start | bytes 786440 | tf_op jit(solution)/shard_map/ppermute | solution.py:278
  9.7 1.5 %collective-permute-start.1 = (bf16[32,4096]{1,0:T(8,128)(2,1)S(1)}, bf16[32,4096]{1,0:T(8,128)(2,1)S(1)}, u32[]{:S(2)}, u32[]{:S(2)}) collective-permute-start(bf16[32,4096]{1,0:T(8,128)(2,1)S(1)} %shard_map.68.own_ref.refs_0_), channel_id=1, source_target_pairs={{0,16},{1,9},{2,18},{3,11},{4,20},{5,13},{6,22},{7,15},{8,24},{9,1... | collective-permute-start | bytes 786440 | tf_op jit(solution)/shard_map/ppermute | solution.py:278
  11.3 0.8 %collective-permute-start.2 = (bf16[32,4096]{1,0:T(8,128)(2,1)S(1)}, bf16[32,4096]{1,0:T(8,128)(2,1)S(1)}, u32[]{:S(2)}, u32[]{:S(2)}) collective-permute-start(bf16[32,4096]{1,0:T(8,128)(2,1)S(1)} %collective-permute-done.refs_1_), channel_id=1, source_target_pairs={{0,16},{1,9},{2,18},{3,11},{4,20},{5,13},{6,22},{7,15},{8,24},{9,1... | collective-permute-start | bytes 786440 | tf_op jit(solution)/shard_map/ppermute | solution.py:278
  12.1 6.8 %collective-permute-done.7.refs_0_.refs_2_.refs_8_ = bf16[32,4096]{1,0:T(8,128)(2,1)S(1)} collective-permute-done((bf16[32,4096]{1,0:T(8,128)(2,1)S(1)}, bf16[32,4096]{1,0:T(8,128)(2,1)S(1)}, u32[]{:S(2)}, u32[]{:S(2)}) %collective-permute-start.7) | collective-permute-done | bytes 262176 | tf_op jit(solution)/shard_map/ppermute | solution.py:278
  18.9 1.5 %collective-permute-start.8 = (bf16[32,4096]{1,0:T(8,128)(2,1)S(1)}, bf16[32,4096]{1,0:T(8,128)(2,1)S(1)}, u32[]{:S(2)}, u32[]{:S(2)}) collective-permute-start(bf16[32,4096]{1,0:T(8,128)(2,1)S(1)} %collective-permute-done.7.refs_0_.refs_2_.refs_8_), channel_id=1, source_target_pairs={{0,8},{1,17},{2,10},{3,19},{4,12},{5,21},{6,14},{7,23},{8,0},{9,25... | collective-permute-start | bytes 786440 | tf_op jit(solution)/shard_map/ppermute | solution.py:278
  20.3 0.9 %collective-permute-done.15.refs_0_.refs_4_.refs_16_ = bf16[32,4096]{1,0:T(8,128)(2,1)S(1)} collective-permute-done((bf16[32,4096]{1,0:T(8,128)(2,1)S(1)}, bf16[32,4096]{1,0:T(8,128)(2,1)S(1)}, u32[]{:S(2)}, u32[]{:S(2)}) %collective-permute-start.15) | collective-permute-done | bytes 262176 | tf_op jit(solution)/shard_map/ppermute | solution.py:278
  21.7 1.6 %collective-permute-start.16 = (bf16[32,4096]{1,0:T(8,128)(2,1)S(1)}, bf16[32,4096]{1,0:T(8,128)(2,1)S(1)}, u32[]{:S(2)}, u32[]{:S(2)}) collective-permute-start(bf16[32,4096]{1,0:T(8,128)(2,1)S(1)} %collective-permute-done.15.refs_0_.refs_4_.refs_16_), channel_id=1, source_target_pairs={{0,8},{1,17},{2,10},{3,19},{4,12},{5,21},{6,14},{7,23},{8,0},{9,25... | collective-permute-start | bytes 786440 | tf_op jit(solution)/shard_map/ppermute | solution.py:278
  23.3 1.5 %collective-permute-start.17 = (bf16[32,4096]{1,0:T(8,128)(2,1)S(1)}, bf16[32,4096]{1,0:T(8,128)(2,1)S(1)}, u32[]{:S(2)}, u32[]{:S(2)}) collective-permute-start(bf16[32,4096]{1,0:T(8,128)(2,1)S(1)} %collective-permute-done.15.refs_0_.refs_4_.refs_16_), channel_id=1, source_target_pairs={{0,16},{1,9},{2,18},{3,11},{4,20},{5,13},{6,22},{7,15},{8,24},{9,1... | collective-permute-start | bytes 786440 | tf_op jit(solution)/shard_map/ppermute | solution.py:278
  24.8 3.0 %collective-permute-done.8.refs_1_.refs_9_ = bf16[32,4096]{1,0:T(8,128)(2,1)S(1)} collective-permute-done((bf16[32,4096]{1,0:T(8,128)(2,1)S(1)}, bf16[32,4096]{1,0:T(8,128)(2,1)S(1)}, u32[]{:S(2)}, u32[]{:S(2)}) %collective-permute-start.8) | collective-permute-done | bytes 262176 | tf_op jit(solution)/shard_map/ppermute | solution.py:278
  27.8 2.6 %collective-permute-done.9.refs_2_.refs_10_ = bf16[32,4096]{1,0:T(8,128)(2,1)S(1)} collective-permute-done((bf16[32,4096]{1,0:T(8,128)(2,1)S(1)}, bf16[32,4096]{1,0:T(8,128)(2,1)S(1)}, u32[]{:S(2)}, u32[]{:S(2)}) %collective-permute-start.9) | collective-permute-done | bytes 262176 | tf_op jit(solution)/shard_map/ppermute | solution.py:278
  30.8 1.7 %collective-permute-done.16.refs_1_.refs_17_ = bf16[32,4096]{1,0:T(8,128)(2,1)S(1)} collective-permute-done((bf16[32,4096]{1,0:T(8,128)(2,1)S(1)}, bf16[32,4096]{1,0:T(8,128)(2,1)S(1)}, u32[]{:S(2)}, u32[]{:S(2)}) %collective-permute-start.16) | collective-permute-done | bytes 262176 | tf_op jit(solution)/shard_map/ppermute | solution.py:278
  32.5 0.7 collective-permute-done.17.refs_2_.refs_18_
  33.2 0.5 collective-permute-start.13
  33.7 0.5 collective-permute-start.18
  34.3 5.3 %collective-permute-done.23.refs_0_.refs_6_.refs_24_ = bf16[32,4096]{1,0:T(8,128)(2,1)S(1)} collective-permute-done((bf16[32,4096]{1,0:T(8,128)(2,1)S(1)}, bf16[32,4096]{1,0:T(8,128)(2,1)S(1)}, u32[]{:S(2)}, u32[]{:S(2)}) %collective-permute-start.23) | collective-permute-done | bytes 262176 | tf_op jit(solution)/shard_map/ppermute | solution.py:278
  39.5 5.2 %collective-permute-done.10.refs_3_.refs_11_ = bf16[32,4096]{1,0:T(8,128)(2,1)S(1)} collective-permute-done((bf16[32,4096]{1,0:T(8,128)(2,1)S(1)}, bf16[32,4096]{1,0:T(8,128)(2,1)S(1)}, u32[]{:S(2)}, u32[]{:S(2)}) %collective-permute-start.10) | collective-permute-done | bytes 262176 | tf_op jit(solution)/shard_map/ppermute | solution.py:278
  44.7 1.5 %collective-permute-start.24 = (bf16[32,4096]{1,0:T(8,128)(2,1)S(1)}, bf16[32,4096]{1,0:T(8,128)(2,1)S(1)}, u32[]{:S(2)}, u32[]{:S(2)}) collective-permute-start(bf16[32,4096]{1,0:T(8,128)(2,1)S(1)} %collective-permute-done.23.refs_0_.refs_6_.refs_24_), channel_id=1, source_target_pairs={{0,8},{1,17},{2,10},{3,19},{4,12},{5,21},{6,14},{7,23},{8,0},{9,25... | collective-permute-start | bytes 786440 | tf_op jit(solution)/shard_map/ppermute | solution.py:278
  47.2 5.3 %collective-permute-done.24.refs_1_.refs_25_ = bf16[32,4096]{1,0:T(8,128)(2,1)S(1)} collective-permute-done((bf16[32,4096]{1,0:T(8,128)(2,1)S(1)}, bf16[32,4096]{1,0:T(8,128)(2,1)S(1)}, u32[]{:S(2)}, u32[]{:S(2)}) %collective-permute-start.24) | collective-permute-done | bytes 262176 | tf_op jit(solution)/shard_map/ppermute | solution.py:278
  52.6 0.5 collective-permute-start.29
  53.6 1.5 %collective-permute-done.26.refs_3_.refs_27_ = bf16[32,4096]{1,0:T(8,128)(2,1)S(1)} collective-permute-done((bf16[32,4096]{1,0:T(8,128)(2,1)S(1)}, bf16[32,4096]{1,0:T(8,128)(2,1)S(1)}, u32[]{:S(2)}, u32[]{:S(2)}) %collective-permute-start.26) | collective-permute-done | bytes 262176 | tf_op jit(solution)/shard_map/ppermute | solution.py:278
  55.1 0.5 collective-permute-start.22
  55.7 0.8 %copy-done = f32[4,2048]{1,0:T(4,128)S(1)} copy-done((f32[4,2048]{1,0:T(4,128)S(1)}, f32[4,2048]{1,0:T(4,128)}, u32[]{:S(2)}) %copy-start) | copy-done | bytes 32792
  56.8 2.1 %shard_map.70 = (bf16[160,256]{1,0:T(8,128)(2,1)S(1)}, bf16[256,4096]{1,0:T(8,128)(2,1)S(1)}) custom-call(s32[8]{0:T(128)S(1)} %copy-done.3, f32[4]{0:T(128)S(1)} %copy-done.4, f32[4,2048]{1,0:T(4,128)S(1)} %copy-done, bf16[160,4096]{1,0:T(8,128)(2,1)S(1)} %shard_map.69.turned_ref, bf16[32,4096]{1,0:T(8,128)(2,1)S(1)} %shard_map.68.own_ref.refs_0_, ...), custom_call_target="tpu_custom_call" | custom-call | tf_op jit(solution)/shard_map/pallas_call | solution.py:288
  58.8 1.3 %shard_map.73.refs_35_ = bf16[160,224]{1,0:T(8,128)(2,1)S(1)} custom-call(s32[8]{0:T(128)S(1)} %copy-done.3, f32[4]{0:T(128)S(1)} %copy-done.4, bf16[160,4096]{1,0:T(8,128)(2,1)S(1)} %shard_map.69.turned_ref, bf16[32,4096]{1,0:T(8,128)(2,1)S(1)} %collective-permute-done.23.refs_0_.refs_6_.refs_24_, ...), custom_call_target="tpu_custom_call" | custom-call | tf_op jit(solution)/shard_map/pallas_call | solution.py:288
  60.1 2.1 %shard_map.71 = (bf16[160,256]{1,0:T(8,128)(2,1)S(1)}, bf16[256,4096]{1,0:T(8,128)(2,1)S(1)}) custom-call(s32[8]{0:T(128)S(1)} %copy-done.3, f32[4]{0:T(128)S(1)} %copy-done.4, f32[4,2048]{1,0:T(4,128)S(1)} %copy-done, bf16[160,4096]{1,0:T(8,128)(2,1)S(1)} %shard_map.69.turned_ref, bf16[32,4096]{1,0:T(8,128)(2,1)S(1)} %collective-permute-done.7.refs_0_.refs_2_.refs_8_, ...), custom_call_target="tpu_custom_call" | custom-call | tf_op jit(solution)/shard_map/pallas_call | solution.py:288
  62.2 1.4 %shard_map.72 = (bf16[160,256]{1,0:T(8,128)(2,1)S(1)}, bf16[256,4096]{1,0:T(8,128)(2,1)S(1)}) custom-call(s32[8]{0:T(128)S(1)} %copy-done.3, f32[4]{0:T(128)S(1)} %copy-done.4, f32[4,2048]{1,0:T(4,128)S(1)} %copy-done, bf16[160,4096]{1,0:T(8,128)(2,1)S(1)} %shard_map.69.turned_ref, bf16[32,4096]{1,0:T(8,128)(2,1)S(1)} %collective-permute-done.15.refs_0_.refs_4_.refs_16_, ...), custom_call_target="tpu_custom_call" | custom-call | tf_op jit(solution)/shard_map/pallas_call | solution.py:288
  63.6 1.5 %shard_map.74.refs_36_ = f32[2,256,256]{2,1,0:T(8,128)S(1)} custom-call(bf16[32,4096]{1,0:T(8,128)(2,1)S(1)} %shard_map.68.own_ref.refs_0_, bf16[32,4096]{1,0:T(8,128)(2,1)S(1)} %collective-permute-done.3.refs_4_.refs_1_, bf16[32,4096]{1,0:T(8,128)(2,1)S(1)} %collective-permute-done.7.refs_0_.refs_2_.refs_8_, ...), custom_call_target="tpu_custom_call" | custom-call | tf_op jit(solution)/shard_map/pallas_call | solution.py:288
  65.2 4.3 %shard_map.75 = (f32[4,256,128]{2,1,0:T(8,128)}, f32[32,4096]{1,0:T(8,128)}) custom-call(s32[8]{0:T(128)S(1)} %copy-done.3, f32[4]{0:T(128)S(1)} %copy-done.4, f32[4,2048]{1,0:T(4,128)S(1)} %copy-done.1, bf16[160,4096]{1,0:T(8,128)(2,1)S(1)} %shard_map.69.turned_ref, bf16[32,4096]{1,0:T(8,128)(2,1)S(1)} %shard_map.68.own_ref.refs_0_, ...), custom_call_target="tpu_custom_call" | custom-call | tf_op jit(solution)/shard_map/pallas_call | solution.py:288
  (50 shorter events, 3.2 us)
Async XLA Ops:
  0.6 56.1 %copy-start.4 = (f32[4]{0:T(128)S(1)}, f32[4]{0:T(128)}, u32[]{:S(2)}) copy-start(f32[4]{0:T(128)} %lag_ref.9) | copy-start | bytes 52
  2.5 8.7 %collective-permute-start = (bf16[32,4096]{1,0:T(8,128)(2,1)S(1)}, bf16[32,4096]{1,0:T(8,128)(2,1)S(1)}, u32[]{:S(2)}, u32[]{:S(2)}) collective-permute-start(bf16[32,4096]{1,0:T(8,128)(2,1)S(1)} %shard_map.68.own_ref.refs_0_), channel_id=1, source_target_pairs={{0,8},{1,17},{2,10},{3,19},{4,12},{5,21},{6,14},{7,23},{8,0},{9,25... | collective-permute-start | bytes 786440 | tf_op jit(solution)/shard_map/ppermute | solution.py:278
  5.6 13.3 %collective-permute-start.7 = (bf16[32,4096]{1,0:T(8,128)(2,1)S(1)}, bf16[32,4096]{1,0:T(8,128)(2,1)S(1)}, u32[]{:S(2)}, u32[]{:S(2)}) collective-permute-start(bf16[32,4096]{1,0:T(8,128)(2,1)S(1)} %shard_map.68.own_ref.refs_0_), channel_id=1, source_target_pairs={{0,2},{1,3},{2,0},{3,1},{4,6},{5,7},{6,4},{7,5},{8,10},{9,11},{10,... | collective-permute-start | bytes 786440 | tf_op jit(solution)/shard_map/ppermute | solution.py:278
  7.1 14.1 %collective-permute-start.15 = (bf16[32,4096]{1,0:T(8,128)(2,1)S(1)}, bf16[32,4096]{1,0:T(8,128)(2,1)S(1)}, u32[]{:S(2)}, u32[]{:S(2)}) collective-permute-start(bf16[32,4096]{1,0:T(8,128)(2,1)S(1)} %shard_map.68.own_ref.refs_0_), channel_id=1, source_target_pairs={{0,4},{1,5},{2,6},{3,7},{4,0},{5,1},{6,2},{7,3},{8,12},{9,13},{10,... | collective-permute-start | bytes 786440 | tf_op jit(solution)/shard_map/ppermute | solution.py:278
  9.7 12.0 %collective-permute-start.1 = (bf16[32,4096]{1,0:T(8,128)(2,1)S(1)}, bf16[32,4096]{1,0:T(8,128)(2,1)S(1)}, u32[]{:S(2)}, u32[]{:S(2)}) collective-permute-start(bf16[32,4096]{1,0:T(8,128)(2,1)S(1)} %shard_map.68.own_ref.refs_0_), channel_id=1, source_target_pairs={{0,16},{1,9},{2,18},{3,11},{4,20},{5,13},{6,22},{7,15},{8,24},{9,1... | collective-permute-start | bytes 786440 | tf_op jit(solution)/shard_map/ppermute | solution.py:278
  11.2 10.5 %collective-permute-start.3 = (bf16[32,4096]{1,0:T(8,128)(2,1)S(1)}, bf16[32,4096]{1,0:T(8,128)(2,1)S(1)}, u32[]{:S(2)}, u32[]{:S(2)}) collective-permute-start(bf16[32,4096]{1,0:T(8,128)(2,1)S(1)} %shard_map.68.own_ref.refs_0_), channel_id=1, source_target_pairs={{0,1},{1,0},{2,3},{3,2},{4,5},{5,4},{6,7},{7,6},{8,9},{9,8},{10,11... | collective-permute-start | bytes 786440 | tf_op jit(solution)/shard_map/ppermute | solution.py:278
  11.3 12.0 %collective-permute-start.2 = (bf16[32,4096]{1,0:T(8,128)(2,1)S(1)}, bf16[32,4096]{1,0:T(8,128)(2,1)S(1)}, u32[]{:S(2)}, u32[]{:S(2)}) collective-permute-start(bf16[32,4096]{1,0:T(8,128)(2,1)S(1)} %collective-permute-done.refs_1_), channel_id=1, source_target_pairs={{0,16},{1,9},{2,18},{3,11},{4,20},{5,13},{6,22},{7,15},{8,24},{9,1... | collective-permute-start | bytes 786440 | tf_op jit(solution)/shard_map/ppermute | solution.py:278
  18.9 8.9 %collective-permute-start.8 = (bf16[32,4096]{1,0:T(8,128)(2,1)S(1)}, bf16[32,4096]{1,0:T(8,128)(2,1)S(1)}, u32[]{:S(2)}, u32[]{:S(2)}) collective-permute-start(bf16[32,4096]{1,0:T(8,128)(2,1)S(1)} %collective-permute-done.7.refs_0_.refs_2_.refs_8_), channel_id=1, source_target_pairs={{0,8},{1,17},{2,10},{3,19},{4,12},{5,21},{6,14},{7,23},{8,0},{9,25... | collective-permute-start | bytes 786440 | tf_op jit(solution)/shard_map/ppermute | solution.py:278
  21.2 9.1 %collective-permute-start.9 = (bf16[32,4096]{1,0:T(8,128)(2,1)S(1)}, bf16[32,4096]{1,0:T(8,128)(2,1)S(1)}, u32[]{:S(2)}, u32[]{:S(2)}) collective-permute-start(bf16[32,4096]{1,0:T(8,128)(2,1)S(1)} %collective-permute-done.7.refs_0_.refs_2_.refs_8_), channel_id=1, source_target_pairs={{0,16},{1,9},{2,18},{3,11},{4,20},{5,13},{6,22},{7,15},{8,24},{9,1... | collective-permute-start | bytes 786440 | tf_op jit(solution)/shard_map/ppermute | solution.py:278
  21.7 8.6 %collective-permute-start.11 = (bf16[32,4096]{1,0:T(8,128)(2,1)S(1)}, bf16[32,4096]{1,0:T(8,128)(2,1)S(1)}, u32[]{:S(2)}, u32[]{:S(2)}) collective-permute-start(bf16[32,4096]{1,0:T(8,128)(2,1)S(1)} %collective-permute-done.7.refs_0_.refs_2_.refs_8_), channel_id=1, source_target_pairs={{0,1},{1,0},{2,3},{3,2},{4,5},{5,4},{6,7},{7,6},{8,9},{9,8},{10,11... | collective-permute-start | bytes 786440 | tf_op jit(solution)/shard_map/ppermute | solution.py:278
  21.7 10.8 %collective-permute-start.16 = (bf16[32,4096]{1,0:T(8,128)(2,1)S(1)}, bf16[32,4096]{1,0:T(8,128)(2,1)S(1)}, u32[]{:S(2)}, u32[]{:S(2)}) collective-permute-start(bf16[32,4096]{1,0:T(8,128)(2,1)S(1)} %collective-permute-done.15.refs_0_.refs_4_.refs_16_), channel_id=1, source_target_pairs={{0,8},{1,17},{2,10},{3,19},{4,12},{5,21},{6,14},{7,23},{8,0},{9,25... | collective-permute-start | bytes 786440 | tf_op jit(solution)/shard_map/ppermute | solution.py:278
  23.3 9.9 %collective-permute-start.17 = (bf16[32,4096]{1,0:T(8,128)(2,1)S(1)}, bf16[32,4096]{1,0:T(8,128)(2,1)S(1)}, u32[]{:S(2)}, u32[]{:S(2)}) collective-permute-start(bf16[32,4096]{1,0:T(8,128)(2,1)S(1)} %collective-permute-done.15.refs_0_.refs_4_.refs_16_), channel_id=1, source_target_pairs={{0,16},{1,9},{2,18},{3,11},{4,20},{5,13},{6,22},{7,15},{8,24},{9,1... | collective-permute-start | bytes 786440 | tf_op jit(solution)/shard_map/ppermute | solution.py:278
  27.8 5.4 %collective-permute-start.4 = (bf16[32,4096]{1,0:T(8,128)(2,1)S(1)}, bf16[32,4096]{1,0:T(8,128)(2,1)S(1)}, u32[]{:S(2)}, u32[]{:S(2)}) collective-permute-start(bf16[32,4096]{1,0:T(8,128)(2,1)S(1)} %collective-permute-done.refs_1_), channel_id=1, source_target_pairs={{0,1},{1,0},{2,3},{3,2},{4,5},{5,4},{6,7},{7,6},{8,9},{9,8},{10,11... | collective-permute-start | bytes 786440 | tf_op jit(solution)/shard_map/ppermute | solution.py:278
  30.3 3.4 %collective-permute-start.5 = (bf16[32,4096]{1,0:T(8,128)(2,1)S(1)}, bf16[32,4096]{1,0:T(8,128)(2,1)S(1)}, u32[]{:S(2)}, u32[]{:S(2)}) collective-permute-start(bf16[32,4096]{1,0:T(8,128)(2,1)S(1)} %collective-permute-done.1.refs_2_), channel_id=1, source_target_pairs={{0,1},{1,0},{2,3},{3,2},{4,5},{5,4},{6,7},{7,6},{8,9},{9,8},{10,11... | collective-permute-start | bytes 786440 | tf_op jit(solution)/shard_map/ppermute | solution.py:278
  30.3 9.2 %collective-permute-start.23 = (bf16[32,4096]{1,0:T(8,128)(2,1)S(1)}, bf16[32,4096]{1,0:T(8,128)(2,1)S(1)}, u32[]{:S(2)}, u32[]{:S(2)}) collective-permute-start(bf16[32,4096]{1,0:T(8,128)(2,1)S(1)} %collective-permute-done.15.refs_0_.refs_4_.refs_16_), channel_id=1, source_target_pairs={{0,2},{1,3},{2,0},{3,1},{4,6},{5,7},{6,4},{7,5},{8,10},{9,11},{10,... | collective-permute-start | bytes 786440 | tf_op jit(solution)/shard_map/ppermute | solution.py:278
  32.5 12.1 %collective-permute-start.10 = (bf16[32,4096]{1,0:T(8,128)(2,1)S(1)}, bf16[32,4096]{1,0:T(8,128)(2,1)S(1)}, u32[]{:S(2)}, u32[]{:S(2)}) collective-permute-start(bf16[32,4096]{1,0:T(8,128)(2,1)S(1)} %collective-permute-done.2.refs_3_), channel_id=1, source_target_pairs={{0,2},{1,3},{2,0},{3,1},{4,6},{5,7},{6,4},{7,5},{8,10},{9,11},{10,... | collective-permute-start | bytes 786440 | tf_op jit(solution)/shard_map/ppermute | solution.py:278
  33.2 13.0 %collective-permute-start.12 = (bf16[32,4096]{1,0:T(8,128)(2,1)S(1)}, bf16[32,4096]{1,0:T(8,128)(2,1)S(1)}, u32[]{:S(2)}, u32[]{:S(2)}) collective-permute-start(bf16[32,4096]{1,0:T(8,128)(2,1)S(1)} %collective-permute-done.8.refs_1_.refs_9_), channel_id=1, source_target_pairs={{0,1},{1,0},{2,3},{3,2},{4,5},{5,4},{6,7},{7,6},{8,9},{9,8},{10,11... | collective-permute-start | bytes 786440 | tf_op jit(solution)/shard_map/ppermute | solution.py:278
  33.2 13.0 %collective-permute-start.13 = (bf16[32,4096]{1,0:T(8,128)(2,1)S(1)}, bf16[32,4096]{1,0:T(8,128)(2,1)S(1)}, u32[]{:S(2)}, u32[]{:S(2)}) collective-permute-start(bf16[32,4096]{1,0:T(8,128)(2,1)S(1)} %collective-permute-done.9.refs_2_.refs_10_), channel_id=1, source_target_pairs={{0,1},{1,0},{2,3},{3,2},{4,5},{5,4},{6,7},{7,6},{8,9},{9,8},{10,11... | collective-permute-start | bytes 786440 | tf_op jit(solution)/shard_map/ppermute | solution.py:278
  33.7 12.5 %collective-permute-start.18 = (bf16[32,4096]{1,0:T(8,128)(2,1)S(1)}, bf16[32,4096]{1,0:T(8,128)(2,1)S(1)}, u32[]{:S(2)}, u32[]{:S(2)}) collective-permute-start(bf16[32,4096]{1,0:T(8,128)(2,1)S(1)} %collective-permute-done.16.refs_1_.refs_17_), channel_id=1, source_target_pairs={{0,16},{1,9},{2,18},{3,11},{4,20},{5,13},{6,22},{7,15},{8,24},{9,1... | collective-permute-start | bytes 786440 | tf_op jit(solution)/shard_map/ppermute | solution.py:278
  39.5 7.2 %collective-permute-start.6 = (bf16[32,4096]{1,0:T(8,128)(2,1)S(1)}, bf16[32,4096]{1,0:T(8,128)(2,1)S(1)}, u32[]{:S(2)}, u32[]{:S(2)}) collective-permute-start(bf16[32,4096]{1,0:T(8,128)(2,1)S(1)} %collective-permute-done.2.refs_3_), channel_id=1, source_target_pairs={{0,1},{1,0},{2,3},{3,2},{4,5},{5,4},{6,7},{7,6},{8,9},{9,8},{10,11... | collective-permute-start | bytes 786440 | tf_op jit(solution)/shard_map/ppermute | solution.py:278
  44.7 7.9 %collective-permute-start.24 = (bf16[32,4096]{1,0:T(8,128)(2,1)S(1)}, bf16[32,4096]{1,0:T(8,128)(2,1)S(1)}, u32[]{:S(2)}, u32[]{:S(2)}) collective-permute-start(bf16[32,4096]{1,0:T(8,128)(2,1)S(1)} %collective-permute-done.23.refs_0_.refs_6_.refs_24_), channel_id=1, source_target_pairs={{0,8},{1,17},{2,10},{3,19},{4,12},{5,21},{6,14},{7,23},{8,0},{9,25... | collective-permute-start | bytes 786440 | tf_op jit(solution)/shard_map/ppermute | solution.py:278
  46.2 6.4 %collective-permute-start.25 = (bf16[32,4096]{1,0:T(8,128)(2,1)S(1)}, bf16[32,4096]{1,0:T(8,128)(2,1)S(1)}, u32[]{:S(2)}, u32[]{:S(2)}) collective-permute-start(bf16[32,4096]{1,0:T(8,128)(2,1)S(1)} %collective-permute-done.23.refs_0_.refs_6_.refs_24_), channel_id=1, source_target_pairs={{0,16},{1,9},{2,18},{3,11},{4,20},{5,13},{6,22},{7,15},{8,24},{9,1... | collective-permute-start | bytes 786440 | tf_op jit(solution)/shard_map/ppermute | solution.py:278
  46.2 6.9 %collective-permute-start.27 = (bf16[32,4096]{1,0:T(8,128)(2,1)S(1)}, bf16[32,4096]{1,0:T(8,128)(2,1)S(1)}, u32[]{:S(2)}, u32[]{:S(2)}) collective-permute-start(bf16[32,4096]{1,0:T(8,128)(2,1)S(1)} %collective-permute-done.23.refs_0_.refs_6_.refs_24_), channel_id=1, source_target_pairs={{0,1},{1,0},{2,3},{3,2},{4,5},{5,4},{6,7},{7,6},{8,9},{9,8},{10,11... | collective-permute-start | bytes 786440 | tf_op jit(solution)/shard_map/ppermute | solution.py:278
  46.3 6.9 %collective-permute-start.14 = (bf16[32,4096]{1,0:T(8,128)(2,1)S(1)}, bf16[32,4096]{1,0:T(8,128)(2,1)S(1)}, u32[]{:S(2)}, u32[]{:S(2)}) collective-permute-start(bf16[32,4096]{1,0:T(8,128)(2,1)S(1)} %collective-permute-done.10.refs_3_.refs_11_), channel_id=1, source_target_pairs={{0,1},{1,0},{2,3},{3,2},{4,5},{5,4},{6,7},{7,6},{8,9},{9,8},{10,11... | collective-permute-start | bytes 786440 | tf_op jit(solution)/shard_map/ppermute | solution.py:278
  46.8 8.3 %collective-permute-start.26 = (bf16[32,4096]{1,0:T(8,128)(2,1)S(1)}, bf16[32,4096]{1,0:T(8,128)(2,1)S(1)}, u32[]{:S(2)}, u32[]{:S(2)}) collective-permute-start(bf16[32,4096]{1,0:T(8,128)(2,1)S(1)} %collective-permute-done.18.refs_3_.refs_19_), channel_id=1, source_target_pairs={{0,2},{1,3},{2,0},{3,1},{4,6},{5,7},{6,4},{7,5},{8,10},{9,11},{10,... | collective-permute-start | bytes 786440 | tf_op jit(solution)/shard_map/ppermute | solution.py:278
  52.6 2.5 %collective-permute-start.28 = (bf16[32,4096]{1,0:T(8,128)(2,1)S(1)}, bf16[32,4096]{1,0:T(8,128)(2,1)S(1)}, u32[]{:S(2)}, u32[]{:S(2)}) collective-permute-start(bf16[32,4096]{1,0:T(8,128)(2,1)S(1)} %collective-permute-done.24.refs_1_.refs_25_), channel_id=1, source_target_pairs={{0,1},{1,0},{2,3},{3,2},{4,5},{5,4},{6,7},{7,6},{8,9},{9,8},{10,11... | collective-permute-start | bytes 786440 | tf_op jit(solution)/shard_map/ppermute | solution.py:278
  52.6 3.0 %collective-permute-start.29 = (bf16[32,4096]{1,0:T(8,128)(2,1)S(1)}, bf16[32,4096]{1,0:T(8,128)(2,1)S(1)}, u32[]{:S(2)}, u32[]{:S(2)}) collective-permute-start(bf16[32,4096]{1,0:T(8,128)(2,1)S(1)} %collective-permute-done.25.refs_2_.refs_26_), channel_id=1, source_target_pairs={{0,1},{1,0},{2,3},{3,2},{4,5},{5,4},{6,7},{7,6},{8,9},{9,8},{10,11... | collective-permute-start | bytes 786440 | tf_op jit(solution)/shard_map/ppermute | solution.py:278
  53.1 9.1 %collective-permute-start.19 = (bf16[32,4096]{1,0:T(8,128)(2,1)S(1)}, bf16[32,4096]{1,0:T(8,128)(2,1)S(1)}, u32[]{:S(2)}, u32[]{:S(2)}) collective-permute-start(bf16[32,4096]{1,0:T(8,128)(2,1)S(1)} %collective-permute-done.15.refs_0_.refs_4_.refs_16_), channel_id=1, source_target_pairs={{0,1},{1,0},{2,3},{3,2},{4,5},{5,4},{6,7},{7,6},{8,9},{9,8},{10,11... | collective-permute-start | bytes 786440 | tf_op jit(solution)/shard_map/ppermute | solution.py:278
  53.1 9.1 %collective-permute-start.20 = (bf16[32,4096]{1,0:T(8,128)(2,1)S(1)}, bf16[32,4096]{1,0:T(8,128)(2,1)S(1)}, u32[]{:S(2)}, u32[]{:S(2)}) collective-permute-start(bf16[32,4096]{1,0:T(8,128)(2,1)S(1)} %collective-permute-done.16.refs_1_.refs_17_), channel_id=1, source_target_pairs={{0,1},{1,0},{2,3},{3,2},{4,5},{5,4},{6,7},{7,6},{8,9},{9,8},{10,11... | collective-permute-start | bytes 786440 | tf_op jit(solution)/shard_map/ppermute | solution.py:278
  55.1 7.1 %collective-permute-start.21 = (bf16[32,4096]{1,0:T(8,128)(2,1)S(1)}, bf16[32,4096]{1,0:T(8,128)(2,1)S(1)}, u32[]{:S(2)}, u32[]{:S(2)}) collective-permute-start(bf16[32,4096]{1,0:T(8,128)(2,1)S(1)} %collective-permute-done.17.refs_2_.refs_18_), channel_id=1, source_target_pairs={{0,1},{1,0},{2,3},{3,2},{4,5},{5,4},{6,7},{7,6},{8,9},{9,8},{10,11... | collective-permute-start | bytes 786440 | tf_op jit(solution)/shard_map/ppermute | solution.py:278
  55.1 7.1 %collective-permute-start.22 = (bf16[32,4096]{1,0:T(8,128)(2,1)S(1)}, bf16[32,4096]{1,0:T(8,128)(2,1)S(1)}, u32[]{:S(2)}, u32[]{:S(2)}) collective-permute-start(bf16[32,4096]{1,0:T(8,128)(2,1)S(1)} %collective-permute-done.18.refs_3_.refs_19_), channel_id=1, source_target_pairs={{0,1},{1,0},{2,3},{3,2},{4,5},{5,4},{6,7},{7,6},{8,9},{9,8},{10,11... | collective-permute-start | bytes 786440 | tf_op jit(solution)/shard_map/ppermute | solution.py:278
  55.6 9.6 %collective-permute-start.30 = (bf16[32,4096]{1,0:T(8,128)(2,1)S(1)}, bf16[32,4096]{1,0:T(8,128)(2,1)S(1)}, u32[]{:S(2)}, u32[]{:S(2)}) collective-permute-start(bf16[32,4096]{1,0:T(8,128)(2,1)S(1)} %collective-permute-done.26.refs_3_.refs_27_), channel_id=1, source_target_pairs={{0,1},{1,0},{2,3},{3,2},{4,5},{5,4},{6,7},{7,6},{8,9},{9,8},{10,11... | collective-permute-start | bytes 786440 | tf_op jit(solution)/shard_map/ppermute | solution.py:278
  (5 other events, 60.1 us)

commit v5 on v4

--- a/solution.py
+++ b/solution.py
@@ -213,13 +213,34 @@
     per_line = PAIR * n_rows
     count = (n_cols // PAIR) * per_line
     every, old_weights = refs[:count], refs[count : count + dz + 1]
-    old_part_ref, corr_ref, grad_ref, weights_ref, staged_ref, picked_ref, part_ref = refs[count + dz + 1 :]
+    old_part_ref, corr_out, grad_out, weights_ref, staged_ref, picked_ref, part_ref = refs[count + dz + 1 : -3]
+    corr_ref, grad_ref, sems = refs[-3:]
+    copies = []
+
+    def write(source, target):
+        copy = pltpu.make_async_copy(source, target, sems.at[len(copies)])
+        copy.start()
+        copies.append(copy)
+
     tiles = every[dz * per_line :]
     lines = every[::n_rows]
     block, width = tiles[0].shape
     freqs = width // 2
     norm = 1.0 / np.sqrt(np.float32(width))
     place = Place(n_rows, n_cols, block)
+    pick_step(place, dz, tiles, table_ref, staged_ref, picked_ref)
+    corr_step(place, dz, lines, picked_ref, part_ref)
+    here = place.inside(dz)
+    wide = PAIR * block
+    for lag in range(LAGS):
+        cols = slice(lag * wide, (lag + 1) * wide)
+        halves = []
+        for half in range(part_ref.shape[0]):
+            fresh = here & (place.half(dz) == half)
+            halves.append(jnp.where(fresh, part_ref[half, :, cols], old_part_ref[half, :, cols]))
+        corr_ref[lag] = jnp.concatenate(halves, axis=1) * norm
+        write(corr_ref.at[lag], corr_out.at[lag])
+
     span = per_line * block
     fresh = bundle_weights(place, dz, tiles[-1:], bins_ref, lag_ref, turned_ref, per_line - 1)
     for at, old_ref in enumerate(old_weights[:-1]):
@@ -244,18 +265,10 @@
                 imag_sum += imag * cosine - real * sine
         grad_ref[:, cols] = real_sum * norm
         grad_ref[:, high] = imag_sum * norm
-
-    pick_step(place, dz, tiles, table_ref, staged_ref, picked_ref)
-    corr_step(place, dz, lines, picked_ref, part_ref)
-    here = place.inside(dz)
-    wide = PAIR * block
-    for lag in range(LAGS):
-        cols = slice(lag * wide, (lag + 1) * wide)
-        halves = []
-        for half in range(part_ref.shape[0]):
-            fresh = here & (place.half(dz) == half)
-            halves.append(jnp.where(fresh, part_ref[half, :, cols], old_part_ref[half, :, cols]))
-        corr_ref[lag] = jnp.concatenate(halves, axis=1) * norm
+        write(grad_ref.at[:, cols], grad_out.at[:, cols])
+        write(grad_ref.at[:, high], grad_out.at[:, high])
+    for copy in copies:
+        copy.wait()
 
 
 def per_device(spectra, band_weights, lag_weights, selected_bins):
@@ -283,13 +296,13 @@
     def send_line(value, step):
         return send(value, lambda r, z, k: (r, z ^ step, k))
 
-    def call(kernel, outs, operands, specs, **more):
+    def call(kernel, outs, operands, specs, out_space=vmem, **more):
         held = sum(x.size * x.dtype.itemsize for x in [*operands, *jax.tree.leaves(outs)])
         return pl.pallas_call(
             kernel,
             out_shape=outs,
             in_specs=specs,
-            out_specs=jax.tree.map(lambda _: vmem, outs),
+            out_specs=jax.tree.map(lambda _: out_space, outs),
             compiler_params=pltpu.CompilerParams(vmem_limit_bytes=min(held + (12 << 20), 60 << 20)),
             **more,
         )(*operands)
@@ -374,7 +387,11 @@
             staged,
             pltpu.VMEM(picked_shape.shape, picked_shape.dtype),
             pltpu.VMEM(part_shape, jnp.float32),
+            pltpu.VMEM((LAGS, n_row, n_col), jnp.float32),
+            pltpu.VMEM((block, width), jnp.float32),
+            pltpu.SemaphoreType.DMA((LAGS + 2 * (freqs // CHUNK),)),
         ],
+        out_space=pl.BlockSpec(memory_space=pltpu.HBM),
     )
     return correlations, gradient
 

time: 69.7 us -> 69.5 us (level)
  no operation moved by 1% of the time
where the time goes in v5:
time: 69.5 us; the launch traced here: 69.3 us
  waiting for transfers between devices  32.9 us (47%)
  starting transfers between devices  20.2 us (29%)
  Pallas kernels  13 us (19%)
  local copies, waits for them, and re-layouts  2.42 us (3%)
  between operations  0.8 us (1%)
    ppermute x31, waiting for transfers between devices, send(): return lax.ppermute(value, ('rows', 'cols'), pairs)  32.9 us
    ppermute x31, starting transfers between devices, send(): return lax.ppermute(value, ('rows', 'cols'), pairs)  20.2 us
    pallas_call x8, Pallas kernels, call(): pl.pallas_call(kernel, out_shape=outs, in_specs=specs, out_specs=jax.tree...  13 us
    unnamed x12, local copies, waits for them, and re-layouts  2.42 us
  transfers between devices with their start and end apart: 31, of which 10 were waited for; matrix products, arithmetic and copies ran while one was open for 0% of the time, Pallas kernels for 12%

profile of v5, /device:TPU:0, one launch (start us, length us, event | category | flops | bytes accessed | tf_op | source)
XLA Modules:
  0.0 69.3 jit_solution(481677972978221274)
XLA Ops:
  0.7 1.0 %copy-done.2 = bf16[32,4096]{1,0:T(8,128)(2,1)S(1)} copy-done((bf16[32,4096]{1,0:T(8,128)(2,1)S(1)}, bf16[32,4096]{1,0:T(8,128)(2,1)}, u32[]{:S(2)}) %copy-start.2) | copy-done | bytes 262168
  1.6 0.7 %copy-done.5 = f32[2048]{0:T(1024)S(1)} copy-done((f32[2048]{0:T(1024)S(1)}, f32[2048]{0:T(1024)}, u32[]{:S(2)}) %copy-start.5) | copy-done | bytes 8216
  2.5 3.0 %collective-permute-start = (bf16[32,4096]{1,0:T(8,128)(2,1)S(1)}, bf16[32,4096]{1,0:T(8,128)(2,1)S(1)}, u32[]{:S(2)}, u32[]{:S(2)}) collective-permute-start(bf16[32,4096]{1,0:T(8,128)(2,1)S(1)} %shard_map.68.own_ref.refs_0_), channel_id=1, source_target_pairs={{0,8},{1,17},{2,10},{3,19},{4,12},{5,21},{6,14},{7,23},{8,0},{9,25... | collective-permute-start | bytes 786440 | tf_op jit(solution)/shard_map/ppermute | solution.py:291
  5.6 1.6 %collective-permute-start.7 = (bf16[32,4096]{1,0:T(8,128)(2,1)S(1)}, bf16[32,4096]{1,0:T(8,128)(2,1)S(1)}, u32[]{:S(2)}, u32[]{:S(2)}) collective-permute-start(bf16[32,4096]{1,0:T(8,128)(2,1)S(1)} %shard_map.68.own_ref.refs_0_), channel_id=1, source_target_pairs={{0,2},{1,3},{2,0},{3,1},{4,6},{5,7},{6,4},{7,5},{8,10},{9,11},{10,... | collective-permute-start | bytes 786440 | tf_op jit(solution)/shard_map/ppermute | solution.py:291
  7.1 2.6 %collective-permute-start.15 = (bf16[32,4096]{1,0:T(8,128)(2,1)S(1)}, bf16[32,4096]{1,0:T(8,128)(2,1)S(1)}, u32[]{:S(2)}, u32[]{:S(2)}) collective-permute-start(bf16[32,4096]{1,0:T(8,128)(2,1)S(1)} %shard_map.68.own_ref.refs_0_), channel_id=1, source_target_pairs={{0,4},{1,5},{2,6},{3,7},{4,0},{5,1},{6,2},{7,3},{8,12},{9,13},{10,... | collective-permute-start | bytes 786440 | tf_op jit(solution)/shard_map/ppermute | solution.py:291
  9.7 1.5 %collective-permute-start.1 = (bf16[32,4096]{1,0:T(8,128)(2,1)S(1)}, bf16[32,4096]{1,0:T(8,128)(2,1)S(1)}, u32[]{:S(2)}, u32[]{:S(2)}) collective-permute-start(bf16[32,4096]{1,0:T(8,128)(2,1)S(1)} %shard_map.68.own_ref.refs_0_), channel_id=1, source_target_pairs={{0,16},{1,9},{2,18},{3,11},{4,20},{5,13},{6,22},{7,15},{8,24},{9,1... | collective-permute-start | bytes 786440 | tf_op jit(solution)/shard_map/ppermute | solution.py:291
  11.3 0.8 %collective-permute-start.2 = (bf16[32,4096]{1,0:T(8,128)(2,1)S(1)}, bf16[32,4096]{1,0:T(8,128)(2,1)S(1)}, u32[]{:S(2)}, u32[]{:S(2)}) collective-permute-start(bf16[32,4096]{1,0:T(8,128)(2,1)S(1)} %collective-permute-done.refs_1_), channel_id=1, source_target_pairs={{0,16},{1,9},{2,18},{3,11},{4,20},{5,13},{6,22},{7,15},{8,24},{9,1... | collective-permute-start | bytes 786440 | tf_op jit(solution)/shard_map/ppermute | solution.py:291
  12.1 6.8 %collective-permute-done.7.refs_0_.refs_2_.refs_8_ = bf16[32,4096]{1,0:T(8,128)(2,1)S(1)} collective-permute-done((bf16[32,4096]{1,0:T(8,128)(2,1)S(1)}, bf16[32,4096]{1,0:T(8,128)(2,1)S(1)}, u32[]{:S(2)}, u32[]{:S(2)}) %collective-permute-start.7) | collective-permute-done | bytes 262176 | tf_op jit(solution)/shard_map/ppermute | solution.py:291
  18.9 1.5 %collective-permute-start.8 = (bf16[32,4096]{1,0:T(8,128)(2,1)S(1)}, bf16[32,4096]{1,0:T(8,128)(2,1)S(1)}, u32[]{:S(2)}, u32[]{:S(2)}) collective-permute-start(bf16[32,4096]{1,0:T(8,128)(2,1)S(1)} %collective-permute-done.7.refs_0_.refs_2_.refs_8_), channel_id=1, source_target_pairs={{0,8},{1,17},{2,10},{3,19},{4,12},{5,21},{6,14},{7,23},{8,0},{9,25... | collective-permute-start | bytes 786440 | tf_op jit(solution)/shard_map/ppermute | solution.py:291
  20.3 0.9 %collective-permute-done.15.refs_0_.refs_4_.refs_16_ = bf16[32,4096]{1,0:T(8,128)(2,1)S(1)} collective-permute-done((bf16[32,4096]{1,0:T(8,128)(2,1)S(1)}, bf16[32,4096]{1,0:T(8,128)(2,1)S(1)}, u32[]{:S(2)}, u32[]{:S(2)}) %collective-permute-start.15) | collective-permute-done | bytes 262176 | tf_op jit(solution)/shard_map/ppermute | solution.py:291
  21.7 1.6 %collective-permute-start.16 = (bf16[32,4096]{1,0:T(8,128)(2,1)S(1)}, bf16[32,4096]{1,0:T(8,128)(2,1)S(1)}, u32[]{:S(2)}, u32[]{:S(2)}) collective-permute-start(bf16[32,4096]{1,0:T(8,128)(2,1)S(1)} %collective-permute-done.15.refs_0_.refs_4_.refs_16_), channel_id=1, source_target_pairs={{0,8},{1,17},{2,10},{3,19},{4,12},{5,21},{6,14},{7,23},{8,0},{9,25... | collective-permute-start | bytes 786440 | tf_op jit(solution)/shard_map/ppermute | solution.py:291
  23.3 1.5 %collective-permute-start.17 = (bf16[32,4096]{1,0:T(8,128)(2,1)S(1)}, bf16[32,4096]{1,0:T(8,128)(2,1)S(1)}, u32[]{:S(2)}, u32[]{:S(2)}) collective-permute-start(bf16[32,4096]{1,0:T(8,128)(2,1)S(1)} %collective-permute-done.15.refs_0_.refs_4_.refs_16_), channel_id=1, source_target_pairs={{0,16},{1,9},{2,18},{3,11},{4,20},{5,13},{6,22},{7,15},{8,24},{9,1... | collective-permute-start | bytes 786440 | tf_op jit(solution)/shard_map/ppermute | solution.py:291
  24.8 3.0 %collective-permute-done.8.refs_1_.refs_9_ = bf16[32,4096]{1,0:T(8,128)(2,1)S(1)} collective-permute-done((bf16[32,4096]{1,0:T(8,128)(2,1)S(1)}, bf16[32,4096]{1,0:T(8,128)(2,1)S(1)}, u32[]{:S(2)}, u32[]{:S(2)}) %collective-permute-start.8) | collective-permute-done | bytes 262176 | tf_op jit(solution)/shard_map/ppermute | solution.py:291
  27.8 2.6 %collective-permute-done.9.refs_2_.refs_10_ = bf16[32,4096]{1,0:T(8,128)(2,1)S(1)} collective-permute-done((bf16[32,4096]{1,0:T(8,128)(2,1)S(1)}, bf16[32,4096]{1,0:T(8,128)(2,1)S(1)}, u32[]{:S(2)}, u32[]{:S(2)}) %collective-permute-start.9) | collective-permute-done | bytes 262176 | tf_op jit(solution)/shard_map/ppermute | solution.py:291
  30.8 1.7 %collective-permute-done.16.refs_1_.refs_17_ = bf16[32,4096]{1,0:T(8,128)(2,1)S(1)} collective-permute-done((bf16[32,4096]{1,0:T(8,128)(2,1)S(1)}, bf16[32,4096]{1,0:T(8,128)(2,1)S(1)}, u32[]{:S(2)}, u32[]{:S(2)}) %collective-permute-start.16) | collective-permute-done | bytes 262176 | tf_op jit(solution)/shard_map/ppermute | solution.py:291
  32.5 0.7 collective-permute-done.17.refs_2_.refs_18_
  33.2 0.5 collective-permute-start.13
  33.7 0.5 collective-permute-start.18
  34.3 5.3 %collective-permute-done.23.refs_0_.refs_6_.refs_24_ = bf16[32,4096]{1,0:T(8,128)(2,1)S(1)} collective-permute-done((bf16[32,4096]{1,0:T(8,128)(2,1)S(1)}, bf16[32,4096]{1,0:T(8,128)(2,1)S(1)}, u32[]{:S(2)}, u32[]{:S(2)}) %collective-permute-start.23) | collective-permute-done | bytes 262176 | tf_op jit(solution)/shard_map/ppermute | solution.py:291
  39.5 5.2 %collective-permute-done.10.refs_3_.refs_11_ = bf16[32,4096]{1,0:T(8,128)(2,1)S(1)} collective-permute-done((bf16[32,4096]{1,0:T(8,128)(2,1)S(1)}, bf16[32,4096]{1,0:T(8,128)(2,1)S(1)}, u32[]{:S(2)}, u32[]{:S(2)}) %collective-permute-start.10) | collective-permute-done | bytes 262176 | tf_op jit(solution)/shard_map/ppermute | solution.py:291
  44.7 1.5 %collective-permute-start.24 = (bf16[32,4096]{1,0:T(8,128)(2,1)S(1)}, bf16[32,4096]{1,0:T(8,128)(2,1)S(1)}, u32[]{:S(2)}, u32[]{:S(2)}) collective-permute-start(bf16[32,4096]{1,0:T(8,128)(2,1)S(1)} %collective-permute-done.23.refs_0_.refs_6_.refs_24_), channel_id=1, source_target_pairs={{0,8},{1,17},{2,10},{3,19},{4,12},{5,21},{6,14},{7,23},{8,0},{9,25... | collective-permute-start | bytes 786440 | tf_op jit(solution)/shard_map/ppermute | solution.py:291
  47.2 5.3 %collective-permute-done.24.refs_1_.refs_25_ = bf16[32,4096]{1,0:T(8,128)(2,1)S(1)} collective-permute-done((bf16[32,4096]{1,0:T(8,128)(2,1)S(1)}, bf16[32,4096]{1,0:T(8,128)(2,1)S(1)}, u32[]{:S(2)}, u32[]{:S(2)}) %collective-permute-start.24) | collective-permute-done | bytes 262176 | tf_op jit(solution)/shard_map/ppermute | solution.py:291
  52.6 0.5 collective-permute-start.29
  53.6 1.5 %collective-permute-done.26.refs_3_.refs_27_ = bf16[32,4096]{1,0:T(8,128)(2,1)S(1)} collective-permute-done((bf16[32,4096]{1,0:T(8,128)(2,1)S(1)}, bf16[32,4096]{1,0:T(8,128)(2,1)S(1)}, u32[]{:S(2)}, u32[]{:S(2)}) %collective-permute-start.26) | collective-permute-done | bytes 262176 | tf_op jit(solution)/shard_map/ppermute | solution.py:291
  55.1 0.5 collective-permute-start.22
  55.7 0.8 %copy-done = f32[4,2048]{1,0:T(4,128)S(1)} copy-done((f32[4,2048]{1,0:T(4,128)S(1)}, f32[4,2048]{1,0:T(4,128)}, u32[]{:S(2)}) %copy-start) | copy-done | bytes 32792
  56.8 2.1 %shard_map.70 = (bf16[160,256]{1,0:T(8,128)(2,1)S(1)}, bf16[256,4096]{1,0:T(8,128)(2,1)S(1)}) custom-call(s32[8]{0:T(128)S(1)} %copy-done.3, f32[4]{0:T(128)S(1)} %copy-done.4, f32[4,2048]{1,0:T(4,128)S(1)} %copy-done, bf16[160,4096]{1,0:T(8,128)(2,1)S(1)} %shard_map.69.turned_ref, bf16[32,4096]{1,0:T(8,128)(2,1)S(1)} %shard_map.68.own_ref.refs_0_, ...), custom_call_target="tpu_custom_call" | custom-call | tf_op jit(solution)/shard_map/pallas_call | solution.py:301
  58.8 1.3 %shard_map.73.refs_35_ = bf16[160,224]{1,0:T(8,128)(2,1)S(1)} custom-call(s32[8]{0:T(128)S(1)} %copy-done.3, f32[4]{0:T(128)S(1)} %copy-done.4, bf16[160,4096]{1,0:T(8,128)(2,1)S(1)} %shard_map.69.turned_ref, bf16[32,4096]{1,0:T(8,128)(2,1)S(1)} %collective-permute-done.23.refs_0_.refs_6_.refs_24_, ...), custom_call_target="tpu_custom_call" | custom-call | tf_op jit(solution)/shard_map/pallas_call | solution.py:301
  60.1 2.1 %shard_map.71 = (bf16[160,256]{1,0:T(8,128)(2,1)S(1)}, bf16[256,4096]{1,0:T(8,128)(2,1)S(1)}) custom-call(s32[8]{0:T(128)S(1)} %copy-done.3, f32[4]{0:T(128)S(1)} %copy-done.4, f32[4,2048]{1,0:T(4,128)S(1)} %copy-done, bf16[160,4096]{1,0:T(8,128)(2,1)S(1)} %shard_map.69.turned_ref, bf16[32,4096]{1,0:T(8,128)(2,1)S(1)} %collective-permute-done.7.refs_0_.refs_2_.refs_8_, ...), custom_call_target="tpu_custom_call" | custom-call | tf_op jit(solution)/shard_map/pallas_call | solution.py:301
  62.2 1.4 %shard_map.72 = (bf16[160,256]{1,0:T(8,128)(2,1)S(1)}, bf16[256,4096]{1,0:T(8,128)(2,1)S(1)}) custom-call(s32[8]{0:T(128)S(1)} %copy-done.3, f32[4]{0:T(128)S(1)} %copy-done.4, f32[4,2048]{1,0:T(4,128)S(1)} %copy-done, bf16[160,4096]{1,0:T(8,128)(2,1)S(1)} %shard_map.69.turned_ref, bf16[32,4096]{1,0:T(8,128)(2,1)S(1)} %collective-permute-done.15.refs_0_.refs_4_.refs_16_, ...), custom_call_target="tpu_custom_call" | custom-call | tf_op jit(solution)/shard_map/pallas_call | solution.py:301
  63.6 1.5 %shard_map.74.refs_36_ = f32[2,256,256]{2,1,0:T(8,128)S(1)} custom-call(bf16[32,4096]{1,0:T(8,128)(2,1)S(1)} %shard_map.68.own_ref.refs_0_, bf16[32,4096]{1,0:T(8,128)(2,1)S(1)} %collective-permute-done.3.refs_4_.refs_1_, bf16[32,4096]{1,0:T(8,128)(2,1)S(1)} %collective-permute-done.7.refs_0_.refs_2_.refs_8_, ...), custom_call_target="tpu_custom_call" | custom-call | tf_op jit(solution)/shard_map/pallas_call | solution.py:301
  65.2 4.1 %shard_map.75 = (f32[4,256,128]{2,1,0:T(8,128)}, f32[32,4096]{1,0:T(8,128)}) custom-call(s32[8]{0:T(128)S(1)} %copy-done.3, f32[4]{0:T(128)S(1)} %copy-done.4, f32[4,2048]{1,0:T(4,128)S(1)} %copy-done.1, bf16[160,4096]{1,0:T(8,128)(2,1)S(1)} %shard_map.69.turned_ref, bf16[32,4096]{1,0:T(8,128)(2,1)S(1)} %shard_map.68.own_ref.refs_0_, ...), custom_call_target="tpu_custom_call" | custom-call | tf_op jit(solution)/shard_map/pallas_call | solution.py:301
  (50 shorter events, 3.2 us)
Async XLA Ops:
  0.6 56.1 %copy-start.4 = (f32[4]{0:T(128)S(1)}, f32[4]{0:T(128)}, u32[]{:S(2)}) copy-start(f32[4]{0:T(128)} %lag_ref.9) | copy-start | bytes 52
  2.5 8.7 %collective-permute-start = (bf16[32,4096]{1,0:T(8,128)(2,1)S(1)}, bf16[32,4096]{1,0:T(8,128)(2,1)S(1)}, u32[]{:S(2)}, u32[]{:S(2)}) collective-permute-start(bf16[32,4096]{1,0:T(8,128)(2,1)S(1)} %shard_map.68.own_ref.refs_0_), channel_id=1, source_target_pairs={{0,8},{1,17},{2,10},{3,19},{4,12},{5,21},{6,14},{7,23},{8,0},{9,25... | collective-permute-start | bytes 786440 | tf_op jit(solution)/shard_map/ppermute | solution.py:291
  5.6 13.3 %collective-permute-start.7 = (bf16[32,4096]{1,0:T(8,128)(2,1)S(1)}, bf16[32,4096]{1,0:T(8,128)(2,1)S(1)}, u32[]{:S(2)}, u32[]{:S(2)}) collective-permute-start(bf16[32,4096]{1,0:T(8,128)(2,1)S(1)} %shard_map.68.own_ref.refs_0_), channel_id=1, source_target_pairs={{0,2},{1,3},{2,0},{3,1},{4,6},{5,7},{6,4},{7,5},{8,10},{9,11},{10,... | collective-permute-start | bytes 786440 | tf_op jit(solution)/shard_map/ppermute | solution.py:291
  7.1 14.1 %collective-permute-start.15 = (bf16[32,4096]{1,0:T(8,128)(2,1)S(1)}, bf16[32,4096]{1,0:T(8,128)(2,1)S(1)}, u32[]{:S(2)}, u32[]{:S(2)}) collective-permute-start(bf16[32,4096]{1,0:T(8,128)(2,1)S(1)} %shard_map.68.own_ref.refs_0_), channel_id=1, source_target_pairs={{0,4},{1,5},{2,6},{3,7},{4,0},{5,1},{6,2},{7,3},{8,12},{9,13},{10,... | collective-permute-start | bytes 786440 | tf_op jit(solution)/shard_map/ppermute | solution.py:291
  9.7 12.0 %collective-permute-start.1 = (bf16[32,4096]{1,0:T(8,128)(2,1)S(1)}, bf16[32,4096]{1,0:T(8,128)(2,1)S(1)}, u32[]{:S(2)}, u32[]{:S(2)}) collective-permute-start(bf16[32,4096]{1,0:T(8,128)(2,1)S(1)} %shard_map.68.own_ref.refs_0_), channel_id=1, source_target_pairs={{0,16},{1,9},{2,18},{3,11},{4,20},{5,13},{6,22},{7,15},{8,24},{9,1... | collective-permute-start | bytes 786440 | tf_op jit(solution)/shard_map/ppermute | solution.py:291
  11.2 10.5 %collective-permute-start.3 = (bf16[32,4096]{1,0:T(8,128)(2,1)S(1)}, bf16[32,4096]{1,0:T(8,128)(2,1)S(1)}, u32[]{:S(2)}, u32[]{:S(2)}) collective-permute-start(bf16[32,4096]{1,0:T(8,128)(2,1)S(1)} %shard_map.68.own_ref.refs_0_), channel_id=1, source_target_pairs={{0,1},{1,0},{2,3},{3,2},{4,5},{5,4},{6,7},{7,6},{8,9},{9,8},{10,11... | collective-permute-start | bytes 786440 | tf_op jit(solution)/shard_map/ppermute | solution.py:291
  11.3 12.0 %collective-permute-start.2 = (bf16[32,4096]{1,0:T(8,128)(2,1)S(1)}, bf16[32,4096]{1,0:T(8,128)(2,1)S(1)}, u32[]{:S(2)}, u32[]{:S(2)}) collective-permute-start(bf16[32,4096]{1,0:T(8,128)(2,1)S(1)} %collective-permute-done.refs_1_), channel_id=1, source_target_pairs={{0,16},{1,9},{2,18},{3,11},{4,20},{5,13},{6,22},{7,15},{8,24},{9,1... | collective-permute-start | bytes 786440 | tf_op jit(solution)/shard_map/ppermute | solution.py:291
  18.9 8.9 %collective-permute-start.8 = (bf16[32,4096]{1,0:T(8,128)(2,1)S(1)}, bf16[32,4096]{1,0:T(8,128)(2,1)S(1)}, u32[]{:S(2)}, u32[]{:S(2)}) collective-permute-start(bf16[32,4096]{1,0:T(8,128)(2,1)S(1)} %collective-permute-done.7.refs_0_.refs_2_.refs_8_), channel_id=1, source_target_pairs={{0,8},{1,17},{2,10},{3,19},{4,12},{5,21},{6,14},{7,23},{8,0},{9,25... | collective-permute-start | bytes 786440 | tf_op jit(solution)/shard_map/ppermute | solution.py:291
  21.2 9.1 %collective-permute-start.9 = (bf16[32,4096]{1,0:T(8,128)(2,1)S(1)}, bf16[32,4096]{1,0:T(8,128)(2,1)S(1)}, u32[]{:S(2)}, u32[]{:S(2)}) collective-permute-start(bf16[32,4096]{1,0:T(8,128)(2,1)S(1)} %collective-permute-done.7.refs_0_.refs_2_.refs_8_), channel_id=1, source_target_pairs={{0,16},{1,9},{2,18},{3,11},{4,20},{5,13},{6,22},{7,15},{8,24},{9,1... | collective-permute-start | bytes 786440 | tf_op jit(solution)/shard_map/ppermute | solution.py:291
  21.7 8.6 %collective-permute-start.11 = (bf16[32,4096]{1,0:T(8,128)(2,1)S(1)}, bf16[32,4096]{1,0:T(8,128)(2,1)S(1)}, u32[]{:S(2)}, u32[]{:S(2)}) collective-permute-start(bf16[32,4096]{1,0:T(8,128)(2,1)S(1)} %collective-permute-done.7.refs_0_.refs_2_.refs_8_), channel_id=1, source_target_pairs={{0,1},{1,0},{2,3},{3,2},{4,5},{5,4},{6,7},{7,6},{8,9},{9,8},{10,11... | collective-permute-start | bytes 786440 | tf_op jit(solution)/shard_map/ppermute | solution.py:291
  21.7 10.8 %collective-permute-start.16 = (bf16[32,4096]{1,0:T(8,128)(2,1)S(1)}, bf16[32,4096]{1,0:T(8,128)(2,1)S(1)}, u32[]{:S(2)}, u32[]{:S(2)}) collective-permute-start(bf16[32,4096]{1,0:T(8,128)(2,1)S(1)} %collective-permute-done.15.refs_0_.refs_4_.refs_16_), channel_id=1, source_target_pairs={{0,8},{1,17},{2,10},{3,19},{4,12},{5,21},{6,14},{7,23},{8,0},{9,25... | collective-permute-start | bytes 786440 | tf_op jit(solution)/shard_map/ppermute | solution.py:291
  23.3 9.9 %collective-permute-start.17 = (bf16[32,4096]{1,0:T(8,128)(2,1)S(1)}, bf16[32,4096]{1,0:T(8,128)(2,1)S(1)}, u32[]{:S(2)}, u32[]{:S(2)}) collective-permute-start(bf16[32,4096]{1,0:T(8,128)(2,1)S(1)} %collective-permute-done.15.refs_0_.refs_4_.refs_16_), channel_id=1, source_target_pairs={{0,16},{1,9},{2,18},{3,11},{4,20},{5,13},{6,22},{7,15},{8,24},{9,1... | collective-permute-start | bytes 786440 | tf_op jit(solution)/shard_map/ppermute | solution.py:291
  27.8 5.4 %collective-permute-start.4 = (bf16[32,4096]{1,0:T(8,128)(2,1)S(1)}, bf16[32,4096]{1,0:T(8,128)(2,1)S(1)}, u32[]{:S(2)}, u32[]{:S(2)}) collective-permute-start(bf16[32,4096]{1,0:T(8,128)(2,1)S(1)} %collective-permute-done.refs_1_), channel_id=1, source_target_pairs={{0,1},{1,0},{2,3},{3,2},{4,5},{5,4},{6,7},{7,6},{8,9},{9,8},{10,11... | collective-permute-start | bytes 786440 | tf_op jit(solution)/shard_map/ppermute | solution.py:291
  30.3 3.4 %collective-permute-start.5 = (bf16[32,4096]{1,0:T(8,128)(2,1)S(1)}, bf16[32,4096]{1,0:T(8,128)(2,1)S(1)}, u32[]{:S(2)}, u32[]{:S(2)}) collective-permute-start(bf16[32,4096]{1,0:T(8,128)(2,1)S(1)} %collective-permute-done.1.refs_2_), channel_id=1, source_target_pairs={{0,1},{1,0},{2,3},{3,2},{4,5},{5,4},{6,7},{7,6},{8,9},{9,8},{10,11... | collective-permute-start | bytes 786440 | tf_op jit(solution)/shard_map/ppermute | solution.py:291
  30.3 9.2 %collective-permute-start.23 = (bf16[32,4096]{1,0:T(8,128)(2,1)S(1)}, bf16[32,4096]{1,0:T(8,128)(2,1)S(1)}, u32[]{:S(2)}, u32[]{:S(2)}) collective-permute-start(bf16[32,4096]{1,0:T(8,128)(2,1)S(1)} %collective-permute-done.15.refs_0_.refs_4_.refs_16_), channel_id=1, source_target_pairs={{0,2},{1,3},{2,0},{3,1},{4,6},{5,7},{6,4},{7,5},{8,10},{9,11},{10,... | collective-permute-start | bytes 786440 | tf_op jit(solution)/shard_map/ppermute | solution.py:291
  32.5 12.1 %collective-permute-start.10 = (bf16[32,4096]{1,0:T(8,128)(2,1)S(1)}, bf16[32,4096]{1,0:T(8,128)(2,1)S(1)}, u32[]{:S(2)}, u32[]{:S(2)}) collective-permute-start(bf16[32,4096]{1,0:T(8,128)(2,1)S(1)} %collective-permute-done.2.refs_3_), channel_id=1, source_target_pairs={{0,2},{1,3},{2,0},{3,1},{4,6},{5,7},{6,4},{7,5},{8,10},{9,11},{10,... | collective-permute-start | bytes 786440 | tf_op jit(solution)/shard_map/ppermute | solution.py:291
  33.2 13.0 %collective-permute-start.12 = (bf16[32,4096]{1,0:T(8,128)(2,1)S(1)}, bf16[32,4096]{1,0:T(8,128)(2,1)S(1)}, u32[]{:S(2)}, u32[]{:S(2)}) collective-permute-start(bf16[32,4096]{1,0:T(8,128)(2,1)S(1)} %collective-permute-done.8.refs_1_.refs_9_), channel_id=1, source_target_pairs={{0,1},{1,0},{2,3},{3,2},{4,5},{5,4},{6,7},{7,6},{8,9},{9,8},{10,11... | collective-permute-start | bytes 786440 | tf_op jit(solution)/shard_map/ppermute | solution.py:291
  33.2 13.0 %collective-permute-start.13 = (bf16[32,4096]{1,0:T(8,128)(2,1)S(1)}, bf16[32,4096]{1,0:T(8,128)(2,1)S(1)}, u32[]{:S(2)}, u32[]{:S(2)}) collective-permute-start(bf16[32,4096]{1,0:T(8,128)(2,1)S(1)} %collective-permute-done.9.refs_2_.refs_10_), channel_id=1, source_target_pairs={{0,1},{1,0},{2,3},{3,2},{4,5},{5,4},{6,7},{7,6},{8,9},{9,8},{10,11... | collective-permute-start | bytes 786440 | tf_op jit(solution)/shard_map/ppermute | solution.py:291
  33.7 12.5 %collective-permute-start.18 = (bf16[32,4096]{1,0:T(8,128)(2,1)S(1)}, bf16[32,4096]{1,0:T(8,128)(2,1)S(1)}, u32[]{:S(2)}, u32[]{:S(2)}) collective-permute-start(bf16[32,4096]{1,0:T(8,128)(2,1)S(1)} %collective-permute-done.16.refs_1_.refs_17_), channel_id=1, source_target_pairs={{0,16},{1,9},{2,18},{3,11},{4,20},{5,13},{6,22},{7,15},{8,24},{9,1... | collective-permute-start | bytes 786440 | tf_op jit(solution)/shard_map/ppermute | solution.py:291
  39.5 7.2 %collective-permute-start.6 = (bf16[32,4096]{1,0:T(8,128)(2,1)S(1)}, bf16[32,4096]{1,0:T(8,128)(2,1)S(1)}, u32[]{:S(2)}, u32[]{:S(2)}) collective-permute-start(bf16[32,4096]{1,0:T(8,128)(2,1)S(1)} %collective-permute-done.2.refs_3_), channel_id=1, source_target_pairs={{0,1},{1,0},{2,3},{3,2},{4,5},{5,4},{6,7},{7,6},{8,9},{9,8},{10,11... | collective-permute-start | bytes 786440 | tf_op jit(solution)/shard_map/ppermute | solution.py:291
  44.7 7.9 %collective-permute-start.24 = (bf16[32,4096]{1,0:T(8,128)(2,1)S(1)}, bf16[32,4096]{1,0:T(8,128)(2,1)S(1)}, u32[]{:S(2)}, u32[]{:S(2)}) collective-permute-start(bf16[32,4096]{1,0:T(8,128)(2,1)S(1)} %collective-permute-done.23.refs_0_.refs_6_.refs_24_), channel_id=1, source_target_pairs={{0,8},{1,17},{2,10},{3,19},{4,12},{5,21},{6,14},{7,23},{8,0},{9,25... | collective-permute-start | bytes 786440 | tf_op jit(solution)/shard_map/ppermute | solution.py:291
  46.2 6.4 %collective-permute-start.25 = (bf16[32,4096]{1,0:T(8,128)(2,1)S(1)}, bf16[32,4096]{1,0:T(8,128)(2,1)S(1)}, u32[]{:S(2)}, u32[]{:S(2)}) collective-permute-start(bf16[32,4096]{1,0:T(8,128)(2,1)S(1)} %collective-permute-done.23.refs_0_.refs_6_.refs_24_), channel_id=1, source_target_pairs={{0,16},{1,9},{2,18},{3,11},{4,20},{5,13},{6,22},{7,15},{8,24},{9,1... | collective-permute-start | bytes 786440 | tf_op jit(solution)/shard_map/ppermute | solution.py:291
  46.2 6.9 %collective-permute-start.27 = (bf16[32,4096]{1,0:T(8,128)(2,1)S(1)}, bf16[32,4096]{1,0:T(8,128)(2,1)S(1)}, u32[]{:S(2)}, u32[]{:S(2)}) collective-permute-start(bf16[32,4096]{1,0:T(8,128)(2,1)S(1)} %collective-permute-done.23.refs_0_.refs_6_.refs_24_), channel_id=1, source_target_pairs={{0,1},{1,0},{2,3},{3,2},{4,5},{5,4},{6,7},{7,6},{8,9},{9,8},{10,11... | collective-permute-start | bytes 786440 | tf_op jit(solution)/shard_map/ppermute | solution.py:291
  46.3 6.9 %collective-permute-start.14 = (bf16[32,4096]{1,0:T(8,128)(2,1)S(1)}, bf16[32,4096]{1,0:T(8,128)(2,1)S(1)}, u32[]{:S(2)}, u32[]{:S(2)}) collective-permute-start(bf16[32,4096]{1,0:T(8,128)(2,1)S(1)} %collective-permute-done.10.refs_3_.refs_11_), channel_id=1, source_target_pairs={{0,1},{1,0},{2,3},{3,2},{4,5},{5,4},{6,7},{7,6},{8,9},{9,8},{10,11... | collective-permute-start | bytes 786440 | tf_op jit(solution)/shard_map/ppermute | solution.py:291
  46.8 8.3 %collective-permute-start.26 = (bf16[32,4096]{1,0:T(8,128)(2,1)S(1)}, bf16[32,4096]{1,0:T(8,128)(2,1)S(1)}, u32[]{:S(2)}, u32[]{:S(2)}) collective-permute-start(bf16[32,4096]{1,0:T(8,128)(2,1)S(1)} %collective-permute-done.18.refs_3_.refs_19_), channel_id=1, source_target_pairs={{0,2},{1,3},{2,0},{3,1},{4,6},{5,7},{6,4},{7,5},{8,10},{9,11},{10,... | collective-permute-start | bytes 786440 | tf_op jit(solution)/shard_map/ppermute | solution.py:291
  52.6 2.5 %collective-permute-start.28 = (bf16[32,4096]{1,0:T(8,128)(2,1)S(1)}, bf16[32,4096]{1,0:T(8,128)(2,1)S(1)}, u32[]{:S(2)}, u32[]{:S(2)}) collective-permute-start(bf16[32,4096]{1,0:T(8,128)(2,1)S(1)} %collective-permute-done.24.refs_1_.refs_25_), channel_id=1, source_target_pairs={{0,1},{1,0},{2,3},{3,2},{4,5},{5,4},{6,7},{7,6},{8,9},{9,8},{10,11... | collective-permute-start | bytes 786440 | tf_op jit(solution)/shard_map/ppermute | solution.py:291
  52.6 3.0 %collective-permute-start.29 = (bf16[32,4096]{1,0:T(8,128)(2,1)S(1)}, bf16[32,4096]{1,0:T(8,128)(2,1)S(1)}, u32[]{:S(2)}, u32[]{:S(2)}) collective-permute-start(bf16[32,4096]{1,0:T(8,128)(2,1)S(1)} %collective-permute-done.25.refs_2_.refs_26_), channel_id=1, source_target_pairs={{0,1},{1,0},{2,3},{3,2},{4,5},{5,4},{6,7},{7,6},{8,9},{9,8},{10,11... | collective-permute-start | bytes 786440 | tf_op jit(solution)/shard_map/ppermute | solution.py:291
  53.1 9.1 %collective-permute-start.19 = (bf16[32,4096]{1,0:T(8,128)(2,1)S(1)}, bf16[32,4096]{1,0:T(8,128)(2,1)S(1)}, u32[]{:S(2)}, u32[]{:S(2)}) collective-permute-start(bf16[32,4096]{1,0:T(8,128)(2,1)S(1)} %collective-permute-done.15.refs_0_.refs_4_.refs_16_), channel_id=1, source_target_pairs={{0,1},{1,0},{2,3},{3,2},{4,5},{5,4},{6,7},{7,6},{8,9},{9,8},{10,11... | collective-permute-start | bytes 786440 | tf_op jit(solution)/shard_map/ppermute | solution.py:291
  53.1 9.1 %collective-permute-start.20 = (bf16[32,4096]{1,0:T(8,128)(2,1)S(1)}, bf16[32,4096]{1,0:T(8,128)(2,1)S(1)}, u32[]{:S(2)}, u32[]{:S(2)}) collective-permute-start(bf16[32,4096]{1,0:T(8,128)(2,1)S(1)} %collective-permute-done.16.refs_1_.refs_17_), channel_id=1, source_target_pairs={{0,1},{1,0},{2,3},{3,2},{4,5},{5,4},{6,7},{7,6},{8,9},{9,8},{10,11... | collective-permute-start | bytes 786440 | tf_op jit(solution)/shard_map/ppermute | solution.py:291
  55.1 7.1 %collective-permute-start.21 = (bf16[32,4096]{1,0:T(8,128)(2,1)S(1)}, bf16[32,4096]{1,0:T(8,128)(2,1)S(1)}, u32[]{:S(2)}, u32[]{:S(2)}) collective-permute-start(bf16[32,4096]{1,0:T(8,128)(2,1)S(1)} %collective-permute-done.17.refs_2_.refs_18_), channel_id=1, source_target_pairs={{0,1},{1,0},{2,3},{3,2},{4,5},{5,4},{6,7},{7,6},{8,9},{9,8},{10,11... | collective-permute-start | bytes 786440 | tf_op jit(solution)/shard_map/ppermute | solution.py:291
  55.1 7.1 %collective-permute-start.22 = (bf16[32,4096]{1,0:T(8,128)(2,1)S(1)}, bf16[32,4096]{1,0:T(8,128)(2,1)S(1)}, u32[]{:S(2)}, u32[]{:S(2)}) collective-permute-start(bf16[32,4096]{1,0:T(8,128)(2,1)S(1)} %collective-permute-done.18.refs_3_.refs_19_), channel_id=1, source_target_pairs={{0,1},{1,0},{2,3},{3,2},{4,5},{5,4},{6,7},{7,6},{8,9},{9,8},{10,11... | collective-permute-start | bytes 786440 | tf_op jit(solution)/shard_map/ppermute | solution.py:291
  55.6 9.6 %collective-permute-start.30 = (bf16[32,4096]{1,0:T(8,128)(2,1)S(1)}, bf16[32,4096]{1,0:T(8,128)(2,1)S(1)}, u32[]{:S(2)}, u32[]{:S(2)}) collective-permute-start(bf16[32,4096]{1,0:T(8,128)(2,1)S(1)} %collective-permute-done.26.refs_3_.refs_27_), channel_id=1, source_target_pairs={{0,1},{1,0},{2,3},{3,2},{4,5},{5,4},{6,7},{7,6},{8,9},{9,8},{10,11... | collective-permute-start | bytes 786440 | tf_op jit(solution)/shard_map/ppermute | solution.py:291
  (5 other events, 60.1 us)
